TPU v7x, 512 devices: a whole 4x8x8 slice. The times are simulated.
512 devices in a mesh: dp: 128 (over z, y, core), blk: 4 (over x).
Axes of the slice: x: 4, y: 8, z: 8, core: 2. Of those that a mesh axis runs over, the one named last changes fastest.
Arguments:
- features: bfloat16 [65536, 440], P('dp'), may hold values from -6 to 6
- residual: float32 [65536, 147], P(('dp', 'blk')), may hold values from -6 to 6
- block_weights: float32 [2, 2048, 147], P(None, ('dp', 'blk')), may hold values from -6 to 6
- block_inverse: float32 [2, 2048, 2048], P(None, None, ('dp', 'blk')), as said below
- block_columns: int32 [2, 2048], replicated, may hold values from 0 to 65535, as said below
Outputs:
- residual_out: float32 [65536, 147], P(('dp', 'blk'))
- weights_out: float32 [2, 2048, 147], P(None, ('dp', 'blk'))
Inputs may be any that keep to these rules, and one draw needn't show every extreme that they name: `block_columns`: every frame number appears at most once over both blocks. `block_inverse`: each block's matrix is symmetric and positive definite.
All inputs are finite; a program needn't handle non-finite values.
Results may differ from a plain program's by a relative error of at most 0.011.
Values may be sent and summed in bfloat16 or wider, within the bound.
No kernel may reach another device: no remote copies, remote signals or barrier semaphores. Data moves between devices by JAX's collectives and lax.ppermute only.
A program may use at most 64 MiB of HBM per device.

v0:
```python
import jax
import jax.numpy as jnp
from jax import lax
from jax.sharding import PartitionSpec as P

RIDGE = 0.3


def on_device(features, residual, block_weights, block_inverse, block_columns):
    data_count = lax.axis_size("dp")
    block_count = lax.axis_size("blk")
    data_index = lax.axis_index("dp")
    block_index = lax.axis_index("blk")
    row_count, width = features.shape
    own_count = block_weights.shape[1]
    column_count = block_columns.shape[1]
    piece_count = data_count * own_count
    gamma_rate = 4.0 / width
    frame_f = features.astype(jnp.float32)
    frame_sq = jnp.sum(frame_f * frame_f, axis=1)
    current = residual
    results = []
    for section in range(block_columns.shape[0]):
        layout = block_columns[section].reshape(data_count, block_count, own_count)
        chosen = lax.dynamic_index_in_dim(layout, block_index, 1, keepdims=False).reshape(
            piece_count
        )
        local_rows = chosen - data_index * row_count
        inside = (local_rows >= 0) & (local_rows < row_count)
        picked = jnp.take(features, jnp.clip(local_rows, 0, row_count - 1), axis=0).astype(
            jnp.float32
        )
        contrib = jnp.where(inside[:, None], picked, jnp.zeros_like(picked))
        centers = lax.psum(contrib, "dp")
        center_sq = jnp.sum(centers * centers, axis=1)
        cross = lax.dot_general(
            features,
            centers.astype(jnp.bfloat16),
            (((1,), (1,)), ((), ())),
            preferred_element_type=jnp.float32,
        )
        kernel = jnp.exp(
            -gamma_rate * (frame_sq[:, None] + center_sq[None, :] - 2.0 * cross)
        ).astype(jnp.bfloat16)
        partial_value = lax.dot_general(
            kernel,
            lax.all_gather(current.astype(jnp.bfloat16), "blk", axis=0, tiled=True),
            (((0,), (0,)), ((), ())),
            preferred_element_type=jnp.float32,
        )
        weights_own = block_weights[section]
        own_part = (
            lax.dynamic_slice_in_dim(partial_value, data_index * own_count, own_count, 0)
            - RIDGE * weights_own
        )
        partial_value = lax.dynamic_update_slice_in_dim(
            partial_value, own_part, data_index * own_count, 0
        )
        grad_piece = lax.psum(partial_value, "dp")
        stacked = lax.all_gather(grad_piece.astype(jnp.bfloat16), "blk", axis=0, tiled=True).astype(
            grad_piece.dtype
        )
        inverse = block_inverse[section].reshape(data_count, block_count, own_count, own_count)
        inverse = jnp.transpose(inverse, (1, 0, 2, 3)).reshape(column_count, own_count)
        change = lax.dot_general(
            inverse,
            stacked,
            (((0,), (0,)), ((), ())),
            precision=lax.Precision.HIGHEST,
            preferred_element_type=jnp.float32,
        )
        results.append(weights_own + change)
        change_all = lax.all_gather(change.astype(jnp.bfloat16), "dp", axis=0, tiled=True)
        current = current - lax.psum_scatter(
            jnp.dot(kernel, change_all, preferred_element_type=jnp.float32).astype(jnp.bfloat16),
            "blk",
            scatter_dimension=0,
            tiled=True,
        ).astype(jnp.float32)
    return (current, jnp.stack(results))


def solution(mesh):
    placed = (
        P("dp", None),
        P(("dp", "blk"), None),
        P(None, ("dp", "blk"), None),
        P(None, None, ("dp", "blk")),
        P(),
    )
    return jax.shard_map(
        on_device,
        mesh=mesh,
        in_specs=placed,
        out_specs=(P(("dp", "blk"), None), P(None, ("dp", "blk"), None)),
        check_vma=False,
    )
```

profile of v0, /device:TPU:1, one launch (start us, length us, event | category | flops | bytes accessed | tf_op | source)
XLA Modules:
  0.0 1401.1 jit_solution(16225051388450603120)
XLA Ops:
  7.2 0.8 slice_reduce_fusion.1
  10.6 2.0 gather_fusion.1
  12.5 2.0 gather_fusion
  14.6 1.2 convert_select_fusion
  15.8 1.2 convert_select_fusion.1
  18.0 0.7 copy-done.3
  18.6 0.8 copy-done.4
  19.4 1.3 reshape_squeeze.13
  20.9 0.7 reshape.58
  21.6 1.4 reshape_squeeze.15
  23.1 0.7 reshape.59
  23.8 9.6 all_gather.18
  33.5 189.5 %all-reduce.5.cloned.1.call-done = (f32[512,440]{1,0:T(8,128)}, f32[512,440]{1,0:T(8,128)}) async-done(((f32[512,440]{1,0:T(8,128)}, f32[512,440]{1,0:T(8,128)}), (f32[512,440]{1,0:T(8,128)}, f32[512,440]{1,0:T(8,128)})) %all-reduce.5.cloned.1.call-update) | async-done | bytes 1802256 | tf_op jit(solution)/shard_map/psum | solution.py:34
  223.0 1.5 multiply_reduce_fusion.1
  225.5 1.0 dynamic_update_slice.6
  226.5 490.4 %all-reduce.6 = bf16[512,147]{0,1:T(8,128)(2,1)S(1)} all-reduce(f32[512,147]{0,1:T(8,128)S(1)} %dynamic_update_slice.6), channel_id=1, replica_groups=mesh['dp'=128,'blk'=4] {'dp'}, use_global_device_ids=true, to_apply=%region_3.5 | all-reduce | flops 75264 | bytes 451584 | tf_op jit(solution)/shard_map/psum | solution.py:59
  716.9 11.0 all_gather.19
  727.9 0.6 fusion.15
  728.6 54.4 %all-gather = bf16[128,4,147]{2,1,0:T(4,128)(2,1)S(1)} all-gather(bf16[1,4,147]{2,1,0:T(4,128)(2,1)S(1)} %copy.29), channel_id=1, replica_groups=mesh['dp'=128,'blk'=4] {'dp'}, dimensions={0}, use_global_device_ids=true | all-gather | bytes 151704 | tf_op jit(solution)/shard_map/all_gather | solution.py:73
  783.5 0.9 copy.39
  785.3 18.5 %reduce-scatter.7.cloned.1.call-done = bf16[128,147]{1,0:T(8,128)(2,1)} async-done(((bf16[512,147]{1,0:T(8,128)(2,1)}), bf16[128,147]{1,0:T(8,128)(2,1)}) %reduce-scatter.7.cloned.1.call-update) | async-done | bytes 37648
  803.8 0.9 copy.40
  804.8 8.5 all_gather.21
  813.7 1.0 dynamic_update_slice.7
  814.6 491.7 %all-reduce.7 = bf16[512,147]{0,1:T(8,128)(2,1)S(1)} all-reduce(f32[512,147]{0,1:T(8,128)S(1)} %dynamic_update_slice.7), channel_id=1, replica_groups=mesh['dp'=128,'blk'=4] {'dp'}, use_global_device_ids=true, to_apply=%region_7.9 | all-reduce | flops 75264 | bytes 451584 | tf_op jit(solution)/shard_map/psum | solution.py:59
  1306.3 10.7 all_gather.22
  1317.0 0.6 fusion.13
  1317.7 54.4 %all-gather.1 = bf16[128,4,147]{2,1,0:T(4,128)(2,1)S(1)} all-gather(bf16[1,4,147]{2,1,0:T(4,128)(2,1)S(1)} %copy.34), channel_id=1, replica_groups=mesh['dp'=128,'blk'=4] {'dp'}, dimensions={0}, use_global_device_ids=true | all-gather | bytes 151704 | tf_op jit(solution)/shard_map/all_gather | solution.py:73
  1372.6 0.8 copy.41
  1374.2 18.7 %reduce-scatter.9.cloned.1.call-done = bf16[128,147]{1,0:T(8,128)(2,1)} async-done(((bf16[512,147]{1,0:T(8,128)(2,1)}), bf16[128,147]{1,0:T(8,128)(2,1)}) %reduce-scatter.9.cloned.1.call-update) | async-done | bytes 37648
  1393.0 0.9 copy.42
  1393.9 0.7 convert_subtract_fusion
  (56 shorter events, 8.1 us)
Async XLA Ops:
  7.2 215.8 %all-reduce.5.cloned.1.call-start = ((), (), s32[]{:S(2)}) async-start(), calls=%async_computation.4 | async-start | bytes 4194304 | tf_op jit(solution)/shard_map/psum | solution.py:34
  8.4 1.8 copy-start
  17.0 0.7 copy-start.5
  17.0 786.8 %reduce-scatter.7.cloned.1.call-start = ((), (), s32[]{:S(2)}) async-start(), calls=%async_computation.2 | async-start | bytes 327680
  17.7 0.9 copy-start.3
  18.6 0.8 copy-start.4
  223.0 1.5 copy-start.2
  783.0 1.6 copy-start.1
  784.4 608.6 %reduce-scatter.9.cloned.1.call-start = ((), (), s32[]{:S(2)}) async-start(), calls=%async_computation.3 | async-start | bytes 327680
Sparse Core Ops, SparseCore 0:
  17.2 205.8 all-reduce.4
  784.5 19.2 reduce-scatter.6
  1373.6 19.3 reduce-scatter.8
where the time goes:
time: 1400 us
  blocking collectives  1130 us (81%)
  waiting for transfers between devices  227 us (16%)
  local copies, waits for them, and re-layouts  19 us (1%)
  between operations  14.1 us (1%)
    psum x2, blocking collectives, on_device(): grad_piece = lax.psum(partial_value, 'dp')  982 us
    psum x1, waiting for transfers between devices, on_device(): centers = lax.psum(contrib, 'dp')  189 us
    all_gather x2, blocking collectives, on_device(): lax.all_gather(change.astype(jnp.bfloat16), 'dp', axis=0, tiled=True)  109 us
    unnamed x5, waiting for transfers between devices  37.3 us
  transfers between devices with their start and end apart: 3, of which 3 were waited for; matrix products, arithmetic and copies ran while one was open for 0% of the time, Pallas kernels for 0%

commit v1 on v0

v1 whole, which is shorter than its diff:
```python
import math

import jax
import jax.numpy as jnp
from jax import lax
from jax.sharding import Mesh
from jax.sharding import PartitionSpec as P

RIDGE = 0.3
DP = ("z", "y", "c")


def swap(pieces, axis):
    return lax.all_to_all(pieces, axis, 0, 0, tiled=True)


def spread(piece, axis):
    return swap(jnp.broadcast_to(piece[None], (lax.axis_size(axis), *piece.shape)), axis)


def total(pieces):
    return jnp.sum(pieces.astype(jnp.float32), axis=0)


def product(left, right, dims, **options):
    return lax.dot_general(
        left, right, (dims, ((), ())), preferred_element_type=jnp.float32, **options
    )


def on_device(features, residual, block_weights, block_inverse, block_columns):
    nz, ny, nc, nx = (lax.axis_size(axis) for axis in ("z", "y", "c", "x"))
    dp, plane = nz * ny * nc, nz * ny
    d, b = lax.axis_index(DP), lax.axis_index("x")
    rows, width = features.shape
    own_rows, classes = residual.shape
    steps, own, _ = block_weights.shape
    columns = block_columns.shape[1]
    group = dp * own
    half = group // nc
    high = -(-classes // 8) * 8
    share = -(-classes // (nz * 8)) * 8
    gamma_rate = 4.0 / width

    inverse_own = (
        block_inverse.reshape(steps, nc, dp // nc, nx, own, own)
        .transpose(0, 5, 1, 3, 2, 4)
        .reshape(steps, own, columns)
    )
    inverse = lax.all_gather(
        inverse_own.astype(jnp.bfloat16).reshape(steps * own, columns), DP, axis=0, tiled=True
    )

    current_own = jnp.pad(residual.T, ((0, high - classes), (0, 0)))
    current = spread(current_own, "x").transpose(1, 0, 2).reshape(high, rows)

    chosen = lax.dynamic_index_in_dim(
        block_columns.reshape(steps, dp, nx, own), b, 2, keepdims=False
    ).reshape(steps * group)
    places = lax.broadcasted_iota(jnp.int32, (steps * group, rows), 1)
    picks = ((chosen - d * rows)[:, None] == places).astype(jnp.bfloat16)
    part = product(picks, features, ((1,), (0,))).astype(jnp.bfloat16)
    part = total(swap(part.reshape(nc, steps * group // nc, width), "c")).astype(jnp.bfloat16)
    part = total(swap(part.reshape(plane, -1, width), ("z", "y"))).astype(jnp.bfloat16)
    part = spread(part, ("z", "y")).reshape(-1, width)
    centers = spread(part, "c").reshape(steps * group, width)

    frame_f = features.astype(jnp.float32)
    frame_sq = jnp.sum(frame_f * frame_f, axis=1)
    center_f = centers.astype(jnp.float32)
    center_sq = jnp.sum(center_f * center_f, axis=1)
    cross = product(centers, features, ((1,), (1,)))
    kernel = jnp.exp(
        -gamma_rate * (frame_sq[None, :] + center_sq[:, None] - 2.0 * cross)
    ).astype(jnp.bfloat16)

    results = []
    for step in range(steps):
        kernel_step = kernel[step * group : (step + 1) * group]
        weights = jnp.pad(block_weights[step].T, ((0, high - classes), (0, 0)))
        gradient = product(current.astype(jnp.bfloat16), kernel_step, ((1,), (1,)))
        lanes = lax.broadcasted_iota(jnp.int32, (high, group), 1) - d * own
        for i in range(own):
            gradient = jnp.where(lanes == i, gradient - RIDGE * weights[:, i : i + 1], gradient)
        gradient = jnp.pad(gradient, ((0, nz * share - high), (0, 0)))
        part = total(swap(gradient.reshape(-1, nc, half).transpose(1, 0, 2), "c"))
        part = total(swap(part.reshape(nz, share, half), "z"))
        part = total(spread(part, "y"))
        part = spread(part.astype(jnp.bfloat16), "z").reshape(nz * share, half)[:high]
        gathered = spread(part, ("c", "x")).transpose(1, 0, 2).reshape(high, columns)
        change_own = product(
            inverse_own[step],
            gathered.astype(jnp.float32),
            ((1,), (1,)),
            precision=lax.Precision.HIGHEST,
        )
        results.append(block_weights[step] + change_own[:, :classes])
        change = product(gathered, inverse, ((1,), (1,))).astype(jnp.bfloat16)
        change = change.reshape(high, dp, steps, own)[:, :, step].reshape(high, group)
        update = product(change, kernel_step, ((1,), (0,))).astype(jnp.bfloat16)
        if step < steps - 1:
            update = total(spread(update, "x"))
            current = current - update
            current_own = current_own - lax.dynamic_slice_in_dim(update, b * own_rows, own_rows, 1)
        else:
            update = update.reshape(high, nx, own_rows).transpose(1, 0, 2)
            current_own = current_own - total(swap(update, "x"))
    return current_own[:classes].T, jnp.stack(results)


def solution(mesh):
    dp, blk = mesh.shape["dp"], mesh.shape["blk"]
    plane = dp // 2
    ny = 1 << (int(math.log2(plane)) // 2)
    fine = Mesh(mesh.devices.reshape(plane // ny, ny, 2, blk), ("z", "y", "c", "x"))
    placed = (
        P(DP, None),
        P((*DP, "x"), None),
        P(None, (*DP, "x"), None),
        P(None, None, (*DP, "x")),
        P(),
    )
    return jax.shard_map(
        on_device,
        mesh=fine,
        in_specs=placed,
        out_specs=(P((*DP, "x"), None), P(None, (*DP, "x"), None)),
        check_vma=False,
    )
```

time: 1400 us -> 258 us (0.18)
  blocking collectives: 1130 us -> 156 us
  waiting for transfers between devices: 227 us -> 32.6 us
  starting transfers between devices: 0.3 us -> 21.8 us
    psum x2 -> x0, blocking collectives: 982 us -> none  [on_device(): grad_piece = lax.psum(partial_value, 'dp')]
    psum x1 -> x0, waiting for transfers between devices: 189 us -> none  [on_device(): centers = lax.psum(contrib, 'dp')]
    all_to_all x0 -> x13, blocking collectives: none -> 156 us  [swap(): return lax.all_to_all(pieces, axis, 0, 0, tiled=True)]
    all_gather x6 -> x0, blocking collectives: 149 us -> none  [the longest x2 109 us: on_device(): lax.all_gather(change.astype(jnp.bfloat16), 'dp', axis=0, tiled=True)]
    unnamed x5 -> x1, waiting for transfers between devices: 37.3 us -> 0.02 us
    all_to_all x0 -> x4, waiting for transfers between devices: none -> 32.5 us  [swap(): return lax.all_to_all(pieces, axis, 0, 0, tiled=True)]
    all_to_all x0 -> x4, starting transfers between devices: none -> 21.8 us  [swap(): return lax.all_to_all(pieces, axis, 0, 0, tiled=True)]
  transfers between devices with their start and end apart: 3 -> 5, of which waited for: 3 -> 4; matrix products, arithmetic and copies ran while one was open for 0% -> 4% of each run, Pallas kernels for 0% -> 0%
where the time goes in v1:
time: 258 us; the launch traced here: 257 us
  blocking collectives  156 us (60%)
  waiting for transfers between devices  32.6 us (13%)
  starting transfers between devices  21.8 us (8%)
  local copies, waits for them, and re-layouts  16.6 us (6%)
  between operations  14.6 us (6%)
  matrix products  12.8 us (5%)
  other arithmetic  2.83 us (1%)
    all_to_all x13, blocking collectives, swap(): return lax.all_to_all(pieces, axis, 0, 0, tiled=True)  156 us
    all_to_all x4, waiting for transfers between devices, swap(): return lax.all_to_all(pieces, axis, 0, 0, tiled=True)  32.5 us
    all_to_all x4, starting transfers between devices, swap(): return lax.all_to_all(pieces, axis, 0, 0, tiled=True)  21.8 us
    dot_general x10, matrix products, product(): lax.dot_general(left, right, (dims, ((), ())), preferred_element_type=jnp...  12.8 us
  transfers between devices with their start and end apart: 5, of which 4 were waited for; matrix products, arithmetic and copies ran while one was open for 4% of the time, Pallas kernels for 0%

profile of v1, /device:TPU:1, one launch (start us, length us, event | category | flops | bytes accessed | tf_op | source)
XLA Modules:
  0.0 256.9 jit_solution(16044828101768763953)
XLA Ops:
  7.2 3.6 %reshape.99 = f32[2,2,64,4,4,4]{4,3,2,1,5,0:T(4,128)S(1)} reshape(f32[2,2048,4]{1,2,0:T(4,128)} %param.8) | data formatting | bytes 131072 | tf_op jit(solution)/shard_map/reshape | solution.py:46
  10.8 0.9 copy.64
  12.3 2.6 %convert_element_type.80 = bf16[8,2048]{1,0:T(8,128)(2,1)} reshape(bf16[2,4,2,4,64,4]{5,4,3,2,1,0:T(8,128)(2,1)S(1)} %copy.65) | data formatting | bytes 65536 | tf_op jit(solution)/shard_map/convert_element_type | solution.py:51
  16.2 0.8 fusion.1
  17.2 11.0 %all_to_all.85 = bf16[2,512,440]{1,2,0:T(8,128)(2,1)S(1)} all-to-all(bf16[2,512,440]{1,2,0:T(8,128)(2,1)S(1)} %bitcast.122), channel_id=1, replica_groups=mesh['z'=8,'y'=8,'c'=2,'x'=4] {'c'}, dimensions={0} | all-to-all | bytes 1802240 | tf_op jit(solution)/shard_map/all_to_all | solution.py:14
  28.7 28.4 %all_to_all.86 = bf16[64,8,440]{2,1,0:T(8,128)(2,1)S(1)} all-to-all(bf16[64,8,440]{2,1,0:T(8,128)(2,1)S(1)} %bitcast.126), channel_id=1, replica_groups=mesh['z'=8,'y'=8,'c'=2,'x'=4] {'z','y'}, dimensions={0} | all-to-all | bytes 901120 | tf_op jit(solution)/shard_map/all_to_all | solution.py:14
  57.3 0.8 broadcast_in_dim.23
  58.1 6.9 %all-to-all-start.3 = ((bf16[64,8,440]{2,1,0:T(8,128)(2,1)}), bf16[64,8,440]{2,1,0:T(8,128)(2,1)S(1)}, u32[]{:S(2)}, u32[]{:S(2)}) async-start(bf16[64,8,440]{2,1,0:T(8,128)(2,1)} %broadcast_in_dim.23), calls=%async_computation.3 | async-start | bytes 1048576 | tf_op jit(solution)/shard_map/all_to_all | solution.py:14
  65.3 16.0 %all-to-all-done.3 = bf16[64,8,440]{2,1,0:T(8,128)(2,1)S(1)} async-done(((bf16[64,8,440]{2,1,0:T(8,128)(2,1)}), bf16[64,8,440]{2,1,0:T(8,128)(2,1)S(1)}, u32[]{:S(2)}, u32[]{:S(2)}) %all-to-all-start.3) | async-done | bytes 450592 | tf_op jit(solution)/shard_map/all_to_all | solution.py:14
  81.5 8.7 %all_to_all.87 = bf16[2,512,440]{1,2,0:T(8,128)(2,1)S(1)} all-to-all(bf16[2,512,440]{1,2,0:T(8,128)(2,1)S(1)} %broadcast_in_dim.25), channel_id=1, replica_groups=mesh['z'=8,'y'=8,'c'=2,'x'=4] {'c'}, dimensions={0} | all-to-all | bytes 1802240 | tf_op jit(solution)/shard_map/all_to_all | solution.py:14
  90.2 0.7 broadcast_in_dim.22
  90.9 4.0 %all-to-all-start = ((f32[4,152,128]{2,1,0:T(8,128)}), f32[4,152,128]{2,1,0:T(8,128)S(1)}, u32[]{:S(2)}, u32[]{:S(2)}) async-start(f32[4,152,128]{2,1,0:T(8,128)} %broadcast_in_dim.22), calls=%async_computation | async-start | bytes 622592 | tf_op jit(solution)/shard_map/all_to_all | solution.py:14
  95.3 0.9 exponential_convert_fusion
  96.2 5.1 %all-to-all-done = f32[4,152,128]{2,1,0:T(8,128)S(1)} async-done(((f32[4,152,128]{2,1,0:T(8,128)}), f32[4,152,128]{2,1,0:T(8,128)S(1)}, u32[]{:S(2)}, u32[]{:S(2)}) %all-to-all-start) | async-done | bytes 311328 | tf_op jit(solution)/shard_map/all_to_all | solution.py:14
  101.8 5.5 %all_to_all.88 = f32[2,192,256]{2,1,0:T(8,128)S(1)} all-to-all(f32[2,192,256]{2,1,0:T(8,128)S(1)} %bitcast.128), channel_id=1, replica_groups=mesh['z'=8,'y'=8,'c'=2,'x'=4] {'c'}, dimensions={0} | all-to-all | bytes 786432 | tf_op jit(solution)/shard_map/all_to_all | solution.py:14
  107.3 12.5 %all_to_all.89 = f32[8,24,256]{2,1,0:T(8,128)S(1)} all-to-all(f32[8,24,256]{2,1,0:T(8,128)S(1)} %bitcast.134), channel_id=1, replica_groups=mesh['z'=8,'y'=8,'c'=2,'x'=4] {'z'}, dimensions={0} | all-to-all | bytes 393216 | tf_op jit(solution)/shard_map/all_to_all | solution.py:14
  119.9 11.8 %all_to_all.90 = f32[8,24,256]{2,1,0:T(8,128)S(1)} all-to-all(f32[8,24,256]{2,1,0:T(8,128)S(1)} %broadcast_in_dim.26), channel_id=1, replica_groups=mesh['z'=8,'y'=8,'c'=2,'x'=4] {'y'}, dimensions={0} | all-to-all | bytes 393216 | tf_op jit(solution)/shard_map/all_to_all | solution.py:14
  131.7 10.1 %all_to_all.91 = bf16[8,24,256]{2,1,0:T(8,128)(2,1)S(1)} all-to-all(bf16[8,24,256]{2,1,0:T(8,128)(2,1)S(1)} %broadcast_in_dim.27), channel_id=1, replica_groups=mesh['z'=8,'y'=8,'c'=2,'x'=4] {'z'}, dimensions={0} | all-to-all | bytes 196608 | tf_op jit(solution)/shard_map/all_to_all | solution.py:14
  141.8 16.9 %all_to_all.92 = bf16[8,152,256]{2,1,0:T(8,128)(2,1)S(1)} all-to-all(bf16[8,152,256]{2,1,0:T(8,128)(2,1)S(1)} %broadcast_in_dim.28), channel_id=1, replica_groups=mesh['z'=8,'y'=8,'c'=2,'x'=4] {'c','x'}, dimensions={0} | all-to-all | bytes 1245184 | tf_op jit(solution)/shard_map/all_to_all | solution.py:14
  158.8 3.7 %convolution_convert_fusion.1 = bf16[152,1024]{1,0:T(8,128)(2,1)S(1)} fusion(bf16[152,2048]{1,0:T(8,128)(2,1)S(1)} %bitcast.118, bf16[1024,2048]{1,0:T(8,128)(2,1)} %all-gather.2.cloned.1.call-done), kind=kOutput, calls=%fused_computation.7 | convolution fusion | flops 637689856 | bytes 5128192 | tf_op jit(solution)/shard_map/dot_general | solution.py:26
  163.2 1.4 convolution_convert_fusion.3
  164.7 12.1 %all_to_all.93 = bf16[4,152,512]{2,1,0:T(8,128)(2,1)S(1)} all-to-all(bf16[4,152,512]{2,1,0:T(8,128)(2,1)S(1)} %broadcast_in_dim.29), channel_id=1, replica_groups=mesh['z'=8,'y'=8,'c'=2,'x'=4] {'x'}, dimensions={0} | all-to-all | bytes 1245184 | tf_op jit(solution)/shard_map/all_to_all | solution.py:14
  177.4 5.4 %all_to_all.94 = f32[2,192,256]{2,1,0:T(8,128)S(1)} all-to-all(f32[2,192,256]{2,1,0:T(8,128)S(1)} %bitcast.130), channel_id=1, replica_groups=mesh['z'=8,'y'=8,'c'=2,'x'=4] {'c'}, dimensions={0} | all-to-all | bytes 786432 | tf_op jit(solution)/shard_map/all_to_all | solution.py:14
  182.8 12.5 %all_to_all.95 = f32[8,24,256]{2,1,0:T(8,128)S(1)} all-to-all(f32[8,24,256]{2,1,0:T(8,128)S(1)} %bitcast.135), channel_id=1, replica_groups=mesh['z'=8,'y'=8,'c'=2,'x'=4] {'z'}, dimensions={0} | all-to-all | bytes 393216 | tf_op jit(solution)/shard_map/all_to_all | solution.py:14
  195.3 10.8 %all_to_all.96 = f32[8,24,256]{2,1,0:T(8,128)S(1)} all-to-all(f32[8,24,256]{2,1,0:T(8,128)S(1)} %broadcast_in_dim.30), channel_id=1, replica_groups=mesh['z'=8,'y'=8,'c'=2,'x'=4] {'y'}, dimensions={0} | all-to-all | bytes 393216 | tf_op jit(solution)/shard_map/all_to_all | solution.py:14
  206.1 10.1 %all_to_all.97 = bf16[8,24,256]{2,1,0:T(8,128)(2,1)S(1)} all-to-all(bf16[8,24,256]{2,1,0:T(8,128)(2,1)S(1)} %broadcast_in_dim.31), channel_id=1, replica_groups=mesh['z'=8,'y'=8,'c'=2,'x'=4] {'z'}, dimensions={0} | all-to-all | bytes 196608 | tf_op jit(solution)/shard_map/all_to_all | solution.py:14
  216.2 0.9 broadcast_in_dim.32
  217.1 7.5 %all-to-all-start.15 = ((bf16[8,152,256]{2,1,0:T(8,128)(2,1)}), bf16[8,152,256]{2,1,0:T(8,128)(2,1)S(1)}, u32[]{:S(2)}, u32[]{:S(2)}) async-start(bf16[8,152,256]{2,1,0:T(8,128)(2,1)} %broadcast_in_dim.32), calls=%async_computation.15 | async-start | bytes 1245184 | tf_op jit(solution)/shard_map/all_to_all | solution.py:14
  227.4 7.7 %all-to-all-done.15 = bf16[8,152,256]{2,1,0:T(8,128)(2,1)S(1)} async-done(((bf16[8,152,256]{2,1,0:T(8,128)(2,1)}), bf16[8,152,256]{2,1,0:T(8,128)(2,1)S(1)}, u32[]{:S(2)}, u32[]{:S(2)}) %all-to-all-start.15) | async-done | bytes 622624 | tf_op jit(solution)/shard_map/all_to_all | solution.py:14
  235.1 3.7 %convolution_convert_fusion = bf16[152,1024]{1,0:T(8,128)(2,1)S(1)} fusion(bf16[152,2048]{1,0:T(8,128)(2,1)S(1)} %bitcast.120, bf16[1024,2048]{1,0:T(8,128)(2,1)} %all-gather.2.cloned.1.call-done), kind=kOutput, calls=%fused_computation.6 | convolution fusion | flops 637689856 | bytes 5128192 | tf_op jit(solution)/shard_map/dot_general | solution.py:26
  241.0 3.3 %all-to-all-start.16 = ((bf16[4,152,128]{2,1,0:T(8,128)(2,1)}), bf16[4,152,128]{2,1,0:T(8,128)(2,1)S(1)}, u32[]{:S(2)}, u32[]{:S(2)}) async-start(bf16[4,152,128]{2,1,0:T(8,128)(2,1)} %bitcast.116), calls=%async_computation.16 | async-start | bytes 311296 | tf_op jit(solution)/shard_map/all_to_all | solution.py:14
  245.6 3.7 %all-to-all-done.16 = bf16[4,152,128]{2,1,0:T(8,128)(2,1)S(1)} async-done(((bf16[4,152,128]{2,1,0:T(8,128)(2,1)}), bf16[4,152,128]{2,1,0:T(8,128)(2,1)S(1)}, u32[]{:S(2)}, u32[]{:S(2)}) %all-to-all-start.16) | async-done | bytes 155680 | tf_op jit(solution)/shard_map/all_to_all | solution.py:14
  (81 shorter events, 12.1 us)
Async XLA Ops:
  7.2 151.7 %all-gather.2.cloned.1.call-start = ((), (), s32[]{:S(2)}) async-start(), calls=%async_computation.17 | async-start | bytes 4227072 | tf_op jit(solution)/shard_map/all_gather | solution.py:50
  10.8 4.2 %copy-start.3 = (s32[2,2048]{1,0:T(2,128)S(1)}, s32[2,2048]{1,0:T(2,128)}, u32[]{:S(2)}) copy-start(s32[2,2048]{1,0:T(2,128)} %param.9) | copy-start | bytes 49156
  11.7 4.5 %copy-start = (bf16[512,440]{0,1:T(8,128)(2,1)S(1)}, bf16[512,440]{0,1:T(8,128)(2,1)}, u32[]{:S(2)}) copy-start(bf16[512,440]{0,1:T(8,128)(2,1)} %param.5) | copy-start | bytes 1351684
  28.5 36.5 %copy-start.1 = (f32[128,147]{0,1:T(8,128)S(1)}, f32[128,147]{0,1:T(8,128)}, u32[]{:S(2)}) copy-start(f32[128,147]{0,1:T(8,128)} %param.6) | copy-start | bytes 225796
  28.5 36.6 %copy-start.2 = (f32[2,4,147]{2,1,0:T(4,128)S(1)}, f32[2,4,147]{2,1,0:T(4,128)}, u32[]{:S(2)}) copy-start(f32[2,4,147]{2,1,0:T(4,128)} %param.7) | copy-start | bytes 14116
  58.1 23.1 %all-to-all-start.3 = ((bf16[64,8,440]{2,1,0:T(8,128)(2,1)}), bf16[64,8,440]{2,1,0:T(8,128)(2,1)S(1)}, u32[]{:S(2)}, u32[]{:S(2)}) async-start(bf16[64,8,440]{2,1,0:T(8,128)(2,1)} %broadcast_in_dim.23), calls=%async_computation.3 | async-start | bytes 1048576 | tf_op jit(solution)/shard_map/all_to_all | solution.py:14
  90.9 10.4 %all-to-all-start = ((f32[4,152,128]{2,1,0:T(8,128)}), f32[4,152,128]{2,1,0:T(8,128)S(1)}, u32[]{:S(2)}, u32[]{:S(2)}) async-start(f32[4,152,128]{2,1,0:T(8,128)} %broadcast_in_dim.22), calls=%async_computation | async-start | bytes 622592 | tf_op jit(solution)/shard_map/all_to_all | solution.py:14
  96.2 5.6 %copy-start.4 = (bf16[1024,512]{1,0:T(8,128)(2,1)}, bf16[1024,512]{1,0:T(8,128)(2,1)S(1)}, u32[]{:S(2)}) copy-start(bf16[1024,512]{1,0:T(8,128)(2,1)S(1)} %exponential_convert_fusion) | copy-start | bytes 3145732
  163.2 13.7 %copy-start.5 = (bf16[1024,512]{1,0:T(8,128)(2,1)S(1)}, bf16[1024,512]{1,0:T(8,128)(2,1)}, u32[]{:S(2)}) copy-start(bf16[1024,512]{1,0:T(8,128)(2,1)} %copy-done.4) | copy-start | bytes 3145732
  217.1 18.0 %all-to-all-start.15 = ((bf16[8,152,256]{2,1,0:T(8,128)(2,1)}), bf16[8,152,256]{2,1,0:T(8,128)(2,1)S(1)}, u32[]{:S(2)}, u32[]{:S(2)}) async-start(bf16[8,152,256]{2,1,0:T(8,128)(2,1)} %broadcast_in_dim.32), calls=%async_computation.15 | async-start | bytes 1245184 | tf_op jit(solution)/shard_map/all_to_all | solution.py:14
  238.8 1.2 copy-start.6
  241.0 8.3 %all-to-all-start.16 = ((bf16[4,152,128]{2,1,0:T(8,128)(2,1)}), bf16[4,152,128]{2,1,0:T(8,128)(2,1)S(1)}, u32[]{:S(2)}, u32[]{:S(2)}) async-start(bf16[4,152,128]{2,1,0:T(8,128)(2,1)} %bitcast.116), calls=%async_computation.16 | async-start | bytes 311296 | tf_op jit(solution)/shard_map/all_to_all | solution.py:14
Sparse Core Ops, SparseCore 0:
  15.1 96.0 all-gather.1

commit v2 on v1

v2 whole, which is shorter than its diff:
```python
import math

import jax
import jax.numpy as jnp
from jax import lax
from jax.sharding import Mesh
from jax.sharding import PartitionSpec as P

RIDGE = 0.3
DP = ("z", "y", "c")
PLANE = ("z", "y")
CELL = ("c", "x")


def swap(pieces, axis):
    return lax.all_to_all(pieces, axis, 0, 0, tiled=True)


def spread(piece, axis):
    return swap(jnp.broadcast_to(piece[None], (lax.axis_size(axis), *piece.shape)), axis)


def total(pieces):
    return jnp.sum(pieces.astype(jnp.float32), axis=0)


def side_by_side(pieces):
    count, high, wide = pieces.shape
    return pieces.transpose(1, 0, 2).reshape(high, count * wide)


def product(left, right, dims, **options):
    return lax.dot_general(
        left, right, (dims, ((), ())), preferred_element_type=jnp.float32, **options
    )


def on_device(features, residual, block_weights, block_inverse, block_columns):
    nz, ny, nc, nx = (lax.axis_size(axis) for axis in ("z", "y", "c", "x"))
    plane, cell = nz * ny, nc * nx
    place, member = lax.axis_index(PLANE), lax.axis_index(CELL)
    width = features.shape[1]
    own_rows, classes = residual.shape
    steps, own, _ = block_weights.shape
    columns = block_columns.shape[1]
    group = plane * own
    high = -(-classes // 8) * 8
    share = -(-classes // (nz * 8)) * 8
    gamma_rate = 4.0 / width
    low = jnp.bfloat16

    inverse = (
        block_inverse.astype(low)
        .reshape(steps, plane, cell, own, own)
        .transpose(0, 4, 2, 1, 3)
        .reshape(steps * own, columns)
    )
    inverse = lax.all_gather(inverse, PLANE, axis=0, tiled=True)
    order = lax.broadcasted_iota(jnp.int32, (steps * group, steps * group), 0)
    order = (order // own % plane) * (steps * own) + order // group * own + order % own
    order = order == lax.broadcasted_iota(jnp.int32, order.shape, 1)
    inverse = product(order.astype(low), inverse, ((1,), (0,))).astype(low)

    current = jnp.pad(residual.T, ((0, high - classes), (0, 0)))
    current_low = side_by_side(spread(current.astype(low), CELL))

    frames = spread(features, "c").reshape(-1, width)
    rows = frames.shape[0]
    chosen = lax.dynamic_index_in_dim(
        block_columns.reshape(steps, plane, cell, own), member, 2, keepdims=False
    ).reshape(steps * group)
    spots = lax.broadcasted_iota(jnp.int32, (steps * group, rows), 1)
    picks = ((chosen - place * rows)[:, None] == spots).astype(low)
    part = product(picks, frames, ((1,), (0,))).astype(low)
    part = total(swap(part.reshape(plane, -1, width), PLANE)).astype(low)
    centers = spread(part, PLANE).reshape(steps * group, width)

    frame_f = frames.astype(jnp.float32)
    frame_sq = jnp.sum(frame_f * frame_f, axis=1)
    center_f = centers.astype(jnp.float32)
    center_sq = jnp.sum(center_f * center_f, axis=1)
    cross = product(centers, frames, ((1,), (1,)))
    kernel = jnp.exp(
        -gamma_rate * (frame_sq[None, :] + center_sq[:, None] - 2.0 * cross)
    ).astype(low)

    lanes = lax.broadcasted_iota(jnp.int32, (high, group), 1) - place * own
    results = []
    for step in range(steps):
        block = slice(step * group, (step + 1) * group)
        weights = jnp.pad(block_weights[step].T, ((0, high - classes), (0, 0)))
        gradient = product(current_low, kernel[block], ((1,), (1,)))
        for i in range(own):
            gradient = jnp.where(lanes == i, gradient - RIDGE * weights[:, i : i + 1], gradient)
        gradient = jnp.pad(gradient, ((0, nz * share - high), (0, 0)))
        part = total(swap(gradient.reshape(nz, share, group), "z"))
        part = total(spread(part, "y"))
        part = side_by_side(spread(part.astype(low), CELL))
        part = product(part, inverse[block], ((1,), (1,)))
        change = spread(part, "z").reshape(nz * share, group)[:high]
        update = product(change.astype(low), kernel[block], ((1,), (0,))).astype(low)
        update = update.reshape(high, cell, own_rows).transpose(1, 0, 2)
        current = current - total(swap(update, CELL))
        if step < steps - 1:
            current_low = side_by_side(spread(current.astype(low), CELL))
        change_own = jnp.stack(
            [jnp.sum(jnp.where(lanes == i, change, 0.0), axis=1)[:classes] for i in range(own)]
        )
        results.append(block_weights[step] + change_own)
    return current[:classes].T, jnp.stack(results)


def solution(mesh):
    dp, blk = mesh.shape["dp"], mesh.shape["blk"]
    plane = dp // 2
    ny = 1 << (int(math.log2(plane)) // 2)
    fine = Mesh(mesh.devices.reshape(plane // ny, ny, 2, blk), ("z", "y", "c", "x"))
    placed = (
        P(DP, None),
        P((*DP, "x"), None),
        P(None, (*DP, "x"), None),
        P(None, None, (*DP, "x")),
        P(),
    )
    return jax.shard_map(
        on_device,
        mesh=fine,
        in_specs=placed,
        out_specs=(P((*DP, "x"), None), P(None, (*DP, "x"), None)),
        check_vma=False,
    )
```

time: 258 us -> 247 us (0.957)
  blocking collectives: 156 us -> 123 us
  starting transfers between devices: 21.8 us -> 38.9 us
  waiting for transfers between devices: 32.6 us -> 44.1 us
  matrix products: 12.8 us -> 7.45 us
  local copies, waits for them, and re-layouts: 16.6 us -> 11.9 us
    all_to_all x13 -> x9, blocking collectives: 156 us -> 123 us  [swap(): return lax.all_to_all(pieces, axis, 0, 0, tiled=True)]
    all_to_all x4 -> x6, starting transfers between devices: 21.8 us -> 38.9 us  [swap(): return lax.all_to_all(pieces, axis, 0, 0, tiled=True)]
    all_to_all x4 -> x6, waiting for transfers between devices: 32.5 us -> 44.1 us  [swap(): return lax.all_to_all(pieces, axis, 0, 0, tiled=True)]
    dot_general x10 -> x9, matrix products: 12.8 us -> 7.45 us  [product(): lax.dot_general(left, right, (dims, ((), ())), preferred_element_type=jnp...]
    convert_element_type x4 -> x2, local copies, waits for them, and re-layouts: 3.56 us -> 0.21 us  [the longest x1 0.2 us: on_device(): part = product(picks, frames, ((1,), (0,))).astype(low)]
    reshape x12 -> x8, local copies, waits for them, and re-layouts: 6.51 us -> 6.33 us  [the longest x2 4.85 us: on_device(): inverse = block_inverse.astype(low).reshape(steps, plane, cell, own, own)...]
  transfers between devices with their start and end apart: 5 -> 7, of which waited for: 4 -> 6; matrix products, arithmetic and copies ran while one was open for 4% -> 3% of each run, Pallas kernels for 0% -> 0%
where the time goes in v2:
time: 247 us; the launch traced here: 246 us
  blocking collectives  123 us (50%)
  waiting for transfers between devices  44.1 us (18%)
  starting transfers between devices  38.9 us (16%)
  between operations  14.4 us (6%)
  local copies, waits for them, and re-layouts  11.9 us (5%)
  matrix products  7.45 us (3%)
  other arithmetic  5.34 us (2%)
    all_to_all x9, blocking collectives, swap(): return lax.all_to_all(pieces, axis, 0, 0, tiled=True)  123 us
    all_to_all x6, waiting for transfers between devices, swap(): return lax.all_to_all(pieces, axis, 0, 0, tiled=True)  44.1 us
    all_to_all x6, starting transfers between devices, swap(): return lax.all_to_all(pieces, axis, 0, 0, tiled=True)  38.9 us
    dot_general x9, matrix products, product(): lax.dot_general(left, right, (dims, ((), ())), preferred_element_type=jnp...  7.45 us
  transfers between devices with their start and end apart: 7, of which 6 were waited for; matrix products, arithmetic and copies ran while one was open for 3% of the time, Pallas kernels for 0%

profile of v2, /device:TPU:1, one launch (start us, length us, event | category | flops | bytes accessed | tf_op | source)
XLA Modules:
  0.0 245.6 jit_solution(5538982991908643533)
XLA Ops:
  7.2 0.9 convert_element_type.76
  8.1 2.2 reshape.104
  10.6 2.6 %reshape.105 = bf16[8,2048]{1,0:T(8,128)(2,1)} reshape(bf16[2,4,8,64,4]{4,3,2,1,0:T(8,128)(2,1)S(1)} %copy.32) | data formatting | bytes 65536 | tf_op jit(solution)/shard_map/reshape | solution.py:56
  13.3 1.0 broadcast_in_dim.31
  14.2 10.4 %all-to-all-start.1 = ((bf16[2,512,440]{1,2,0:T(8,128)(2,1)}), bf16[2,512,440]{1,2,0:T(8,128)(2,1)S(1)}, u32[]{:S(2)}, u32[]{:S(2)}) async-start(bf16[2,512,440]{1,2,0:T(8,128)(2,1)} %broadcast_in_dim.31), calls=%async_computation.1 | async-start | bytes 1802240 | tf_op jit(solution)/shard_map/all_to_all | solution.py:16
  25.5 0.8 all-to-all-done.1
  26.4 0.8 fusion.1
  27.5 28.5 %all_to_all.75 = bf16[64,8,440]{2,1,0:T(8,128)(2,1)S(1)} all-to-all(bf16[64,8,440]{2,1,0:T(8,128)(2,1)S(1)} %bitcast.113), channel_id=1, replica_groups=mesh['z'=8,'y'=8,'c'=2,'x'=4] {'z','y'}, dimensions={0} | all-to-all | bytes 901120 | tf_op jit(solution)/shard_map/all_to_all | solution.py:16
  56.1 0.8 broadcast_in_dim.33
  56.9 7.1 %all-to-all-start.3 = ((bf16[64,8,440]{2,1,0:T(8,128)(2,1)}), bf16[64,8,440]{2,1,0:T(8,128)(2,1)S(1)}, u32[]{:S(2)}, u32[]{:S(2)}) async-start(bf16[64,8,440]{2,1,0:T(8,128)(2,1)} %broadcast_in_dim.33), calls=%async_computation.3 | async-start | bytes 1048576 | tf_op jit(solution)/shard_map/all_to_all | solution.py:16
  64.4 16.2 %all-to-all-done.3 = bf16[64,8,440]{2,1,0:T(8,128)(2,1)S(1)} async-done(((bf16[64,8,440]{2,1,0:T(8,128)(2,1)}), bf16[64,8,440]{2,1,0:T(8,128)(2,1)S(1)}, u32[]{:S(2)}, u32[]{:S(2)}) %all-to-all-start.3) | async-done | bytes 450592 | tf_op jit(solution)/shard_map/all_to_all | solution.py:16
  80.7 0.8 broadcast_in_dim.30
  81.4 8.2 %all-to-all-start = ((bf16[8,152,128]{2,1,0:T(8,128)(2,1)}), bf16[8,152,128]{2,1,0:T(8,128)(2,1)S(1)}, u32[]{:S(2)}, u32[]{:S(2)}) async-start(bf16[8,152,128]{2,1,0:T(8,128)(2,1)} %broadcast_in_dim.30), calls=%async_computation | async-start | bytes 622592 | tf_op jit(solution)/shard_map/all_to_all | solution.py:16
  90.0 0.9 exponential_convert_fusion
  90.8 5.9 %all-to-all-done = bf16[8,152,128]{2,1,0:T(8,128)(2,1)S(1)} async-done(((bf16[8,152,128]{2,1,0:T(8,128)(2,1)}), bf16[8,152,128]{2,1,0:T(8,128)(2,1)S(1)}, u32[]{:S(2)}, u32[]{:S(2)}) %all-to-all-start) | async-done | bytes 311328 | tf_op jit(solution)/shard_map/all_to_all | solution.py:16
  97.1 15.0 %all_to_all.76 = f32[8,24,256]{2,1,0:T(8,128)S(1)} all-to-all(f32[8,24,256]{2,1,0:T(8,128)S(1)} %bitcast.121), channel_id=1, replica_groups=mesh['z'=8,'y'=8,'c'=2,'x'=4] {'z'}, dimensions={0} | all-to-all | bytes 393216 | tf_op jit(solution)/shard_map/all_to_all | solution.py:16
  112.9 3.4 %all-to-all-start.5 = ((f32[8,24,256]{2,1,0:T(8,128)}), f32[8,24,256]{2,1,0:T(8,128)S(1)}, u32[]{:S(2)}, u32[]{:S(2)}) async-start(f32[8,24,256]{2,1,0:T(8,128)} %broadcast_in_dim.34), calls=%async_computation.5 | async-start | bytes 393216 | tf_op jit(solution)/shard_map/all_to_all | solution.py:16
  116.3 9.7 %all-to-all-done.5 = f32[8,24,256]{2,1,0:T(8,128)S(1)} async-done(((f32[8,24,256]{2,1,0:T(8,128)}), f32[8,24,256]{2,1,0:T(8,128)S(1)}, u32[]{:S(2)}, u32[]{:S(2)}) %all-to-all-start.5) | async-done | bytes 196640 | tf_op jit(solution)/shard_map/all_to_all | solution.py:16
  126.7 4.9 %all-to-all-start.6 = ((bf16[8,24,256]{2,1,0:T(8,128)(2,1)}), bf16[8,24,256]{2,1,0:T(8,128)(2,1)S(1)}, u32[]{:S(2)}, u32[]{:S(2)}) async-start(bf16[8,24,256]{2,1,0:T(8,128)(2,1)} %broadcast_in_dim.35), calls=%async_computation.6 | async-start | bytes 196608 | tf_op jit(solution)/shard_map/all_to_all | solution.py:16
  131.6 5.0 %all-to-all-done.6 = bf16[8,24,256]{2,1,0:T(8,128)(2,1)S(1)} async-done(((bf16[8,24,256]{2,1,0:T(8,128)(2,1)}), bf16[8,24,256]{2,1,0:T(8,128)(2,1)S(1)}, u32[]{:S(2)}, u32[]{:S(2)}) %all-to-all-start.6) | async-done | bytes 98336 | tf_op jit(solution)/shard_map/all_to_all | solution.py:16
  136.6 3.8 %convolution_convert_fusion = bf16[512,2048]{1,0:T(8,128)(2,1)S(1)} fusion(bf16[512,2048]{1,0:T(8,128)(2,1)} %all-gather.2.cloned.1.call-done, s32[512]{0:T(512)S(1)} %get-tuple-element.38, s32[512]{0:T(512)S(1)} %get-tuple-element.39, s32[512]{0:T(512)S(1)} %get-tuple-element.36, s32[512]{0:T(512)S(1)} %get-tuple-element.42, s32[512]{0:T(512)S(1)} %get-tuple-element.37, ...), kind=kOutput, calls=%fused_computation | convolution fusion | flops 1079771136 | bytes 4208128 | tf_op jit(solution)/shard_map/dot_general | solution.py:33
  140.9 12.4 %all_to_all.77 = f32[8,24,256]{2,1,0:T(8,128)S(1)} all-to-all(f32[8,24,256]{2,1,0:T(8,128)S(1)} %broadcast_in_dim.36), channel_id=1, replica_groups=mesh['z'=8,'y'=8,'c'=2,'x'=4] {'z'}, dimensions={0} | all-to-all | bytes 393216 | tf_op jit(solution)/shard_map/all_to_all | solution.py:16
  153.6 11.3 %all_to_all.78 = bf16[8,152,128]{2,1,0:T(8,128)(2,1)S(1)} all-to-all(bf16[8,152,128]{2,1,0:T(8,128)(2,1)S(1)} %bitcast.118), channel_id=1, replica_groups=mesh['z'=8,'y'=8,'c'=2,'x'=4] {'c','x'}, dimensions={0} | all-to-all | bytes 622592 | tf_op jit(solution)/shard_map/all_to_all | solution.py:16
  165.6 10.3 %all_to_all.79 = bf16[8,152,128]{2,1,0:T(8,128)(2,1)S(1)} all-to-all(bf16[8,152,128]{2,1,0:T(8,128)(2,1)S(1)} %broadcast_in_dim.37), channel_id=1, replica_groups=mesh['z'=8,'y'=8,'c'=2,'x'=4] {'c','x'}, dimensions={0} | all-to-all | bytes 622592 | tf_op jit(solution)/shard_map/all_to_all | solution.py:16
  176.3 12.4 %all_to_all.80 = f32[8,24,256]{2,1,0:T(8,128)S(1)} all-to-all(f32[8,24,256]{2,1,0:T(8,128)S(1)} %bitcast.122), channel_id=1, replica_groups=mesh['z'=8,'y'=8,'c'=2,'x'=4] {'z'}, dimensions={0} | all-to-all | bytes 393216 | tf_op jit(solution)/shard_map/all_to_all | solution.py:16
  190.0 10.8 %all_to_all.81 = f32[8,24,256]{2,1,0:T(8,128)S(1)} all-to-all(f32[8,24,256]{2,1,0:T(8,128)S(1)} %broadcast_in_dim.38), channel_id=1, replica_groups=mesh['z'=8,'y'=8,'c'=2,'x'=4] {'y'}, dimensions={0} | all-to-all | bytes 393216 | tf_op jit(solution)/shard_map/all_to_all | solution.py:16
  200.8 10.4 %all_to_all.82 = bf16[8,24,256]{2,1,0:T(8,128)(2,1)S(1)} all-to-all(bf16[8,24,256]{2,1,0:T(8,128)(2,1)S(1)} %broadcast_in_dim.39), channel_id=1, replica_groups=mesh['z'=8,'y'=8,'c'=2,'x'=4] {'c','x'}, dimensions={0} | all-to-all | bytes 196608 | tf_op jit(solution)/shard_map/all_to_all | solution.py:16
  211.7 12.4 %all_to_all.83 = f32[8,24,256]{2,1,0:T(8,128)S(1)} all-to-all(f32[8,24,256]{2,1,0:T(8,128)S(1)} %broadcast_in_dim.40), channel_id=1, replica_groups=mesh['z'=8,'y'=8,'c'=2,'x'=4] {'z'}, dimensions={0} | all-to-all | bytes 393216 | tf_op jit(solution)/shard_map/all_to_all | solution.py:16
  224.4 1.0 select_reduce_fusion.3
  225.4 0.8 copy.71
  226.2 4.8 %all-to-all-start.14 = ((bf16[8,152,128]{2,1,0:T(8,128)(2,1)}), bf16[8,152,128]{2,1,0:T(8,128)(2,1)S(1)}, u32[]{:S(2)}, u32[]{:S(2)}) async-start(bf16[8,152,128]{2,1,0:T(8,128)(2,1)} %bitcast.100), calls=%async_computation.14 | async-start | bytes 622592 | tf_op jit(solution)/shard_map/all_to_all | solution.py:16
  231.6 6.5 %all-to-all-done.14 = bf16[8,152,128]{2,1,0:T(8,128)(2,1)S(1)} async-done(((bf16[8,152,128]{2,1,0:T(8,128)(2,1)}), bf16[8,152,128]{2,1,0:T(8,128)(2,1)S(1)}, u32[]{:S(2)}, u32[]{:S(2)}) %all-to-all-start.14) | async-done | bytes 311328 | tf_op jit(solution)/shard_map/all_to_all | solution.py:16
  (70 shorter events, 9.1 us)
Async XLA Ops:
  7.2 129.4 %all-gather.2.cloned.1.call-start = ((), (), s32[]{:S(2)}) async-start(), calls=%async_computation.15 | async-start | bytes 2129920 | tf_op jit(solution)/shard_map/all_gather | solution.py:58
  8.1 5.2 %copy-start = (bf16[512,440]{0,1:T(8,128)(2,1)S(1)}, bf16[512,440]{0,1:T(8,128)(2,1)}, u32[]{:S(2)}) copy-start(bf16[512,440]{0,1:T(8,128)(2,1)} %param.5) | copy-start | bytes 1351684
  10.6 14.1 %copy-start.5 = (s32[2,2048]{1,0:T(2,128)S(1)}, s32[2,2048]{1,0:T(2,128)}, u32[]{:S(2)}) copy-start(s32[2,2048]{1,0:T(2,128)} %param.9) | copy-start | bytes 49156
  14.2 12.1 %all-to-all-start.1 = ((bf16[2,512,440]{1,2,0:T(8,128)(2,1)}), bf16[2,512,440]{1,2,0:T(8,128)(2,1)S(1)}, u32[]{:S(2)}, u32[]{:S(2)}) async-start(bf16[2,512,440]{1,2,0:T(8,128)(2,1)} %broadcast_in_dim.31), calls=%async_computation.1 | async-start | bytes 1802240 | tf_op jit(solution)/shard_map/all_to_all | solution.py:16
  27.5 36.9 %copy-start.3 = (f32[2,4,147]{2,1,0:T(4,128)S(1)}, f32[2,4,147]{2,1,0:T(4,128)}, u32[]{:S(2)}) copy-start(f32[2,4,147]{2,1,0:T(4,128)} %param.7) | copy-start | bytes 14116
  27.5 36.9 %copy-start.1 = (f32[128,147]{0,1:T(8,128)S(1)}, f32[128,147]{0,1:T(8,128)}, u32[]{:S(2)}) copy-start(f32[128,147]{0,1:T(8,128)} %param.6) | copy-start | bytes 225796
  56.9 23.7 %all-to-all-start.3 = ((bf16[64,8,440]{2,1,0:T(8,128)(2,1)}), bf16[64,8,440]{2,1,0:T(8,128)(2,1)S(1)}, u32[]{:S(2)}, u32[]{:S(2)}) async-start(bf16[64,8,440]{2,1,0:T(8,128)(2,1)} %broadcast_in_dim.33), calls=%async_computation.3 | async-start | bytes 1048576 | tf_op jit(solution)/shard_map/all_to_all | solution.py:16
  64.3 111.6 %copy-start.6 = (pred[256]{0:T(512)(128)(4,1)}, pred[256]{0:T(512)(128)(4,1)S(1)}, u32[]{:S(2)}) copy-start(pred[256]{0:T(512)(128)(4,1)S(1)} %get-tuple-element.35) | copy-start | bytes 772
  64.3 111.6 %copy-start.7 = (pred[256]{0:T(512)(128)(4,1)}, pred[256]{0:T(512)(128)(4,1)S(1)}, u32[]{:S(2)}) copy-start(pred[256]{0:T(512)(128)(4,1)S(1)} %get-tuple-element.32) | copy-start | bytes 772
  64.4 111.5 %copy-start.8 = (pred[256]{0:T(512)(128)(4,1)}, pred[256]{0:T(512)(128)(4,1)S(1)}, u32[]{:S(2)}) copy-start(pred[256]{0:T(512)(128)(4,1)S(1)} %get-tuple-element.33) | copy-start | bytes 772
  81.4 15.3 %all-to-all-start = ((bf16[8,152,128]{2,1,0:T(8,128)(2,1)}), bf16[8,152,128]{2,1,0:T(8,128)(2,1)S(1)}, u32[]{:S(2)}, u32[]{:S(2)}) async-start(bf16[8,152,128]{2,1,0:T(8,128)(2,1)} %broadcast_in_dim.30), calls=%async_computation | async-start | bytes 622592 | tf_op jit(solution)/shard_map/all_to_all | solution.py:16
  112.9 13.1 %all-to-all-start.5 = ((f32[8,24,256]{2,1,0:T(8,128)}), f32[8,24,256]{2,1,0:T(8,128)S(1)}, u32[]{:S(2)}, u32[]{:S(2)}) async-start(f32[8,24,256]{2,1,0:T(8,128)} %broadcast_in_dim.34), calls=%async_computation.5 | async-start | bytes 393216 | tf_op jit(solution)/shard_map/all_to_all | solution.py:16
  126.7 9.9 %all-to-all-start.6 = ((bf16[8,24,256]{2,1,0:T(8,128)(2,1)}), bf16[8,24,256]{2,1,0:T(8,128)(2,1)S(1)}, u32[]{:S(2)}, u32[]{:S(2)}) async-start(bf16[8,24,256]{2,1,0:T(8,128)(2,1)} %broadcast_in_dim.35), calls=%async_computation.6 | async-start | bytes 196608 | tf_op jit(solution)/shard_map/all_to_all | solution.py:16
  211.3 19.7 %copy-start.4 = (f32[2,4,147]{2,1,0:T(4,128)S(1)}, f32[2,4,147]{2,1,0:T(4,128)}, u32[]{:S(2)}) copy-start(f32[2,4,147]{2,1,0:T(4,128)} %param.7) | copy-start | bytes 14116
  211.7 26.4 %copy-start.2 = (f32[152,128]{1,0:T(8,128)S(1)}, f32[152,128]{1,0:T(8,128)}, u32[]{:S(2)}) copy-start(f32[152,128]{1,0:T(8,128)} %get-tuple-element.15) | copy-start | bytes 233476
  226.2 11.9 %all-to-all-start.14 = ((bf16[8,152,128]{2,1,0:T(8,128)(2,1)}), bf16[8,152,128]{2,1,0:T(8,128)(2,1)S(1)}, u32[]{:S(2)}, u32[]{:S(2)}) async-start(bf16[8,152,128]{2,1,0:T(8,128)(2,1)} %bitcast.100), calls=%async_computation.14 | async-start | bytes 622592 | tf_op jit(solution)/shard_map/all_to_all | solution.py:16
Sparse Core Ops, SparseCore 0:
  13.4 89.9 all-gather.1

commit v3 on v2

--- a/solution.py
+++ b/solution.py
@@ -35,6 +35,14 @@
     )
 
 
+def in_step_order(rows, steps, plane, own):
+    count = steps * plane * own
+    row = lax.broadcasted_iota(jnp.int32, (count, count), 0)
+    source = (row // own % plane) * (steps * own) + row // (plane * own) * own + row % own
+    order = source == lax.broadcasted_iota(jnp.int32, (count, count), 1)
+    return product(order.astype(rows.dtype), rows, ((1,), (0,))).astype(rows.dtype)
+
+
 def on_device(features, residual, block_weights, block_inverse, block_columns):
     nz, ny, nc, nx = (lax.axis_size(axis) for axis in ("z", "y", "c", "x"))
     plane, cell = nz * ny, nc * nx
@@ -49,22 +57,29 @@
     gamma_rate = 4.0 / width
     low = jnp.bfloat16
 
+    span = min(plane, 128 // own)
+    row = lax.broadcasted_iota(jnp.int32, (cell * span * own, cell * span * own), 0)
+    col = lax.broadcasted_iota(jnp.int32, row.shape, 1)
+    there = row // own % cell * (span * own) + row // (own * cell) * own + row % own
+    inverse = product(
+        block_inverse.transpose(0, 2, 1).astype(low).reshape(steps * own, -1, row.shape[0]),
+        (there == col).astype(low),
+        ((2,), (0,)),
+    ).astype(low)
     inverse = (
-        block_inverse.astype(low)
-        .reshape(steps, plane, cell, own, own)
-        .transpose(0, 4, 2, 1, 3)
+        inverse.reshape(steps * own, -1, cell, span * own)
+        .transpose(0, 2, 1, 3)
         .reshape(steps * own, columns)
     )
     inverse = lax.all_gather(inverse, PLANE, axis=0, tiled=True)
-    order = lax.broadcasted_iota(jnp.int32, (steps * group, steps * group), 0)
-    order = (order // own % plane) * (steps * own) + order // group * own + order % own
-    order = order == lax.broadcasted_iota(jnp.int32, order.shape, 1)
-    inverse = product(order.astype(low), inverse, ((1,), (0,))).astype(low)
+    current = jnp.pad(residual.T, ((0, high - classes), (0, 0)))
+    current_low = side_by_side(lax.all_gather(current.astype(low), CELL))
 
-    current = jnp.pad(residual.T, ((0, high - classes), (0, 0)))
-    current_low = side_by_side(spread(current.astype(low), CELL))
-
-    frames = spread(features, "c").reshape(-1, width)
+    other = lax.ppermute(features, "c", [(i, (i + 1) % nc) for i in range(nc)])
+    first = lax.axis_index("c") == 0
+    frames = jnp.concatenate(
+        [jnp.where(first, features, other), jnp.where(first, other, features)]
+    )
     rows = frames.shape[0]
     chosen = lax.dynamic_index_in_dim(
         block_columns.reshape(steps, plane, cell, own), member, 2, keepdims=False
@@ -92,10 +107,14 @@
         gradient = product(current_low, kernel[block], ((1,), (1,)))
         for i in range(own):
             gradient = jnp.where(lanes == i, gradient - RIDGE * weights[:, i : i + 1], gradient)
-        gradient = jnp.pad(gradient, ((0, nz * share - high), (0, 0)))
+        gradient = jnp.pad(gradient.astype(low), ((0, nz * share - high), (0, 0)))
         part = total(swap(gradient.reshape(nz, share, group), "z"))
-        part = total(spread(part, "y"))
-        part = side_by_side(spread(part.astype(low), CELL))
+        part = total(spread(part.astype(low), "y"))
+        part = part.astype(low)
+        if step == 0:
+            part, inverse = lax.optimization_barrier((part, inverse))
+            inverse = in_step_order(inverse, steps, plane, own)
+        part = side_by_side(spread(part, CELL))
         part = product(part, inverse[block], ((1,), (1,)))
         change = spread(part, "z").reshape(nz * share, group)[:high]
         update = product(change.astype(low), kernel[block], ((1,), (0,))).astype(low)

time: 247 us -> 227 us (0.919)
  waiting for transfers between devices: 44.1 us -> 24.5 us
  blocking collectives: 123 us -> 130 us
  local copies, waits for them, and re-layouts: 11.9 us -> 5.44 us
    all_gather x0 -> x1, blocking collectives: none -> 24.6 us  [on_device(): current_low = side_by_side(lax.all_gather(current.astype(low), CELL))]
    all_to_all x6 -> x5, waiting for transfers between devices: 44.1 us -> 23.9 us  [swap(): return lax.all_to_all(pieces, axis, 0, 0, tiled=True)]
    all_to_all x9 -> x8, blocking collectives: 123 us -> 106 us  [swap(): return lax.all_to_all(pieces, axis, 0, 0, tiled=True)]
    ppermute x0 -> x1, starting transfers between devices: none -> 8.79 us  [on_device(): other = lax.ppermute(features, 'c', [(i, (i + 1) % nc) for i in range(nc)])]
    all_to_all x6 -> x5, starting transfers between devices: 38.9 us -> 30.7 us  [swap(): return lax.all_to_all(pieces, axis, 0, 0, tiled=True)]
    reshape x3, local copies, waits for them, and re-layouts: 4.96 us -> 0.7 us  [the longest x1 0.63 us: on_device(): inverse = inverse.reshape(steps * own, -1, cell, span * own).transpose(0,...]
    broadcast_in_dim x10 -> x8, local copies, waits for them, and re-layouts: 4.8 us -> 2.25 us  [spread(): jnp.broadcast_to(piece[None], (lax.axis_size(axis), *piece.shape))]
    dot_general x9 -> x10, matrix products: 7.45 us -> 8.88 us  [product(): lax.dot_general(left, right, (dims, ((), ())), preferred_element_type=jnp...]
  transfers between devices with their start and end apart: 7 -> 7, of which waited for: 6 -> 5; matrix products, arithmetic and copies ran while one was open for 3% -> 5% of each run, Pallas kernels for 0% -> 0%
where the time goes in v3:
time: 227 us; the launch traced here: 226 us
  blocking collectives  130 us (57%)
  starting transfers between devices  39.5 us (17%)
  waiting for transfers between devices  24.5 us (11%)
  between operations  14.4 us (6%)
  matrix products  8.88 us (4%)
  local copies, waits for them, and re-layouts  5.44 us (2%)
  other arithmetic  3.55 us (2%)
    all_to_all x8, blocking collectives, swap(): return lax.all_to_all(pieces, axis, 0, 0, tiled=True)  106 us
    all_to_all x5, starting transfers between devices, swap(): return lax.all_to_all(pieces, axis, 0, 0, tiled=True)  30.7 us
    all_gather x1, blocking collectives, on_device(): current_low = side_by_side(lax.all_gather(current.astype(low), CELL))  24.6 us
    all_to_all x5, waiting for transfers between devices, swap(): return lax.all_to_all(pieces, axis, 0, 0, tiled=True)  23.9 us
    dot_general x10, matrix products, product(): lax.dot_general(left, right, (dims, ((), ())), preferred_element_type=jnp...  8.88 us
    ppermute x1, starting transfers between devices, on_device(): other = lax.ppermute(features, 'c', [(i, (i + 1) % nc) for i in range(nc)])  8.79 us
  transfers between devices with their start and end apart: 7, of which 5 were waited for; matrix products, arithmetic and copies ran while one was open for 5% of the time, Pallas kernels for 0%

profile of v3, /device:TPU:1, one launch (start us, length us, event | category | flops | bytes accessed | tf_op | source)
XLA Modules:
  0.0 226.5 jit_solution(7922359199263880121)
XLA Ops:
  7.3 0.9 convert_bitcast_fusion
  8.2 1.5 fusion.29
  9.7 0.6 reshape.96
  10.4 8.8 %collective-permute-start = (bf16[512,440]{0,1:T(8,128)(2,1)S(1)}, bf16[512,440]{0,1:T(8,128)(2,1)S(1)}, u32[]{:S(2)}, u32[]{:S(2)}) collective-permute-start(bf16[512,440]{0,1:T(8,128)(2,1)S(1)} %copy-done), channel_id=1, source_target_pairs={{0,4},{4,0},{1,5},{5,1},{2,6},{6,2},{3,7},{7,3},{8,12},{12,8},{9,1... | collective-permute-start | bytes 1351688 | tf_op jit(solution)/shard_map/ppermute | solution.py:78
  20.6 0.8 fusion.23
  21.7 28.4 %all_to_all.65 = bf16[64,8,440]{2,1,0:T(8,128)(2,1)S(1)} all-to-all(bf16[64,8,440]{2,1,0:T(8,128)(2,1)S(1)} %bitcast.118), channel_id=1, replica_groups=mesh['z'=8,'y'=8,'c'=2,'x'=4] {'z','y'}, dimensions={0} | all-to-all | bytes 901120 | tf_op jit(solution)/shard_map/all_to_all | solution.py:16
  50.2 0.8 broadcast_in_dim.27
  51.1 6.9 %all-to-all-start.1 = ((bf16[64,8,440]{2,1,0:T(8,128)(2,1)}), bf16[64,8,440]{2,1,0:T(8,128)(2,1)S(1)}, u32[]{:S(2)}, u32[]{:S(2)}) async-start(bf16[64,8,440]{2,1,0:T(8,128)(2,1)} %broadcast_in_dim.27), calls=%async_computation.1 | async-start | bytes 1048576 | tf_op jit(solution)/shard_map/all_to_all | solution.py:16
  58.0 24.6 %all-gather = bf16[1216,128]{1,0:T(8,128)(2,1)S(1)} all-gather(bf16[152,128]{1,0:T(8,128)(2,1)S(1)} %pad_convert_fusion), channel_id=2, replica_groups=mesh['z'=8,'y'=8,'c'=2,'x'=4] {'c','x'}, dimensions={0}, use_global_device_ids=true | all-gather | bytes 350208 | tf_op jit(solution)/shard_map/all_gather | solution.py:76
  83.2 0.9 exponential_convert_fusion
  84.5 0.6 pad.20
  85.1 6.7 %all-to-all-start.2 = ((bf16[8,24,256]{2,1,0:T(8,128)(2,1)}), bf16[8,24,256]{2,1,0:T(8,128)(2,1)S(1)}, u32[]{:S(2)}, u32[]{:S(2)}) async-start(bf16[8,24,256]{2,1,0:T(8,128)(2,1)} %bitcast.11), calls=%async_computation.2 | async-start | bytes 196608 | tf_op jit(solution)/shard_map/all_to_all | solution.py:16
  91.8 8.8 %all-to-all-done.2 = bf16[8,24,256]{2,1,0:T(8,128)(2,1)S(1)} async-done(((bf16[8,24,256]{2,1,0:T(8,128)(2,1)}), bf16[8,24,256]{2,1,0:T(8,128)(2,1)S(1)}, u32[]{:S(2)}, u32[]{:S(2)}) %all-to-all-start.2) | async-done | bytes 98336 | tf_op jit(solution)/shard_map/all_to_all | solution.py:16
  100.6 0.6 broadcast_in_dim.28
  101.3 6.5 %all-to-all-start.3 = ((bf16[8,24,256]{2,1,0:T(8,128)(2,1)}), bf16[8,24,256]{2,1,0:T(8,128)(2,1)S(1)}, u32[]{:S(2)}, u32[]{:S(2)}) async-start(bf16[8,24,256]{2,1,0:T(8,128)(2,1)} %broadcast_in_dim.28), calls=%async_computation.3 | async-start | bytes 196608 | tf_op jit(solution)/shard_map/all_to_all | solution.py:16
  107.8 7.4 %all-to-all-done.3 = bf16[8,24,256]{2,1,0:T(8,128)(2,1)S(1)} async-done(((bf16[8,24,256]{2,1,0:T(8,128)(2,1)}), bf16[8,24,256]{2,1,0:T(8,128)(2,1)S(1)}, u32[]{:S(2)}, u32[]{:S(2)}) %all-to-all-start.3) | async-done | bytes 98336 | tf_op jit(solution)/shard_map/all_to_all | solution.py:16
  115.3 0.6 broadcast_in_dim.29
  115.9 5.8 %all-to-all-start.4 = ((bf16[8,24,256]{2,1,0:T(8,128)(2,1)}), bf16[8,24,256]{2,1,0:T(8,128)(2,1)S(1)}, u32[]{:S(2)}, u32[]{:S(2)}) async-start(bf16[8,24,256]{2,1,0:T(8,128)(2,1)} %broadcast_in_dim.29), calls=%async_computation.4 | async-start | bytes 196608 | tf_op jit(solution)/shard_map/all_to_all | solution.py:16
  121.7 3.8 %convolution_convert_fusion = bf16[512,2048]{1,0:T(8,128)(2,1)S(1)} fusion(bf16[512,2048]{1,0:T(8,128)(2,1)} %all-gather.3.cloned.1.call-done, s32[512]{0:T(512)S(1)} %get-tuple-element.52, s32[512]{0:T(512)S(1)} %get-tuple-element.53, s32[512]{0:T(512)S(1)} %get-tuple-element.50, s32[512]{0:T(512)S(1)} %get-tuple-element.56, ...), kind=kOutput, calls=%fused_computation.12 | convolution fusion | flops 1079771136 | bytes 4208128 | tf_op jit(solution)/shard_map/dot_general | solution.py:33
  125.5 1.2 all-to-all-done.4
  127.2 12.4 %all_to_all.66 = f32[8,24,256]{2,1,0:T(8,128)S(1)} all-to-all(f32[8,24,256]{2,1,0:T(8,128)S(1)} %broadcast_in_dim.30), channel_id=1, replica_groups=mesh['z'=8,'y'=8,'c'=2,'x'=4] {'z'}, dimensions={0} | all-to-all | bytes 393216 | tf_op jit(solution)/shard_map/all_to_all | solution.py:16
  139.8 12.0 %all_to_all.67 = bf16[8,152,128]{2,1,0:T(8,128)(2,1)S(1)} all-to-all(bf16[8,152,128]{2,1,0:T(8,128)(2,1)S(1)} %bitcast.124), channel_id=1, replica_groups=mesh['z'=8,'y'=8,'c'=2,'x'=4] {'c','x'}, dimensions={0} | all-to-all | bytes 622592 | tf_op jit(solution)/shard_map/all_to_all | solution.py:16
  151.9 10.3 %all_to_all.68 = bf16[8,152,128]{2,1,0:T(8,128)(2,1)S(1)} all-to-all(bf16[8,152,128]{2,1,0:T(8,128)(2,1)S(1)} %broadcast_in_dim.31), channel_id=1, replica_groups=mesh['z'=8,'y'=8,'c'=2,'x'=4] {'c','x'}, dimensions={0} | all-to-all | bytes 622592 | tf_op jit(solution)/shard_map/all_to_all | solution.py:16
  162.6 9.9 %all_to_all.69 = bf16[8,24,256]{2,1,0:T(8,128)(2,1)S(1)} all-to-all(bf16[8,24,256]{2,1,0:T(8,128)(2,1)S(1)} %bitcast.129), channel_id=1, replica_groups=mesh['z'=8,'y'=8,'c'=2,'x'=4] {'z'}, dimensions={0} | all-to-all | bytes 196608 | tf_op jit(solution)/shard_map/all_to_all | solution.py:16
  172.6 10.0 %all_to_all.70 = bf16[8,24,256]{2,1,0:T(8,128)(2,1)S(1)} all-to-all(bf16[8,24,256]{2,1,0:T(8,128)(2,1)S(1)} %broadcast_in_dim.32), channel_id=1, replica_groups=mesh['z'=8,'y'=8,'c'=2,'x'=4] {'y'}, dimensions={0} | all-to-all | bytes 196608 | tf_op jit(solution)/shard_map/all_to_all | solution.py:16
  182.6 10.3 %all_to_all.71 = bf16[8,24,256]{2,1,0:T(8,128)(2,1)S(1)} all-to-all(bf16[8,24,256]{2,1,0:T(8,128)(2,1)S(1)} %broadcast_in_dim.33), channel_id=1, replica_groups=mesh['z'=8,'y'=8,'c'=2,'x'=4] {'c','x'}, dimensions={0} | all-to-all | bytes 196608 | tf_op jit(solution)/shard_map/all_to_all | solution.py:16
  193.3 12.4 %all_to_all.72 = f32[8,24,256]{2,1,0:T(8,128)S(1)} all-to-all(f32[8,24,256]{2,1,0:T(8,128)S(1)} %broadcast_in_dim.34), channel_id=1, replica_groups=mesh['z'=8,'y'=8,'c'=2,'x'=4] {'z'}, dimensions={0} | all-to-all | bytes 393216 | tf_op jit(solution)/shard_map/all_to_all | solution.py:16
  206.3 0.8 copy.69
  207.1 4.8 %all-to-all-start.12 = ((bf16[8,152,128]{2,1,0:T(8,128)(2,1)}), bf16[8,152,128]{2,1,0:T(8,128)(2,1)S(1)}, u32[]{:S(2)}, u32[]{:S(2)}) async-start(bf16[8,152,128]{2,1,0:T(8,128)(2,1)} %bitcast.106), calls=%async_computation.12 | async-start | bytes 622592 | tf_op jit(solution)/shard_map/all_to_all | solution.py:16
  211.9 0.6 pad_maximum_fusion.3
  212.5 6.5 %all-to-all-done.12 = bf16[8,152,128]{2,1,0:T(8,128)(2,1)S(1)} async-done(((bf16[8,152,128]{2,1,0:T(8,128)(2,1)}), bf16[8,152,128]{2,1,0:T(8,128)(2,1)S(1)}, u32[]{:S(2)}, u32[]{:S(2)}) %all-to-all-start.12) | async-done | bytes 311328 | tf_op jit(solution)/shard_map/all_to_all | solution.py:16
  219.0 0.6 fusion.113
  (64 shorter events, 5.3 us)
Async XLA Ops:
  7.2 108.1 %all-gather.3.cloned.1.call-start = ((), (), s32[]{:S(2)}) async-start(), calls=%async_computation.13 | async-start | bytes 2129920 | tf_op jit(solution)/shard_map/all_gather | solution.py:74
  8.2 2.2 copy-start
  8.2 11.0 %copy-start.3 = (s32[2,2048]{1,0:T(2,128)S(1)}, s32[2,2048]{1,0:T(2,128)}, u32[]{:S(2)}) copy-start(s32[2,2048]{1,0:T(2,128)} %param.9) | copy-start | bytes 49156
  10.4 10.2 %collective-permute-start = (bf16[512,440]{0,1:T(8,128)(2,1)S(1)}, bf16[512,440]{0,1:T(8,128)(2,1)S(1)}, u32[]{:S(2)}, u32[]{:S(2)}) collective-permute-start(bf16[512,440]{0,1:T(8,128)(2,1)S(1)} %copy-done), channel_id=1, source_target_pairs={{0,4},{4,0},{1,5},{5,1},{2,6},{6,2},{3,7},{7,3},{8,12},{12,8},{9,1... | collective-permute-start | bytes 1351688 | tf_op jit(solution)/shard_map/ppermute | solution.py:78
  21.4 36.5 %copy-start.1 = (f32[128,147]{0,1:T(8,128)S(1)}, f32[128,147]{0,1:T(8,128)}, u32[]{:S(2)}) copy-start(f32[128,147]{0,1:T(8,128)} %param.6) | copy-start | bytes 225796
  21.7 61.0 %copy-start.2 = (f32[2,4,147]{2,1,0:T(4,128)S(1)}, f32[2,4,147]{2,1,0:T(4,128)}, u32[]{:S(2)}) copy-start(f32[2,4,147]{2,1,0:T(4,128)} %param.7) | copy-start | bytes 14116
  51.1 31.9 %all-to-all-start.1 = ((bf16[64,8,440]{2,1,0:T(8,128)(2,1)}), bf16[64,8,440]{2,1,0:T(8,128)(2,1)S(1)}, u32[]{:S(2)}, u32[]{:S(2)}) async-start(bf16[64,8,440]{2,1,0:T(8,128)(2,1)} %broadcast_in_dim.27), calls=%async_computation.1 | async-start | bytes 1048576 | tf_op jit(solution)/shard_map/all_to_all | solution.py:16
  85.1 15.5 %all-to-all-start.2 = ((bf16[8,24,256]{2,1,0:T(8,128)(2,1)}), bf16[8,24,256]{2,1,0:T(8,128)(2,1)S(1)}, u32[]{:S(2)}, u32[]{:S(2)}) async-start(bf16[8,24,256]{2,1,0:T(8,128)(2,1)} %bitcast.11), calls=%async_computation.2 | async-start | bytes 196608 | tf_op jit(solution)/shard_map/all_to_all | solution.py:16
  101.3 14.0 %all-to-all-start.3 = ((bf16[8,24,256]{2,1,0:T(8,128)(2,1)}), bf16[8,24,256]{2,1,0:T(8,128)(2,1)S(1)}, u32[]{:S(2)}, u32[]{:S(2)}) async-start(bf16[8,24,256]{2,1,0:T(8,128)(2,1)} %broadcast_in_dim.28), calls=%async_computation.3 | async-start | bytes 196608 | tf_op jit(solution)/shard_map/all_to_all | solution.py:16
  115.9 10.8 %all-to-all-start.4 = ((bf16[8,24,256]{2,1,0:T(8,128)(2,1)}), bf16[8,24,256]{2,1,0:T(8,128)(2,1)S(1)}, u32[]{:S(2)}, u32[]{:S(2)}) async-start(bf16[8,24,256]{2,1,0:T(8,128)(2,1)} %broadcast_in_dim.29), calls=%async_computation.4 | async-start | bytes 196608 | tf_op jit(solution)/shard_map/all_to_all | solution.py:16
  207.1 11.9 %all-to-all-start.12 = ((bf16[8,152,128]{2,1,0:T(8,128)(2,1)}), bf16[8,152,128]{2,1,0:T(8,128)(2,1)S(1)}, u32[]{:S(2)}, u32[]{:S(2)}) async-start(bf16[8,152,128]{2,1,0:T(8,128)(2,1)} %bitcast.106), calls=%async_computation.12 | async-start | bytes 622592 | tf_op jit(solution)/shard_map/all_to_all | solution.py:16
Sparse Core Ops, SparseCore 0:
  11.6 95.0 all-gather.2

commit v4 on v3

--- a/solution.py
+++ b/solution.py
@@ -18,6 +18,11 @@
 
 def spread(piece, axis):
     return swap(jnp.broadcast_to(piece[None], (lax.axis_size(axis), *piece.shape)), axis)
+
+
+def both(piece, first):
+    other = lax.ppermute(piece, "c", [(0, 1), (1, 0)])
+    return jnp.stack([jnp.where(first, piece, other), jnp.where(first, other, piece)])
 
 
 def total(pieces):
@@ -73,13 +78,12 @@
     )
     inverse = lax.all_gather(inverse, PLANE, axis=0, tiled=True)
     current = jnp.pad(residual.T, ((0, high - classes), (0, 0)))
-    current_low = side_by_side(lax.all_gather(current.astype(low), CELL))
+    first = lax.axis_index("c") == 0
+    pair = both(current.astype(low), first)
+    pair = lax.all_gather(pair, "x")
+    current_low = side_by_side(pair.swapaxes(0, 1).reshape(cell, high, own_rows))
 
-    other = lax.ppermute(features, "c", [(i, (i + 1) % nc) for i in range(nc)])
-    first = lax.axis_index("c") == 0
-    frames = jnp.concatenate(
-        [jnp.where(first, features, other), jnp.where(first, other, features)]
-    )
+    frames = both(features, first).reshape(nc * features.shape[0], width)
     rows = frames.shape[0]
     chosen = lax.dynamic_index_in_dim(
         block_columns.reshape(steps, plane, cell, own), member, 2, keepdims=False
@@ -115,9 +119,9 @@
             part, inverse = lax.optimization_barrier((part, inverse))
             inverse = in_step_order(inverse, steps, plane, own)
         part = side_by_side(spread(part, CELL))
-        part = product(part, inverse[block], ((1,), (1,)))
+        part = product(part, inverse[block], ((1,), (1,))).astype(low)
         change = spread(part, "z").reshape(nz * share, group)[:high]
-        update = product(change.astype(low), kernel[block], ((1,), (0,))).astype(low)
+        update = product(change, kernel[block], ((1,), (0,))).astype(low)
         update = update.reshape(high, cell, own_rows).transpose(1, 0, 2)
         current = current - total(swap(update, CELL))
         if step < steps - 1:

time: 227 us -> 222 us (0.978)
  blocking collectives: 130 us -> 87.7 us
  waiting for transfers between devices: 24.5 us -> 48.8 us
  starting transfers between devices: 39.5 us -> 51.4 us
    all_to_all x8 -> x7, blocking collectives: 106 us -> 77 us  [swap(): return lax.all_to_all(pieces, axis, 0, 0, tiled=True)]
    all_to_all x5 -> x6, waiting for transfers between devices: 23.9 us -> 43.9 us  [swap(): return lax.all_to_all(pieces, axis, 0, 0, tiled=True)]
    all_gather x1, blocking collectives: 24.6 us -> 10.8 us  [on_device(): pair = lax.all_gather(pair, 'x')]
    all_to_all x5 -> x6, starting transfers between devices: 30.7 us -> 40.1 us  [swap(): return lax.all_to_all(pieces, axis, 0, 0, tiled=True)]
    all_gather x1, waiting for transfers between devices: 0.02 us -> 4.35 us  [on_device(): inverse = lax.all_gather(inverse, PLANE, axis=0, tiled=True)]
    ppermute x1 -> x2, starting transfers between devices: 8.79 us -> 11.3 us  [both(): other = lax.ppermute(piece, 'c', [(0, 1), (1, 0)])]
  transfers between devices with their start and end apart: 7 -> 9, of which waited for: 5 -> 8; matrix products, arithmetic and copies ran while one was open for 5% -> 5% of each run, Pallas kernels for 0% -> 0%
where the time goes in v4:
time: 222 us; the launch traced here: 221 us
  blocking collectives  87.7 us (40%)
  starting transfers between devices  51.4 us (23%)
  waiting for transfers between devices  48.8 us (22%)
  between operations  14.5 us (7%)
  matrix products  8.91 us (4%)
  local copies, waits for them, and re-layouts  6.34 us (3%)
  other arithmetic  3.66 us (2%)
    all_to_all x7, blocking collectives, swap(): return lax.all_to_all(pieces, axis, 0, 0, tiled=True)  77 us
    all_to_all x6, waiting for transfers between devices, swap(): return lax.all_to_all(pieces, axis, 0, 0, tiled=True)  43.9 us
    all_to_all x6, starting transfers between devices, swap(): return lax.all_to_all(pieces, axis, 0, 0, tiled=True)  40.1 us
    ppermute x2, starting transfers between devices, both(): other = lax.ppermute(piece, 'c', [(0, 1), (1, 0)])  11.3 us
    all_gather x1, blocking collectives, on_device(): pair = lax.all_gather(pair, 'x')  10.8 us
    dot_general x10, matrix products, product(): lax.dot_general(left, right, (dims, ((), ())), preferred_element_type=jnp...  8.91 us
  transfers between devices with their start and end apart: 9, of which 8 were waited for; matrix products, arithmetic and copies ran while one was open for 5% of the time, Pallas kernels for 0%

profile of v4, /device:TPU:1, one launch (start us, length us, event | category | flops | bytes accessed | tf_op | source)
XLA Modules:
  0.0 221.3 jit_solution(3364023224955181681)
XLA Ops:
  7.3 0.9 convert_bitcast_fusion
  8.2 1.5 fusion.29
  10.4 8.8 %collective-permute-start.1 = (bf16[512,440]{0,1:T(8,128)(2,1)S(1)}, bf16[512,440]{0,1:T(8,128)(2,1)S(1)}, u32[]{:S(2)}, u32[]{:S(2)}) collective-permute-start(bf16[512,440]{0,1:T(8,128)(2,1)S(1)} %copy-done.1), channel_id=1, source_target_pairs={{0,4},{4,0},{1,5},{5,1},{2,6},{6,2},{3,7},{7,3},{8,12},{12,8},{9,1... | collective-permute-start | bytes 1351688 | tf_op jit(solution)/shard_map/ppermute | solution.py:24
  20.9 0.8 fusion.23
  21.7 1.0 copy.33
  22.7 10.9 %all-to-all-start = ((bf16[64,8,440]{2,1,0:T(8,128)(2,1)}), bf16[64,8,440]{2,1,0:T(8,128)(2,1)S(1)}, u32[]{:S(2)}, u32[]{:S(2)}) async-start(bf16[64,8,440]{2,1,0:T(8,128)(2,1)} %bitcast.9), calls=%async_computation | async-start | bytes 1048576 | tf_op jit(solution)/shard_map/all_to_all | solution.py:16
  33.7 2.5 %collective-permute-start = (bf16[152,128]{1,0:T(8,128)(2,1)S(1)}, bf16[152,128]{1,0:T(8,128)(2,1)S(1)}, u32[]{:S(2)}, u32[]{:S(2)}) collective-permute-start(bf16[152,128]{1,0:T(8,128)(2,1)S(1)} %pad_convert_fusion), channel_id=1, source_target_pairs={{0,4},{4,0},{1,5},{5,1},{2,6},{6,2},{3,7},{7,3},{8,12},{12,8},{9,1... | collective-permute-start | bytes 116744 | tf_op jit(solution)/shard_map/ppermute | solution.py:24
  36.2 15.5 %all-to-all-done = bf16[64,8,440]{2,1,0:T(8,128)(2,1)S(1)} async-done(((bf16[64,8,440]{2,1,0:T(8,128)(2,1)}), bf16[64,8,440]{2,1,0:T(8,128)(2,1)S(1)}, u32[]{:S(2)}, u32[]{:S(2)}) %all-to-all-start) | async-done | bytes 450592 | tf_op jit(solution)/shard_map/all_to_all | solution.py:16
  51.8 0.8 broadcast_in_dim.27
  52.7 6.7 %all-to-all-start.1 = ((bf16[64,8,440]{2,1,0:T(8,128)(2,1)}), bf16[64,8,440]{2,1,0:T(8,128)(2,1)S(1)}, u32[]{:S(2)}, u32[]{:S(2)}) async-start(bf16[64,8,440]{2,1,0:T(8,128)(2,1)} %broadcast_in_dim.27), calls=%async_computation.1 | async-start | bytes 1048576 | tf_op jit(solution)/shard_map/all_to_all | solution.py:16
  59.5 10.8 %all-gather = bf16[8,152,128]{2,1,0:T(8,128)(2,1)S(1)} all-gather(bf16[2,152,128]{2,1,0:T(8,128)(2,1)S(1)} %pad_maximum_fusion.1), channel_id=2, replica_groups=mesh['z'=8,'y'=8,'c'=2,'x'=4] {'x'}, dimensions={0}, use_global_device_ids=true | all-gather | bytes 389120 | tf_op jit(solution)/shard_map/all_gather | solution.py:83
  70.5 5.2 %all-to-all-done.1 = bf16[64,8,440]{2,1,0:T(8,128)(2,1)S(1)} async-done(((bf16[64,8,440]{2,1,0:T(8,128)(2,1)}), bf16[64,8,440]{2,1,0:T(8,128)(2,1)S(1)}, u32[]{:S(2)}, u32[]{:S(2)}) %all-to-all-start.1) | async-done | bytes 450592 | tf_op jit(solution)/shard_map/all_to_all | solution.py:16
  75.9 0.9 exponential_convert_fusion
  77.8 4.5 %all-to-all-start.2 = ((bf16[8,24,256]{2,1,0:T(8,128)(2,1)}), bf16[8,24,256]{2,1,0:T(8,128)(2,1)S(1)}, u32[]{:S(2)}, u32[]{:S(2)}) async-start(bf16[8,24,256]{2,1,0:T(8,128)(2,1)} %bitcast.17), calls=%async_computation.2 | async-start | bytes 196608 | tf_op jit(solution)/shard_map/all_to_all | solution.py:16
  82.3 7.8 %all-to-all-done.2 = bf16[8,24,256]{2,1,0:T(8,128)(2,1)S(1)} async-done(((bf16[8,24,256]{2,1,0:T(8,128)(2,1)}), bf16[8,24,256]{2,1,0:T(8,128)(2,1)S(1)}, u32[]{:S(2)}, u32[]{:S(2)}) %all-to-all-start.2) | async-done | bytes 98336 | tf_op jit(solution)/shard_map/all_to_all | solution.py:16
  90.8 4.0 %all-to-all-start.3 = ((bf16[8,24,256]{2,1,0:T(8,128)(2,1)}), bf16[8,24,256]{2,1,0:T(8,128)(2,1)S(1)}, u32[]{:S(2)}, u32[]{:S(2)}) async-start(bf16[8,24,256]{2,1,0:T(8,128)(2,1)} %broadcast_in_dim.28), calls=%async_computation.3 | async-start | bytes 196608 | tf_op jit(solution)/shard_map/all_to_all | solution.py:16
  94.8 7.7 %all-to-all-done.3 = bf16[8,24,256]{2,1,0:T(8,128)(2,1)S(1)} async-done(((bf16[8,24,256]{2,1,0:T(8,128)(2,1)}), bf16[8,24,256]{2,1,0:T(8,128)(2,1)S(1)}, u32[]{:S(2)}, u32[]{:S(2)}) %all-to-all-start.3) | async-done | bytes 98336 | tf_op jit(solution)/shard_map/all_to_all | solution.py:16
  102.6 4.4 %all-gather.3.cloned.1.call-done = bf16[512,2048]{1,0:T(8,128)(2,1)} async-done(((bf16[8,2048]{1,0:T(8,128)(2,1)}), bf16[512,2048]{1,0:T(8,128)(2,1)}) %all-gather.3.cloned.1.call-update) | async-done | bytes 2097168 | tf_op jit(solution)/shard_map/all_gather | solution.py:79
  107.6 8.9 %all-to-all-start.4 = ((bf16[8,24,256]{2,1,0:T(8,128)(2,1)}), bf16[8,24,256]{2,1,0:T(8,128)(2,1)S(1)}, u32[]{:S(2)}, u32[]{:S(2)}) async-start(bf16[8,24,256]{2,1,0:T(8,128)(2,1)} %broadcast_in_dim.29), calls=%async_computation.4 | async-start | bytes 196608 | tf_op jit(solution)/shard_map/all_to_all | solution.py:16
  116.4 3.8 %convolution_convert_fusion = bf16[512,2048]{1,0:T(8,128)(2,1)S(1)} fusion(bf16[512,2048]{1,0:T(8,128)(2,1)} %all-gather.3.cloned.1.call-done, s32[512]{0:T(512)S(1)} %get-tuple-element.54, s32[512]{0:T(512)S(1)} %get-tuple-element.55, s32[512]{0:T(512)S(1)} %get-tuple-element.52, s32[512]{0:T(512)S(1)} %get-tuple-element.58, ...), kind=kOutput, calls=%fused_computation.12 | convolution fusion | flops 1079771136 | bytes 4208128 | tf_op jit(solution)/shard_map/dot_general | solution.py:38
  120.2 1.2 all-to-all-done.4
  121.9 11.4 %all_to_all.65 = bf16[8,24,256]{2,1,0:T(8,128)(2,1)S(1)} all-to-all(bf16[8,24,256]{2,1,0:T(8,128)(2,1)S(1)} %broadcast_in_dim.30), channel_id=1, replica_groups=mesh['z'=8,'y'=8,'c'=2,'x'=4] {'z'}, dimensions={0} | all-to-all | bytes 196608 | tf_op jit(solution)/shard_map/all_to_all | solution.py:16
  133.6 12.5 %all_to_all.66 = bf16[8,152,128]{2,1,0:T(8,128)(2,1)S(1)} all-to-all(bf16[8,152,128]{2,1,0:T(8,128)(2,1)S(1)} %bitcast.130), channel_id=1, replica_groups=mesh['z'=8,'y'=8,'c'=2,'x'=4] {'c','x'}, dimensions={0} | all-to-all | bytes 622592 | tf_op jit(solution)/shard_map/all_to_all | solution.py:16
  146.3 10.3 %all_to_all.67 = bf16[8,152,128]{2,1,0:T(8,128)(2,1)S(1)} all-to-all(bf16[8,152,128]{2,1,0:T(8,128)(2,1)S(1)} %broadcast_in_dim.31), channel_id=1, replica_groups=mesh['z'=8,'y'=8,'c'=2,'x'=4] {'c','x'}, dimensions={0} | all-to-all | bytes 622592 | tf_op jit(solution)/shard_map/all_to_all | solution.py:16
  156.9 9.9 %all_to_all.68 = bf16[8,24,256]{2,1,0:T(8,128)(2,1)S(1)} all-to-all(bf16[8,24,256]{2,1,0:T(8,128)(2,1)S(1)} %bitcast.144), channel_id=1, replica_groups=mesh['z'=8,'y'=8,'c'=2,'x'=4] {'z'}, dimensions={0} | all-to-all | bytes 196608 | tf_op jit(solution)/shard_map/all_to_all | solution.py:16
  166.9 12.3 %all_to_all.69 = bf16[8,24,256]{2,1,0:T(8,128)(2,1)S(1)} all-to-all(bf16[8,24,256]{2,1,0:T(8,128)(2,1)S(1)} %broadcast_in_dim.32), channel_id=1, replica_groups=mesh['z'=8,'y'=8,'c'=2,'x'=4] {'y'}, dimensions={0} | all-to-all | bytes 196608 | tf_op jit(solution)/shard_map/all_to_all | solution.py:16
  179.3 10.5 %all_to_all.70 = bf16[8,24,256]{2,1,0:T(8,128)(2,1)S(1)} all-to-all(bf16[8,24,256]{2,1,0:T(8,128)(2,1)S(1)} %broadcast_in_dim.33), channel_id=1, replica_groups=mesh['z'=8,'y'=8,'c'=2,'x'=4] {'c','x'}, dimensions={0} | all-to-all | bytes 196608 | tf_op jit(solution)/shard_map/all_to_all | solution.py:16
  190.2 9.9 %all_to_all.71 = bf16[8,24,256]{2,1,0:T(8,128)(2,1)S(1)} all-to-all(bf16[8,24,256]{2,1,0:T(8,128)(2,1)S(1)} %broadcast_in_dim.34), channel_id=1, replica_groups=mesh['z'=8,'y'=8,'c'=2,'x'=4] {'z'}, dimensions={0} | all-to-all | bytes 196608 | tf_op jit(solution)/shard_map/all_to_all | solution.py:16
  200.8 0.8 copy.82
  201.6 5.1 %all-to-all-start.12 = ((bf16[8,152,128]{2,1,0:T(8,128)(2,1)}), bf16[8,152,128]{2,1,0:T(8,128)(2,1)S(1)}, u32[]{:S(2)}, u32[]{:S(2)}) async-start(bf16[8,152,128]{2,1,0:T(8,128)(2,1)} %bitcast.117), calls=%async_computation.12 | async-start | bytes 622592 | tf_op jit(solution)/shard_map/all_to_all | solution.py:16
  207.3 6.5 %all-to-all-done.12 = bf16[8,152,128]{2,1,0:T(8,128)(2,1)S(1)} async-done(((bf16[8,152,128]{2,1,0:T(8,128)(2,1)}), bf16[8,152,128]{2,1,0:T(8,128)(2,1)S(1)}, u32[]{:S(2)}, u32[]{:S(2)}) %all-to-all-start.12) | async-done | bytes 311328 | tf_op jit(solution)/shard_map/all_to_all | solution.py:16
  213.8 0.6 fusion.112
  (80 shorter events, 8.4 us)
Async XLA Ops:
  7.2 99.8 %all-gather.3.cloned.1.call-start = ((), (), s32[]{:S(2)}) async-start(), calls=%async_computation.13 | async-start | bytes 2129920 | tf_op jit(solution)/shard_map/all_gather | solution.py:79
  8.2 2.2 copy-start.1
  8.2 11.0 %copy-start.3 = (s32[2,2048]{1,0:T(2,128)S(1)}, s32[2,2048]{1,0:T(2,128)}, u32[]{:S(2)}) copy-start(s32[2,2048]{1,0:T(2,128)} %param.9) | copy-start | bytes 49156
  10.4 10.2 %collective-permute-start.1 = (bf16[512,440]{0,1:T(8,128)(2,1)S(1)}, bf16[512,440]{0,1:T(8,128)(2,1)S(1)}, u32[]{:S(2)}, u32[]{:S(2)}) collective-permute-start(bf16[512,440]{0,1:T(8,128)(2,1)S(1)} %copy-done.1), channel_id=1, source_target_pairs={{0,4},{4,0},{1,5},{5,1},{2,6},{6,2},{3,7},{7,3},{8,12},{12,8},{9,1... | collective-permute-start | bytes 1351688 | tf_op jit(solution)/shard_map/ppermute | solution.py:24
  20.8 12.8 %copy-start = (f32[128,147]{0,1:T(8,128)S(1)}, f32[128,147]{0,1:T(8,128)}, u32[]{:S(2)}) copy-start(f32[128,147]{0,1:T(8,128)} %param.6) | copy-start | bytes 225796
  20.8 15.4 %copy-start.2 = (f32[2,4,147]{2,1,0:T(4,128)S(1)}, f32[2,4,147]{2,1,0:T(4,128)}, u32[]{:S(2)}) copy-start(f32[2,4,147]{2,1,0:T(4,128)} %param.7) | copy-start | bytes 14116
  22.7 29.0 %all-to-all-start = ((bf16[64,8,440]{2,1,0:T(8,128)(2,1)}), bf16[64,8,440]{2,1,0:T(8,128)(2,1)S(1)}, u32[]{:S(2)}, u32[]{:S(2)}) async-start(bf16[64,8,440]{2,1,0:T(8,128)(2,1)} %bitcast.9), calls=%async_computation | async-start | bytes 1048576 | tf_op jit(solution)/shard_map/all_to_all | solution.py:16
  33.7 25.8 %collective-permute-start = (bf16[152,128]{1,0:T(8,128)(2,1)S(1)}, bf16[152,128]{1,0:T(8,128)(2,1)S(1)}, u32[]{:S(2)}, u32[]{:S(2)}) collective-permute-start(bf16[152,128]{1,0:T(8,128)(2,1)S(1)} %pad_convert_fusion), channel_id=1, source_target_pairs={{0,4},{4,0},{1,5},{5,1},{2,6},{6,2},{3,7},{7,3},{8,12},{12,8},{9,1... | collective-permute-start | bytes 116744 | tf_op jit(solution)/shard_map/ppermute | solution.py:24
  52.7 23.0 %all-to-all-start.1 = ((bf16[64,8,440]{2,1,0:T(8,128)(2,1)}), bf16[64,8,440]{2,1,0:T(8,128)(2,1)S(1)}, u32[]{:S(2)}, u32[]{:S(2)}) async-start(bf16[64,8,440]{2,1,0:T(8,128)(2,1)} %broadcast_in_dim.27), calls=%async_computation.1 | async-start | bytes 1048576 | tf_op jit(solution)/shard_map/all_to_all | solution.py:16
  77.8 12.3 %all-to-all-start.2 = ((bf16[8,24,256]{2,1,0:T(8,128)(2,1)}), bf16[8,24,256]{2,1,0:T(8,128)(2,1)S(1)}, u32[]{:S(2)}, u32[]{:S(2)}) async-start(bf16[8,24,256]{2,1,0:T(8,128)(2,1)} %bitcast.17), calls=%async_computation.2 | async-start | bytes 196608 | tf_op jit(solution)/shard_map/all_to_all | solution.py:16
  90.8 11.7 %all-to-all-start.3 = ((bf16[8,24,256]{2,1,0:T(8,128)(2,1)}), bf16[8,24,256]{2,1,0:T(8,128)(2,1)S(1)}, u32[]{:S(2)}, u32[]{:S(2)}) async-start(bf16[8,24,256]{2,1,0:T(8,128)(2,1)} %broadcast_in_dim.28), calls=%async_computation.3 | async-start | bytes 196608 | tf_op jit(solution)/shard_map/all_to_all | solution.py:16
  107.6 13.9 %all-to-all-start.4 = ((bf16[8,24,256]{2,1,0:T(8,128)(2,1)}), bf16[8,24,256]{2,1,0:T(8,128)(2,1)S(1)}, u32[]{:S(2)}, u32[]{:S(2)}) async-start(bf16[8,24,256]{2,1,0:T(8,128)(2,1)} %broadcast_in_dim.29), calls=%async_computation.4 | async-start | bytes 196608 | tf_op jit(solution)/shard_map/all_to_all | solution.py:16
  201.6 12.2 %all-to-all-start.12 = ((bf16[8,152,128]{2,1,0:T(8,128)(2,1)}), bf16[8,152,128]{2,1,0:T(8,128)(2,1)S(1)}, u32[]{:S(2)}, u32[]{:S(2)}) async-start(bf16[8,152,128]{2,1,0:T(8,128)(2,1)} %bitcast.117), calls=%async_computation.12 | async-start | bytes 622592 | tf_op jit(solution)/shard_map/all_to_all | solution.py:16
Sparse Core Ops, SparseCore 0:
  11.6 95.2 all-gather.2

commit v5 on v4

--- a/solution.py
+++ b/solution.py
@@ -3,6 +3,8 @@
 import jax
 import jax.numpy as jnp
 from jax import lax
+from jax.experimental import pallas as pl
+from jax.experimental.pallas import tpu as pltpu
 from jax.sharding import Mesh
 from jax.sharding import PartitionSpec as P
 
@@ -40,12 +42,47 @@
     )
 
 
-def in_step_order(rows, steps, plane, own):
-    count = steps * plane * own
-    row = lax.broadcasted_iota(jnp.int32, (count, count), 0)
-    source = (row // own % plane) * (steps * own) + row // (plane * own) * own + row % own
-    order = source == lax.broadcasted_iota(jnp.int32, (count, count), 1)
-    return product(order.astype(rows.dtype), rows, ((1,), (0,))).astype(rows.dtype)
+def arranged(rows, plane, cell):
+    steps, own, columns = rows.shape
+    count = steps * own
+    if columns % 2048 or count != 8 or cell * own != 32:
+        rows = rows.astype(jnp.bfloat16).reshape(count, plane, cell, own)
+        return rows.transpose(0, 2, 1, 3).reshape(count, columns)
+    blocks = columns // 128
+    run = 128 // cell
+
+    def kernel(rows_ref, out_ref):
+        tall = jnp.concatenate([rows_ref[step] for step in range(steps)], axis=0)
+        tall = jnp.concatenate([tall[:, 128 * q : 128 * (q + 1)] for q in range(blocks)], axis=0)
+        source = lax.broadcasted_iota(jnp.int32, (128, 128), 0)
+        target = lax.broadcasted_iota(jnp.int32, (128, 128), 1)
+        member, lane = (source >> 2) & 7, ((source >> 5) << 2) | (source & 3)
+        order = jnp.where(member * run + lane == target, 1.0, 0.0).astype(jnp.bfloat16)
+        tall = jnp.dot(tall.astype(jnp.bfloat16), order, preferred_element_type=jnp.float32)
+        part = lax.broadcasted_iota(jnp.int32, (count, 128), 1) >> 4
+        for out in range(blocks):
+            member, first = out * cell // blocks, out % (blocks // cell) * cell
+            joined = jnp.zeros((count, 128), jnp.float32)
+            for k in range(cell):
+                q = first + k
+                piece = tall[count * q : count * (q + 1)]
+                if k != member:
+                    piece = pltpu.roll(piece, (k - member) * run % 128, 1)
+                joined = jnp.where(part == k, piece, joined)
+            out_ref[:, 128 * out : 128 * (out + 1)] = joined.astype(out_ref.dtype)
+
+    return pl.pallas_call(
+        kernel,
+        out_shape=jax.ShapeDtypeStruct((count, columns), jnp.bfloat16),
+        name="arrange",
+    )(rows)
+
+
+def step_places(step, steps, plane, own):
+    shape = (plane * own, steps * plane * own)
+    row = lax.broadcasted_iota(jnp.int32, shape, 0)
+    source = row // own * (steps * own) + step * own + row % own
+    return (source == lax.broadcasted_iota(jnp.int32, shape, 1)).astype(jnp.bfloat16)
 
 
 def on_device(features, residual, block_weights, block_inverse, block_columns):
@@ -59,23 +96,11 @@
     group = plane * own
     high = -(-classes // 8) * 8
     share = -(-classes // (nz * 8)) * 8
+    tall = nz * share
     gamma_rate = 4.0 / width
     low = jnp.bfloat16
 
-    span = min(plane, 128 // own)
-    row = lax.broadcasted_iota(jnp.int32, (cell * span * own, cell * span * own), 0)
-    col = lax.broadcasted_iota(jnp.int32, row.shape, 1)
-    there = row // own % cell * (span * own) + row // (own * cell) * own + row % own
-    inverse = product(
-        block_inverse.transpose(0, 2, 1).astype(low).reshape(steps * own, -1, row.shape[0]),
-        (there == col).astype(low),
-        ((2,), (0,)),
-    ).astype(low)
-    inverse = (
-        inverse.reshape(steps * own, -1, cell, span * own)
-        .transpose(0, 2, 1, 3)
-        .reshape(steps * own, columns)
-    )
+    inverse = arranged(block_inverse.transpose(0, 2, 1), plane, cell)
     inverse = lax.all_gather(inverse, PLANE, axis=0, tiled=True)
     current = jnp.pad(residual.T, ((0, high - classes), (0, 0)))
     first = lax.axis_index("c") == 0
@@ -103,31 +128,37 @@
         -gamma_rate * (frame_sq[None, :] + center_sq[:, None] - 2.0 * cross)
     ).astype(low)
 
-    lanes = lax.broadcasted_iota(jnp.int32, (high, group), 1) - place * own
+    lanes = lax.broadcasted_iota(jnp.int32, (tall, group), 1) - place * own
     results = []
     for step in range(steps):
         block = slice(step * group, (step + 1) * group)
-        weights = jnp.pad(block_weights[step].T, ((0, high - classes), (0, 0)))
+        weights = jnp.pad(block_weights[step].T, ((0, tall - classes), (0, 0)))
+        current_low = jnp.pad(current_low, ((0, tall - high), (0, 0)))
         gradient = product(current_low, kernel[block], ((1,), (1,)))
         for i in range(own):
             gradient = jnp.where(lanes == i, gradient - RIDGE * weights[:, i : i + 1], gradient)
-        gradient = jnp.pad(gradient.astype(low), ((0, nz * share - high), (0, 0)))
+        gradient = gradient.astype(low)
         part = total(swap(gradient.reshape(nz, share, group), "z"))
         part = total(spread(part.astype(low), "y"))
         part = part.astype(low)
+        places = step_places(step, steps, plane, own)
         if step == 0:
+            part = side_by_side(spread(part, CELL))
+            part = product(part, inverse, ((1,), (1,))).astype(low)
+            part = product(part, places, ((1,), (1,))).astype(low)
+        else:
             part, inverse = lax.optimization_barrier((part, inverse))
-            inverse = in_step_order(inverse, steps, plane, own)
-        part = side_by_side(spread(part, CELL))
-        part = product(part, inverse[block], ((1,), (1,))).astype(low)
-        change = spread(part, "z").reshape(nz * share, group)[:high]
+            inverse_step = product(places, inverse, ((1,), (0,))).astype(low)
+            part = side_by_side(spread(part, CELL))
+            part = product(part, inverse_step, ((1,), (1,))).astype(low)
+        change = spread(part, "z").reshape(tall, group)[:high]
         update = product(change, kernel[block], ((1,), (0,))).astype(low)
         update = update.reshape(high, cell, own_rows).transpose(1, 0, 2)
         current = current - total(swap(update, CELL))
         if step < steps - 1:
             current_low = side_by_side(spread(current.astype(low), CELL))
         change_own = jnp.stack(
-            [jnp.sum(jnp.where(lanes == i, change, 0.0), axis=1)[:classes] for i in range(own)]
+            [jnp.sum(jnp.where(lanes[:high] == i, change, 0.0), axis=1)[:classes] for i in range(own)]
         )
         results.append(block_weights[step] + change_own)
     return current[:classes].T, jnp.stack(results)

time: 222 us -> 218 us (0.982)
  waiting for transfers between devices: 48.8 us -> 40.6 us
  blocking collectives: 87.7 us -> 94.5 us
  starting transfers between devices: 51.4 us -> 48.5 us
  matrix products: 8.91 us -> 6.5 us
    all_to_all x7 -> x8, blocking collectives: 77 us -> 83.6 us  [swap(): return lax.all_to_all(pieces, axis, 0, 0, tiled=True)]
    all_gather x1, waiting for transfers between devices: 4.35 us -> 0.02 us  [on_device(): inverse = lax.all_gather(inverse, PLANE, axis=0, tiled=True)]
    all_to_all x6 -> x5, waiting for transfers between devices: 43.9 us -> 40.5 us  [swap(): return lax.all_to_all(pieces, axis, 0, 0, tiled=True)]
    all_to_all x6 -> x5, starting transfers between devices: 40.1 us -> 37.5 us  [swap(): return lax.all_to_all(pieces, axis, 0, 0, tiled=True)]
    dot_general x10 -> x8, matrix products: 8.91 us -> 6.5 us  [product(): lax.dot_general(left, right, (dims, ((), ())), preferred_element_type=jnp...]
  transfers between devices with their start and end apart: 9 -> 8, of which waited for: 8 -> 5; matrix products, arithmetic and copies ran while one was open for 5% -> 5% of each run, Pallas kernels for 0% -> 1%
where the time goes in v5:
time: 218 us; the launch traced here: 217 us
  blocking collectives  94.5 us (43%)
  starting transfers between devices  48.5 us (22%)
  waiting for transfers between devices  40.6 us (19%)
  between operations  14.5 us (7%)
  local copies, waits for them, and re-layouts  6.67 us (3%)
  matrix products  6.5 us (3%)
  other arithmetic  3.77 us (2%)
    all_to_all x8, blocking collectives, swap(): return lax.all_to_all(pieces, axis, 0, 0, tiled=True)  83.6 us
    all_to_all x5, waiting for transfers between devices, swap(): return lax.all_to_all(pieces, axis, 0, 0, tiled=True)  40.5 us
    all_to_all x5, starting transfers between devices, swap(): return lax.all_to_all(pieces, axis, 0, 0, tiled=True)  37.5 us
    ppermute x2, starting transfers between devices, both(): other = lax.ppermute(piece, 'c', [(0, 1), (1, 0)])  11 us
    all_gather x1, blocking collectives, on_device(): pair = lax.all_gather(pair, 'x')  10.8 us
    dot_general x8, matrix products, product(): lax.dot_general(left, right, (dims, ((), ())), preferred_element_type=jnp...  6.5 us
  transfers between devices with their start and end apart: 8, of which 5 were waited for; matrix products, arithmetic and copies ran while one was open for 5% of the time, Pallas kernels for 1%

profile of v5, /device:TPU:1, one launch (start us, length us, event | category | flops | bytes accessed | tf_op | source)
XLA Modules:
  0.0 216.7 jit_solution(6308531576974571507)
XLA Ops:
  7.2 8.8 %collective-permute-start.1 = (bf16[512,440]{0,1:T(8,128)(2,1)}, bf16[512,440]{0,1:T(8,128)(2,1)S(1)}, u32[]{:S(2)}, u32[]{:S(2)}) collective-permute-start(bf16[512,440]{0,1:T(8,128)(2,1)} %param.5), channel_id=1, source_target_pairs={{0,4},{4,0},{1,5},{5,1},{2,6},{6,2},{3,7},{7,3},{8,12},{12,8},{9,1... | collective-permute-start | bytes 1351688 | tf_op jit(solution)/shard_map/ppermute | solution.py:26
  16.0 1.7 arrange.1
  17.8 1.2 reshape.192
  19.4 1.1 select_bitcast_fusion.1
  20.7 0.8 fusion.2
  21.5 1.0 copy.26
  22.5 10.9 %all-to-all-start = ((bf16[64,8,440]{2,1,0:T(8,128)(2,1)}), bf16[64,8,440]{2,1,0:T(8,128)(2,1)S(1)}, u32[]{:S(2)}, u32[]{:S(2)}) async-start(bf16[64,8,440]{2,1,0:T(8,128)(2,1)} %bitcast.9), calls=%async_computation | async-start | bytes 1048576 | tf_op jit(solution)/shard_map/all_to_all | solution.py:18
  33.5 2.2 %collective-permute-start = (bf16[152,128]{1,0:T(8,128)(2,1)S(1)}, bf16[152,128]{1,0:T(8,128)(2,1)S(1)}, u32[]{:S(2)}, u32[]{:S(2)}) collective-permute-start(bf16[152,128]{1,0:T(8,128)(2,1)S(1)} %pad_convert_fusion), channel_id=1, source_target_pairs={{0,4},{4,0},{1,5},{5,1},{2,6},{6,2},{3,7},{7,3},{8,12},{12,8},{9,1... | collective-permute-start | bytes 116744 | tf_op jit(solution)/shard_map/ppermute | solution.py:26
  35.7 16.0 %all-to-all-done = bf16[64,8,440]{2,1,0:T(8,128)(2,1)S(1)} async-done(((bf16[64,8,440]{2,1,0:T(8,128)(2,1)}), bf16[64,8,440]{2,1,0:T(8,128)(2,1)S(1)}, u32[]{:S(2)}, u32[]{:S(2)}) %all-to-all-start) | async-done | bytes 450592 | tf_op jit(solution)/shard_map/all_to_all | solution.py:18
  51.8 0.8 broadcast_in_dim.27
  52.7 6.6 %all-to-all-start.1 = ((bf16[64,8,440]{2,1,0:T(8,128)(2,1)}), bf16[64,8,440]{2,1,0:T(8,128)(2,1)S(1)}, u32[]{:S(2)}, u32[]{:S(2)}) async-start(bf16[64,8,440]{2,1,0:T(8,128)(2,1)} %broadcast_in_dim.27), calls=%async_computation.1 | async-start | bytes 1048576 | tf_op jit(solution)/shard_map/all_to_all | solution.py:18
  59.4 10.8 %all-gather = bf16[8,152,128]{2,1,0:T(8,128)(2,1)S(1)} all-gather(bf16[2,152,128]{2,1,0:T(8,128)(2,1)S(1)} %pad_maximum_fusion.1), channel_id=2, replica_groups=mesh['z'=8,'y'=8,'c'=2,'x'=4] {'x'}, dimensions={0}, use_global_device_ids=true | all-gather | bytes 389120 | tf_op jit(solution)/shard_map/all_gather | solution.py:108
  70.2 0.8 copy.44
  71.2 4.7 %all-to-all-done.1 = bf16[64,8,440]{2,1,0:T(8,128)(2,1)S(1)} async-done(((bf16[64,8,440]{2,1,0:T(8,128)(2,1)}), bf16[64,8,440]{2,1,0:T(8,128)(2,1)S(1)}, u32[]{:S(2)}, u32[]{:S(2)}) %all-to-all-start.1) | async-done | bytes 450592 | tf_op jit(solution)/shard_map/all_to_all | solution.py:18
  76.2 0.9 exponential_convert_fusion
  77.5 11.5 %all_to_all.65 = bf16[8,24,256]{2,1,0:T(8,128)(2,1)S(1)} all-to-all(bf16[8,24,256]{2,1,0:T(8,128)(2,1)S(1)} %bitcast.110), channel_id=1, replica_groups=mesh['z'=8,'y'=8,'c'=2,'x'=4] {'z'}, dimensions={0} | all-to-all | bytes 196608 | tf_op jit(solution)/shard_map/all_to_all | solution.py:18
  89.6 4.1 %all-to-all-start.3 = ((bf16[8,24,256]{2,1,0:T(8,128)(2,1)}), bf16[8,24,256]{2,1,0:T(8,128)(2,1)S(1)}, u32[]{:S(2)}, u32[]{:S(2)}) async-start(bf16[8,24,256]{2,1,0:T(8,128)(2,1)} %broadcast_in_dim.28), calls=%async_computation.3 | async-start | bytes 196608 | tf_op jit(solution)/shard_map/all_to_all | solution.py:18
  93.8 8.4 %all-to-all-done.3 = bf16[8,24,256]{2,1,0:T(8,128)(2,1)S(1)} async-done(((bf16[8,24,256]{2,1,0:T(8,128)(2,1)}), bf16[8,24,256]{2,1,0:T(8,128)(2,1)S(1)}, u32[]{:S(2)}, u32[]{:S(2)}) %all-to-all-start.3) | async-done | bytes 98336 | tf_op jit(solution)/shard_map/all_to_all | solution.py:18
  102.8 10.8 %all-to-all-start.4 = ((bf16[8,24,256]{2,1,0:T(8,128)(2,1)}), bf16[8,24,256]{2,1,0:T(8,128)(2,1)S(1)}, u32[]{:S(2)}, u32[]{:S(2)}) async-start(bf16[8,24,256]{2,1,0:T(8,128)(2,1)} %broadcast_in_dim.29), calls=%async_computation.4 | async-start | bytes 196608 | tf_op jit(solution)/shard_map/all_to_all | solution.py:18
  113.6 5.0 %all-to-all-done.4 = bf16[8,24,256]{2,1,0:T(8,128)(2,1)S(1)} async-done(((bf16[8,24,256]{2,1,0:T(8,128)(2,1)}), bf16[8,24,256]{2,1,0:T(8,128)(2,1)S(1)}, u32[]{:S(2)}, u32[]{:S(2)}) %all-to-all-start.4) | async-done | bytes 98336 | tf_op jit(solution)/shard_map/all_to_all | solution.py:18
  118.7 2.4 %fusion.6 = bf16[24,256]{1,0:T(8,128)(2,1)S(1)} fusion(bf16[24,2048]{1,0:T(8,128)(2,1)S(1)} %bitcast.108, bf16[512,2048]{1,0:T(8,128)(2,1)} %all-gather.3.cloned.1.call-done, s32[256]{0:T(256)S(1)} %get-tuple-element.45, s32[256]{0:T(256)S(1)} %get-tuple-element.48, s32[256]{0:T(256)S(1)} %get-tuple-element.44, s32[256]{0:T(256)S(1)} %get-tuple-element.49, ...), kind=kOutput, calls=%fused_computation.13 | convolution fusion | flops 57296896 | bytes 2212352 | tf_op jit(solution)/shard_map/dot_general | solution.py:40
  121.1 9.9 %all_to_all.66 = bf16[8,24,256]{2,1,0:T(8,128)(2,1)S(1)} all-to-all(bf16[8,24,256]{2,1,0:T(8,128)(2,1)S(1)} %broadcast_in_dim.30), channel_id=1, replica_groups=mesh['z'=8,'y'=8,'c'=2,'x'=4] {'z'}, dimensions={0} | all-to-all | bytes 196608 | tf_op jit(solution)/shard_map/all_to_all | solution.py:18
  131.4 11.7 %all_to_all.67 = bf16[8,152,128]{2,1,0:T(8,128)(2,1)S(1)} all-to-all(bf16[8,152,128]{2,1,0:T(8,128)(2,1)S(1)} %bitcast.95), channel_id=1, replica_groups=mesh['z'=8,'y'=8,'c'=2,'x'=4] {'c','x'}, dimensions={0} | all-to-all | bytes 622592 | tf_op jit(solution)/shard_map/all_to_all | solution.py:18
  143.2 10.4 %all_to_all.68 = bf16[8,152,128]{2,1,0:T(8,128)(2,1)S(1)} all-to-all(bf16[8,152,128]{2,1,0:T(8,128)(2,1)S(1)} %broadcast_in_dim.31), channel_id=1, replica_groups=mesh['z'=8,'y'=8,'c'=2,'x'=4] {'c','x'}, dimensions={0} | all-to-all | bytes 622592 | tf_op jit(solution)/shard_map/all_to_all | solution.py:18
  154.1 9.9 %all_to_all.69 = bf16[8,24,256]{2,1,0:T(8,128)(2,1)S(1)} all-to-all(bf16[8,24,256]{2,1,0:T(8,128)(2,1)S(1)} %bitcast.111), channel_id=1, replica_groups=mesh['z'=8,'y'=8,'c'=2,'x'=4] {'z'}, dimensions={0} | all-to-all | bytes 196608 | tf_op jit(solution)/shard_map/all_to_all | solution.py:18
  164.0 10.0 %all_to_all.70 = bf16[8,24,256]{2,1,0:T(8,128)(2,1)S(1)} all-to-all(bf16[8,24,256]{2,1,0:T(8,128)(2,1)S(1)} %broadcast_in_dim.32), channel_id=1, replica_groups=mesh['z'=8,'y'=8,'c'=2,'x'=4] {'y'}, dimensions={0} | all-to-all | bytes 196608 | tf_op jit(solution)/shard_map/all_to_all | solution.py:18
  174.1 10.3 %all_to_all.71 = bf16[8,24,256]{2,1,0:T(8,128)(2,1)S(1)} all-to-all(bf16[8,24,256]{2,1,0:T(8,128)(2,1)S(1)} %broadcast_in_dim.33), channel_id=1, replica_groups=mesh['z'=8,'y'=8,'c'=2,'x'=4] {'c','x'}, dimensions={0} | all-to-all | bytes 196608 | tf_op jit(solution)/shard_map/all_to_all | solution.py:18
  184.4 1.2 fusion.7
  185.6 9.9 %all_to_all.72 = bf16[8,24,256]{2,1,0:T(8,128)(2,1)S(1)} all-to-all(bf16[8,24,256]{2,1,0:T(8,128)(2,1)S(1)} %broadcast_in_dim.34), channel_id=1, replica_groups=mesh['z'=8,'y'=8,'c'=2,'x'=4] {'z'}, dimensions={0} | all-to-all | bytes 196608 | tf_op jit(solution)/shard_map/all_to_all | solution.py:18
  196.2 0.8 copy.45
  197.0 5.1 %all-to-all-start.12 = ((bf16[8,152,128]{2,1,0:T(8,128)(2,1)}), bf16[8,152,128]{2,1,0:T(8,128)(2,1)S(1)}, u32[]{:S(2)}, u32[]{:S(2)}) async-start(bf16[8,152,128]{2,1,0:T(8,128)(2,1)} %bitcast.82), calls=%async_computation.12 | async-start | bytes 622592 | tf_op jit(solution)/shard_map/all_to_all | solution.py:18
  202.7 6.5 %all-to-all-done.12 = bf16[8,152,128]{2,1,0:T(8,128)(2,1)S(1)} async-done(((bf16[8,152,128]{2,1,0:T(8,128)(2,1)}), bf16[8,152,128]{2,1,0:T(8,128)(2,1)S(1)}, u32[]{:S(2)}, u32[]{:S(2)}) %all-to-all-start.12) | async-done | bytes 311328 | tf_op jit(solution)/shard_map/all_to_all | solution.py:18
  (75 shorter events, 6.0 us)
Async XLA Ops:
  7.2 111.5 %all-gather.3.cloned.1.call-start = ((), (), s32[]{:S(2)}) async-start(), calls=%async_computation.13 | async-start | bytes 2129920 | tf_op jit(solution)/shard_map/all_gather | solution.py:104
  7.2 12.2 %collective-permute-start.1 = (bf16[512,440]{0,1:T(8,128)(2,1)}, bf16[512,440]{0,1:T(8,128)(2,1)S(1)}, u32[]{:S(2)}, u32[]{:S(2)}) collective-permute-start(bf16[512,440]{0,1:T(8,128)(2,1)} %param.5), channel_id=1, source_target_pairs={{0,4},{4,0},{1,5},{5,1},{2,6},{6,2},{3,7},{7,3},{8,12},{12,8},{9,1... | collective-permute-start | bytes 1351688 | tf_op jit(solution)/shard_map/ppermute | solution.py:26
  20.7 12.8 %copy-start = (f32[128,147]{0,1:T(8,128)S(1)}, f32[128,147]{0,1:T(8,128)}, u32[]{:S(2)}) copy-start(f32[128,147]{0,1:T(8,128)} %param.6) | copy-start | bytes 225796
  21.5 37.8 %copy-start.2 = (f32[2,4,147]{2,1,0:T(4,128)S(1)}, f32[2,4,147]{2,1,0:T(4,128)}, u32[]{:S(2)}) copy-start(f32[2,4,147]{2,1,0:T(4,128)} %param.7) | copy-start | bytes 14116
  22.5 29.2 %all-to-all-start = ((bf16[64,8,440]{2,1,0:T(8,128)(2,1)}), bf16[64,8,440]{2,1,0:T(8,128)(2,1)S(1)}, u32[]{:S(2)}, u32[]{:S(2)}) async-start(bf16[64,8,440]{2,1,0:T(8,128)(2,1)} %bitcast.9), calls=%async_computation | async-start | bytes 1048576 | tf_op jit(solution)/shard_map/all_to_all | solution.py:18
  33.5 25.9 %collective-permute-start = (bf16[152,128]{1,0:T(8,128)(2,1)S(1)}, bf16[152,128]{1,0:T(8,128)(2,1)S(1)}, u32[]{:S(2)}, u32[]{:S(2)}) collective-permute-start(bf16[152,128]{1,0:T(8,128)(2,1)S(1)} %pad_convert_fusion), channel_id=1, source_target_pairs={{0,4},{4,0},{1,5},{5,1},{2,6},{6,2},{3,7},{7,3},{8,12},{12,8},{9,1... | collective-permute-start | bytes 116744 | tf_op jit(solution)/shard_map/ppermute | solution.py:26
  52.7 23.2 %all-to-all-start.1 = ((bf16[64,8,440]{2,1,0:T(8,128)(2,1)}), bf16[64,8,440]{2,1,0:T(8,128)(2,1)S(1)}, u32[]{:S(2)}, u32[]{:S(2)}) async-start(bf16[64,8,440]{2,1,0:T(8,128)(2,1)} %broadcast_in_dim.27), calls=%async_computation.1 | async-start | bytes 1048576 | tf_op jit(solution)/shard_map/all_to_all | solution.py:18
  76.2 1.0 copy-start.1
  89.6 12.5 %all-to-all-start.3 = ((bf16[8,24,256]{2,1,0:T(8,128)(2,1)}), bf16[8,24,256]{2,1,0:T(8,128)(2,1)S(1)}, u32[]{:S(2)}, u32[]{:S(2)}) async-start(bf16[8,24,256]{2,1,0:T(8,128)(2,1)} %broadcast_in_dim.28), calls=%async_computation.3 | async-start | bytes 196608 | tf_op jit(solution)/shard_map/all_to_all | solution.py:18
  102.8 15.8 %all-to-all-start.4 = ((bf16[8,24,256]{2,1,0:T(8,128)(2,1)}), bf16[8,24,256]{2,1,0:T(8,128)(2,1)S(1)}, u32[]{:S(2)}, u32[]{:S(2)}) async-start(bf16[8,24,256]{2,1,0:T(8,128)(2,1)} %broadcast_in_dim.29), calls=%async_computation.4 | async-start | bytes 196608 | tf_op jit(solution)/shard_map/all_to_all | solution.py:18
  113.6 17.8 %copy-start.4 = (pred[256]{0:T(512)(128)(4,1)}, pred[256]{0:T(512)(128)(4,1)S(1)}, u32[]{:S(2)}) copy-start(pred[256]{0:T(512)(128)(4,1)S(1)} %get-tuple-element.46) | copy-start | bytes 772
  113.6 17.8 %copy-start.6 = (pred[256]{0:T(512)(128)(4,1)}, pred[256]{0:T(512)(128)(4,1)S(1)}, u32[]{:S(2)}) copy-start(pred[256]{0:T(512)(128)(4,1)S(1)} %get-tuple-element.47) | copy-start | bytes 772
  143.2 41.1 %copy-start.3 = (bf16[512,2048]{1,0:T(8,128)(2,1)S(1)}, bf16[512,2048]{1,0:T(8,128)(2,1)}, u32[]{:S(2)}) copy-start(bf16[512,2048]{1,0:T(8,128)(2,1)} %all-gather.3.cloned.1.call-done) | copy-start | bytes 6291460
  143.2 41.1 %copy-start.5 = (pred[256]{0:T(512)(128)(4,1)S(1)}, pred[256]{0:T(512)(128)(4,1)}, u32[]{:S(2)}) copy-start(pred[256]{0:T(512)(128)(4,1)} %copy-done.4) | copy-start | bytes 772
  143.2 41.1 %copy-start.7 = (pred[256]{0:T(512)(128)(4,1)S(1)}, pred[256]{0:T(512)(128)(4,1)}, u32[]{:S(2)}) copy-start(pred[256]{0:T(512)(128)(4,1)} %copy-done.6) | copy-start | bytes 772
  197.0 12.2 %all-to-all-start.12 = ((bf16[8,152,128]{2,1,0:T(8,128)(2,1)}), bf16[8,152,128]{2,1,0:T(8,128)(2,1)S(1)}, u32[]{:S(2)}, u32[]{:S(2)}) async-start(bf16[8,152,128]{2,1,0:T(8,128)(2,1)} %bitcast.82), calls=%async_computation.12 | async-start | bytes 622592 | tf_op jit(solution)/shard_map/all_to_all | solution.py:18
Sparse Core Ops, SparseCore 0:
  17.9 88.7 all-gather.2

commit v6 on v5

--- a/solution.py
+++ b/solution.py
@@ -22,8 +22,7 @@
     return swap(jnp.broadcast_to(piece[None], (lax.axis_size(axis), *piece.shape)), axis)
 
 
-def both(piece, first):
-    other = lax.ppermute(piece, "c", [(0, 1), (1, 0)])
+def ordered(piece, other, first):
     return jnp.stack([jnp.where(first, piece, other), jnp.where(first, other, piece)])
 
 
@@ -42,40 +41,55 @@
     )
 
 
-def arranged(rows, plane, cell):
+def arranged(rows, numbers, plane, cell):
     steps, own, columns = rows.shape
-    count = steps * own
+    count, group = steps * own, plane * own
     if columns % 2048 or count != 8 or cell * own != 32:
         rows = rows.astype(jnp.bfloat16).reshape(count, plane, cell, own)
-        return rows.transpose(0, 2, 1, 3).reshape(count, columns)
+        numbers = numbers.reshape(steps, plane, cell, own).transpose(2, 0, 1, 3)
+        return (
+            rows.transpose(0, 2, 1, 3).reshape(count, columns),
+            numbers.reshape(cell, steps, group),
+        )
     blocks = columns // 128
     run = 128 // cell
 
-    def kernel(rows_ref, out_ref):
-        tall = jnp.concatenate([rows_ref[step] for step in range(steps)], axis=0)
+    def kernel(rows_ref, numbers_ref, rows_out, numbers_out):
+        number = numbers_ref[...]
+        tall = [rows_ref[step] for step in range(steps)]
+        tall += [(number >> 8).astype(jnp.float32), (number & 255).astype(jnp.float32)]
+        tall += [jnp.zeros((16 - count - 2 * steps, columns), jnp.float32)]
+        tall = jnp.concatenate(tall, axis=0)
         tall = jnp.concatenate([tall[:, 128 * q : 128 * (q + 1)] for q in range(blocks)], axis=0)
         source = lax.broadcasted_iota(jnp.int32, (128, 128), 0)
         target = lax.broadcasted_iota(jnp.int32, (128, 128), 1)
         member, lane = (source >> 2) & 7, ((source >> 5) << 2) | (source & 3)
         order = jnp.where(member * run + lane == target, 1.0, 0.0).astype(jnp.bfloat16)
         tall = jnp.dot(tall.astype(jnp.bfloat16), order, preferred_element_type=jnp.float32)
-        part = lax.broadcasted_iota(jnp.int32, (count, 128), 1) >> 4
+        part = lax.broadcasted_iota(jnp.int32, (16, 128), 1) >> 4
+        wide = blocks // cell
         for out in range(blocks):
-            member, first = out * cell // blocks, out % (blocks // cell) * cell
-            joined = jnp.zeros((count, 128), jnp.float32)
+            member, first = out // wide, out % wide * cell
+            joined = jnp.zeros((16, 128), jnp.float32)
             for k in range(cell):
                 q = first + k
-                piece = tall[count * q : count * (q + 1)]
+                piece = tall[16 * q : 16 * (q + 1)]
                 if k != member:
                     piece = pltpu.roll(piece, (k - member) * run % 128, 1)
                 joined = jnp.where(part == k, piece, joined)
-            out_ref[:, 128 * out : 128 * (out + 1)] = joined.astype(out_ref.dtype)
+            rows_out[:, 128 * out : 128 * (out + 1)] = joined[:count].astype(rows_out.dtype)
+            number = joined[count : count + steps] * 256.0 + joined[count + steps : count + 2 * steps]
+            at = out % wide * 128
+            numbers_out[member, :, at : at + 128] = number.astype(jnp.int32)
 
     return pl.pallas_call(
         kernel,
-        out_shape=jax.ShapeDtypeStruct((count, columns), jnp.bfloat16),
+        out_shape=(
+            jax.ShapeDtypeStruct((count, columns), jnp.bfloat16),
+            jax.ShapeDtypeStruct((cell, steps, group), jnp.int32),
+        ),
         name="arrange",
-    )(rows)
+    )(rows, numbers)
 
 
 def step_places(step, steps, plane, own):
@@ -100,23 +114,26 @@
     gamma_rate = 4.0 / width
     low = jnp.bfloat16
 
-    inverse = arranged(block_inverse.transpose(0, 2, 1), plane, cell)
+    inverse, chosen = arranged(block_inverse.transpose(0, 2, 1), block_columns, plane, cell)
     inverse = lax.all_gather(inverse, PLANE, axis=0, tiled=True)
     current = jnp.pad(residual.T, ((0, high - classes), (0, 0)))
     first = lax.axis_index("c") == 0
-    pair = both(current.astype(low), first)
+
+    chosen = lax.dynamic_index_in_dim(chosen, member, 0, keepdims=False).reshape(steps * group)
+
+    other = lax.ppermute(features, "c", [(0, 1), (1, 0)])
+    frames = ordered(features, other, first).reshape(nc * features.shape[0], width)
+    spots = lax.broadcasted_iota(jnp.int32, (steps * group, frames.shape[0]), 1)
+    picks = ((chosen - place * frames.shape[0])[:, None] == spots).astype(low)
+    part = product(picks, frames, ((1,), (0,))).astype(low)
+    part, pair = lax.optimization_barrier((part, residual))
+    pair = jnp.pad(pair.T, ((0, high - classes), (0, 0))).astype(low)
+    pair = ordered(pair, lax.ppermute(pair, "c", [(0, 1), (1, 0)]), first)
+    part = total(swap(part.reshape(plane, -1, width), PLANE)).astype(low)
+    places = step_places(0, steps, plane, own)
+    part, pair, places = lax.optimization_barrier((part, pair, places))
     pair = lax.all_gather(pair, "x")
     current_low = side_by_side(pair.swapaxes(0, 1).reshape(cell, high, own_rows))
-
-    frames = both(features, first).reshape(nc * features.shape[0], width)
-    rows = frames.shape[0]
-    chosen = lax.dynamic_index_in_dim(
-        block_columns.reshape(steps, plane, cell, own), member, 2, keepdims=False
-    ).reshape(steps * group)
-    spots = lax.broadcasted_iota(jnp.int32, (steps * group, rows), 1)
-    picks = ((chosen - place * rows)[:, None] == spots).astype(low)
-    part = product(picks, frames, ((1,), (0,))).astype(low)
-    part = total(swap(part.reshape(plane, -1, width), PLANE)).astype(low)
     centers = spread(part, PLANE).reshape(steps * group, width)
 
     frame_f = frames.astype(jnp.float32)
@@ -141,16 +158,11 @@
         part = total(swap(gradient.reshape(nz, share, group), "z"))
         part = total(spread(part.astype(low), "y"))
         part = part.astype(low)
-        places = step_places(step, steps, plane, own)
-        if step == 0:
-            part = side_by_side(spread(part, CELL))
-            part = product(part, inverse, ((1,), (1,))).astype(low)
-            part = product(part, places, ((1,), (1,))).astype(low)
-        else:
-            part, inverse = lax.optimization_barrier((part, inverse))
-            inverse_step = product(places, inverse, ((1,), (0,))).astype(low)
-            part = side_by_side(spread(part, CELL))
-            part = product(part, inverse_step, ((1,), (1,))).astype(low)
+        if step > 0:
+            places = step_places(step, steps, plane, own)
+        part = side_by_side(spread(part, CELL))
+        part = product(part, inverse, ((1,), (1,))).astype(low)
+        part = product(part, places, ((1,), (1,))).astype(low)
         change = spread(part, "z").reshape(tall, group)[:high]
         update = product(change, kernel[block], ((1,), (0,))).astype(low)
         update = update.reshape(high, cell, own_rows).transpose(1, 0, 2)

time: 218 us -> 215 us (0.986)
  blocking collectives: 94.5 us -> 122 us
  starting transfers between devices: 48.5 us -> 34.3 us
  waiting for transfers between devices: 40.6 us -> 27.7 us
  local copies, waits for them, and re-layouts: 6.67 us -> 3.23 us
    all_to_all x8 -> x10, blocking collectives: 83.6 us -> 111 us  [swap(): return lax.all_to_all(pieces, axis, 0, 0, tiled=True)]
    all_to_all x5 -> x3, starting transfers between devices: 37.5 us -> 22.9 us  [swap(): return lax.all_to_all(pieces, axis, 0, 0, tiled=True)]
    all_to_all x5 -> x3, waiting for transfers between devices: 40.5 us -> 26.2 us  [swap(): return lax.all_to_all(pieces, axis, 0, 0, tiled=True)]
  transfers between devices with their start and end apart: 8 -> 6, of which waited for: 5 -> 5; matrix products, arithmetic and copies ran while one was open for 5% -> 4% of each run, Pallas kernels for 1% -> 0%
where the time goes in v6:
time: 215 us; the launch traced here: 214 us
  blocking collectives  122 us (57%)
  starting transfers between devices  34.3 us (16%)
  waiting for transfers between devices  27.7 us (13%)
  between operations  14.4 us (7%)
  matrix products  6.13 us (3%)
  other arithmetic  4.51 us (2%)
  local copies, waits for them, and re-layouts  3.23 us (2%)
    all_to_all x10, blocking collectives, swap(): return lax.all_to_all(pieces, axis, 0, 0, tiled=True)  111 us
    all_to_all x3, waiting for transfers between devices, swap(): return lax.all_to_all(pieces, axis, 0, 0, tiled=True)  26.2 us
    all_to_all x3, starting transfers between devices, swap(): return lax.all_to_all(pieces, axis, 0, 0, tiled=True)  22.9 us
    all_gather x1, blocking collectives, on_device(): pair = lax.all_gather(pair, 'x')  10.8 us
    ppermute x1, starting transfers between devices, on_device(): other = lax.ppermute(features, 'c', [(0, 1), (1, 0)])  8.79 us
    dot_general x8, matrix products, product(): lax.dot_general(left, right, (dims, ((), ())), preferred_element_type=jnp...  6.13 us
  transfers between devices with their start and end apart: 6, of which 5 were waited for; matrix products, arithmetic and copies ran while one was open for 4% of the time, Pallas kernels for 0%

profile of v6, /device:TPU:1, one launch (start us, length us, event | category | flops | bytes accessed | tf_op | source)
XLA Modules:
  0.0 213.7 jit_solution(15753050521826161901)
XLA Ops:
  7.2 1.9 arrange.1
  9.1 8.8 %collective-permute-start = (bf16[512,440]{0,1:T(8,128)(2,1)}, bf16[512,440]{0,1:T(8,128)(2,1)S(1)}, u32[]{:S(2)}, u32[]{:S(2)}) collective-permute-start(bf16[512,440]{0,1:T(8,128)(2,1)} %param.5), channel_id=1, source_target_pairs={{0,4},{4,0},{1,5},{5,1},{2,6},{6,2},{3,7},{7,3},{8,12},{12,8},{9,1... | collective-permute-start | bytes 1351688 | tf_op jit(solution)/shard_map/ppermute | solution.py:124
  17.9 0.7 subtract_bitcast_fusion
  18.6 0.9 collective-permute-done
  19.5 1.1 select_bitcast_fusion.1
  20.8 0.8 fusion.1
  21.6 1.0 copy.24
  22.6 11.1 %all-to-all-start = ((bf16[64,8,440]{2,1,0:T(8,128)(2,1)}), bf16[64,8,440]{2,1,0:T(8,128)(2,1)S(1)}, u32[]{:S(2)}, u32[]{:S(2)}) async-start(bf16[64,8,440]{2,1,0:T(8,128)(2,1)} %bitcast.4), calls=%async_computation | async-start | bytes 1048576 | tf_op jit(solution)/shard_map/all_to_all | solution.py:18
  33.8 2.6 %collective-permute-start.1 = (bf16[152,128]{1,0:T(8,128)(2,1)S(1)}, bf16[152,128]{1,0:T(8,128)(2,1)S(1)}, u32[]{:S(2)}, u32[]{:S(2)}) collective-permute-start(bf16[152,128]{1,0:T(8,128)(2,1)S(1)} %pad.23), channel_id=1, source_target_pairs={{0,4},{4,0},{1,5},{5,1},{2,6},{6,2},{3,7},{7,3},{8,12},{12,8},{9,1... | collective-permute-start | bytes 116744 | tf_op jit(solution)/shard_map/ppermute | solution.py:131
  37.2 14.5 %all-to-all-done = bf16[64,8,440]{2,1,0:T(8,128)(2,1)S(1)} async-done(((bf16[64,8,440]{2,1,0:T(8,128)(2,1)}), bf16[64,8,440]{2,1,0:T(8,128)(2,1)S(1)}, u32[]{:S(2)}, u32[]{:S(2)}) %all-to-all-start) | async-done | bytes 450592 | tf_op jit(solution)/shard_map/all_to_all | solution.py:18
  51.9 0.8 broadcast_in_dim.27
  52.7 6.7 %all-to-all-start.1 = ((bf16[64,8,440]{2,1,0:T(8,128)(2,1)}), bf16[64,8,440]{2,1,0:T(8,128)(2,1)S(1)}, u32[]{:S(2)}, u32[]{:S(2)}) async-start(bf16[64,8,440]{2,1,0:T(8,128)(2,1)} %broadcast_in_dim.27), calls=%async_computation.1 | async-start | bytes 1048576 | tf_op jit(solution)/shard_map/all_to_all | solution.py:18
  59.7 10.8 %all-gather = bf16[8,152,128]{2,1,0:T(8,128)(2,1)S(1)} all-gather(bf16[2,152,128]{2,1,0:T(8,128)(2,1)S(1)} %pad_maximum_fusion.1), channel_id=2, replica_groups=mesh['z'=8,'y'=8,'c'=2,'x'=4] {'x'}, dimensions={0}, use_global_device_ids=true | all-gather | bytes 389120 | tf_op jit(solution)/shard_map/all_gather | solution.py:135
  70.6 5.2 %all-to-all-done.1 = bf16[64,8,440]{2,1,0:T(8,128)(2,1)S(1)} async-done(((bf16[64,8,440]{2,1,0:T(8,128)(2,1)}), bf16[64,8,440]{2,1,0:T(8,128)(2,1)S(1)}, u32[]{:S(2)}, u32[]{:S(2)}) %all-to-all-start.1) | async-done | bytes 450592 | tf_op jit(solution)/shard_map/all_to_all | solution.py:18
  76.1 0.9 exponential_convert_fusion
  77.4 11.8 %all_to_all.65 = bf16[8,24,256]{2,1,0:T(8,128)(2,1)S(1)} all-to-all(bf16[8,24,256]{2,1,0:T(8,128)(2,1)S(1)} %bitcast.114), channel_id=1, replica_groups=mesh['z'=8,'y'=8,'c'=2,'x'=4] {'z'}, dimensions={0} | all-to-all | bytes 196608 | tf_op jit(solution)/shard_map/all_to_all | solution.py:18
  89.2 11.5 %all_to_all.66 = bf16[8,24,256]{2,1,0:T(8,128)(2,1)S(1)} all-to-all(bf16[8,24,256]{2,1,0:T(8,128)(2,1)S(1)} %broadcast_in_dim.28), channel_id=1, replica_groups=mesh['z'=8,'y'=8,'c'=2,'x'=4] {'y'}, dimensions={0} | all-to-all | bytes 196608 | tf_op jit(solution)/shard_map/all_to_all | solution.py:18
  100.7 15.3 %all_to_all.67 = bf16[8,24,256]{2,1,0:T(8,128)(2,1)S(1)} all-to-all(bf16[8,24,256]{2,1,0:T(8,128)(2,1)S(1)} %broadcast_in_dim.29), channel_id=1, replica_groups=mesh['z'=8,'y'=8,'c'=2,'x'=4] {'c','x'}, dimensions={0} | all-to-all | bytes 196608 | tf_op jit(solution)/shard_map/all_to_all | solution.py:18
  116.1 2.4 %fusion.7 = bf16[24,256]{1,0:T(8,128)(2,1)S(1)} fusion(bf16[256,512]{1,0:T(8,128)(2,1)S(1)} %fusion.14, bf16[24,2048]{1,0:T(8,128)(2,1)S(1)} %bitcast.108, bf16[512,2048]{1,0:T(8,128)(2,1)} %all-gather.3.cloned.1.call-done), kind=kOutput, calls=%fused_computation.14 | convolution fusion | flops 56641536 | bytes 2469888 | tf_op jit(solution)/shard_map/dot_general | solution.py:39
  118.5 9.9 %all_to_all.68 = bf16[8,24,256]{2,1,0:T(8,128)(2,1)S(1)} all-to-all(bf16[8,24,256]{2,1,0:T(8,128)(2,1)S(1)} %broadcast_in_dim.30), channel_id=1, replica_groups=mesh['z'=8,'y'=8,'c'=2,'x'=4] {'z'}, dimensions={0} | all-to-all | bytes 196608 | tf_op jit(solution)/shard_map/all_to_all | solution.py:18
  128.8 11.7 %all_to_all.69 = bf16[8,152,128]{2,1,0:T(8,128)(2,1)S(1)} all-to-all(bf16[8,152,128]{2,1,0:T(8,128)(2,1)S(1)} %bitcast.101), channel_id=1, replica_groups=mesh['z'=8,'y'=8,'c'=2,'x'=4] {'c','x'}, dimensions={0} | all-to-all | bytes 622592 | tf_op jit(solution)/shard_map/all_to_all | solution.py:18
  140.6 10.4 %all_to_all.70 = bf16[8,152,128]{2,1,0:T(8,128)(2,1)S(1)} all-to-all(bf16[8,152,128]{2,1,0:T(8,128)(2,1)S(1)} %broadcast_in_dim.31), channel_id=1, replica_groups=mesh['z'=8,'y'=8,'c'=2,'x'=4] {'c','x'}, dimensions={0} | all-to-all | bytes 622592 | tf_op jit(solution)/shard_map/all_to_all | solution.py:18
  151.4 9.9 %all_to_all.71 = bf16[8,24,256]{2,1,0:T(8,128)(2,1)S(1)} all-to-all(bf16[8,24,256]{2,1,0:T(8,128)(2,1)S(1)} %bitcast.115), channel_id=1, replica_groups=mesh['z'=8,'y'=8,'c'=2,'x'=4] {'z'}, dimensions={0} | all-to-all | bytes 196608 | tf_op jit(solution)/shard_map/all_to_all | solution.py:18
  161.4 10.0 %all_to_all.72 = bf16[8,24,256]{2,1,0:T(8,128)(2,1)S(1)} all-to-all(bf16[8,24,256]{2,1,0:T(8,128)(2,1)S(1)} %broadcast_in_dim.32), channel_id=1, replica_groups=mesh['z'=8,'y'=8,'c'=2,'x'=4] {'y'}, dimensions={0} | all-to-all | bytes 196608 | tf_op jit(solution)/shard_map/all_to_all | solution.py:18
  171.4 10.3 %all_to_all.73 = bf16[8,24,256]{2,1,0:T(8,128)(2,1)S(1)} all-to-all(bf16[8,24,256]{2,1,0:T(8,128)(2,1)S(1)} %broadcast_in_dim.33), channel_id=1, replica_groups=mesh['z'=8,'y'=8,'c'=2,'x'=4] {'c','x'}, dimensions={0} | all-to-all | bytes 196608 | tf_op jit(solution)/shard_map/all_to_all | solution.py:18
  181.7 0.8 fusion.6
  182.6 9.9 %all_to_all.74 = bf16[8,24,256]{2,1,0:T(8,128)(2,1)S(1)} all-to-all(bf16[8,24,256]{2,1,0:T(8,128)(2,1)S(1)} %broadcast_in_dim.34), channel_id=1, replica_groups=mesh['z'=8,'y'=8,'c'=2,'x'=4] {'z'}, dimensions={0} | all-to-all | bytes 196608 | tf_op jit(solution)/shard_map/all_to_all | solution.py:18
  193.2 0.8 copy.46
  194.0 5.1 %all-to-all-start.12 = ((bf16[8,152,128]{2,1,0:T(8,128)(2,1)}), bf16[8,152,128]{2,1,0:T(8,128)(2,1)S(1)}, u32[]{:S(2)}, u32[]{:S(2)}) async-start(bf16[8,152,128]{2,1,0:T(8,128)(2,1)} %bitcast.88), calls=%async_computation.12 | async-start | bytes 622592 | tf_op jit(solution)/shard_map/all_to_all | solution.py:18
  199.1 0.6 pad_maximum_fusion.2
  199.7 6.5 %all-to-all-done.12 = bf16[8,152,128]{2,1,0:T(8,128)(2,1)S(1)} async-done(((bf16[8,152,128]{2,1,0:T(8,128)(2,1)}), bf16[8,152,128]{2,1,0:T(8,128)(2,1)S(1)}, u32[]{:S(2)}, u32[]{:S(2)}) %all-to-all-start.12) | async-done | bytes 311328 | tf_op jit(solution)/shard_map/all_to_all | solution.py:18
  206.3 0.6 fusion.73
  (64 shorter events, 4.0 us)
Async XLA Ops:
  7.2 108.9 %all-gather.3.cloned.1.call-start = ((), (), s32[]{:S(2)}) async-start(), calls=%async_computation.13 | async-start | bytes 2129920 | tf_op jit(solution)/shard_map/all_gather | solution.py:118
  9.1 10.4 %collective-permute-start = (bf16[512,440]{0,1:T(8,128)(2,1)}, bf16[512,440]{0,1:T(8,128)(2,1)S(1)}, u32[]{:S(2)}, u32[]{:S(2)}) collective-permute-start(bf16[512,440]{0,1:T(8,128)(2,1)} %param.5), channel_id=1, source_target_pairs={{0,4},{4,0},{1,5},{5,1},{2,6},{6,2},{3,7},{7,3},{8,12},{12,8},{9,1... | collective-permute-start | bytes 1351688 | tf_op jit(solution)/shard_map/ppermute | solution.py:124
  20.8 12.9 %copy-start.1 = (f32[128,147]{0,1:T(8,128)S(1)}, f32[128,147]{0,1:T(8,128)}, u32[]{:S(2)}) copy-start(f32[128,147]{0,1:T(8,128)} %param.6) | copy-start | bytes 225796
  22.6 36.9 %copy-start.2 = (f32[2,4,147]{2,1,0:T(4,128)S(1)}, f32[2,4,147]{2,1,0:T(4,128)}, u32[]{:S(2)}) copy-start(f32[2,4,147]{2,1,0:T(4,128)} %param.7) | copy-start | bytes 14116
  22.6 29.1 %all-to-all-start = ((bf16[64,8,440]{2,1,0:T(8,128)(2,1)}), bf16[64,8,440]{2,1,0:T(8,128)(2,1)S(1)}, u32[]{:S(2)}, u32[]{:S(2)}) async-start(bf16[64,8,440]{2,1,0:T(8,128)(2,1)} %bitcast.4), calls=%async_computation | async-start | bytes 1048576 | tf_op jit(solution)/shard_map/all_to_all | solution.py:18
  33.8 3.4 %collective-permute-start.1 = (bf16[152,128]{1,0:T(8,128)(2,1)S(1)}, bf16[152,128]{1,0:T(8,128)(2,1)S(1)}, u32[]{:S(2)}, u32[]{:S(2)}) collective-permute-start(bf16[152,128]{1,0:T(8,128)(2,1)S(1)} %pad.23), channel_id=1, source_target_pairs={{0,4},{4,0},{1,5},{5,1},{2,6},{6,2},{3,7},{7,3},{8,12},{12,8},{9,1... | collective-permute-start | bytes 116744 | tf_op jit(solution)/shard_map/ppermute | solution.py:131
  52.7 23.1 %all-to-all-start.1 = ((bf16[64,8,440]{2,1,0:T(8,128)(2,1)}), bf16[64,8,440]{2,1,0:T(8,128)(2,1)S(1)}, u32[]{:S(2)}, u32[]{:S(2)}) async-start(bf16[64,8,440]{2,1,0:T(8,128)(2,1)} %broadcast_in_dim.27), calls=%async_computation.1 | async-start | bytes 1048576 | tf_op jit(solution)/shard_map/all_to_all | solution.py:18
  140.6 41.1 %copy-start = (bf16[512,2048]{1,0:T(8,128)(2,1)S(1)}, bf16[512,2048]{1,0:T(8,128)(2,1)}, u32[]{:S(2)}) copy-start(bf16[512,2048]{1,0:T(8,128)(2,1)} %all-gather.3.cloned.1.call-done) | copy-start | bytes 6291460
  194.0 12.2 %all-to-all-start.12 = ((bf16[8,152,128]{2,1,0:T(8,128)(2,1)}), bf16[8,152,128]{2,1,0:T(8,128)(2,1)S(1)}, u32[]{:S(2)}, u32[]{:S(2)}) async-start(bf16[8,152,128]{2,1,0:T(8,128)(2,1)} %bitcast.88), calls=%async_computation.12 | async-start | bytes 622592 | tf_op jit(solution)/shard_map/all_to_all | solution.py:18
Sparse Core Ops, SparseCore 0:
  11.6 93.4 all-gather.2

commit v7 on v6

--- a/solution.py
+++ b/solution.py
@@ -121,11 +121,16 @@
 
     chosen = lax.dynamic_index_in_dim(chosen, member, 0, keepdims=False).reshape(steps * group)
 
+    def picked(block, holder):
+        spots = lax.broadcasted_iota(jnp.int32, (steps * group, block.shape[0]), 1)
+        picks = ((chosen - holder * block.shape[0])[:, None] == spots).astype(low)
+        return product(picks, block, ((1,), (0,)))
+
+    core = lax.axis_index("c")
     other = lax.ppermute(features, "c", [(0, 1), (1, 0)])
     frames = ordered(features, other, first).reshape(nc * features.shape[0], width)
-    spots = lax.broadcasted_iota(jnp.int32, (steps * group, frames.shape[0]), 1)
-    picks = ((chosen - place * frames.shape[0])[:, None] == spots).astype(low)
-    part = product(picks, frames, ((1,), (0,))).astype(low)
+    part = picked(features, place * nc + core) + picked(other, place * nc + 1 - core)
+    part = part.astype(low)
     part, pair = lax.optimization_barrier((part, residual))
     pair = jnp.pad(pair.T, ((0, high - classes), (0, 0))).astype(low)
     pair = ordered(pair, lax.ppermute(pair, "c", [(0, 1), (1, 0)]), first)

time: 215 us -> 216 us (level)
    dot_general x8 -> x9, matrix products: 6.13 us -> 7.51 us  [product(): lax.dot_general(left, right, (dims, ((), ())), preferred_element_type=jnp...]
  transfers between devices with their start and end apart: 6 -> 6, of which waited for: 5 -> 4; matrix products, arithmetic and copies ran while one was open for 4% -> 4% of each run, Pallas kernels for 0% -> 0%
where the time goes in v7:
time: 216 us; the launch traced here: 215 us
  blocking collectives  123 us (57%)
  starting transfers between devices  34 us (16%)
  waiting for transfers between devices  26.8 us (12%)
  between operations  14.5 us (7%)
  matrix products  7.51 us (3%)
  other arithmetic  3.51 us (2%)
  local copies, waits for them, and re-layouts  3.23 us (1%)
    all_to_all x10, blocking collectives, swap(): return lax.all_to_all(pieces, axis, 0, 0, tiled=True)  112 us
    all_to_all x3, waiting for transfers between devices, swap(): return lax.all_to_all(pieces, axis, 0, 0, tiled=True)  25.9 us
    all_to_all x3, starting transfers between devices, swap(): return lax.all_to_all(pieces, axis, 0, 0, tiled=True)  22.9 us
    all_gather x1, blocking collectives, on_device(): pair = lax.all_gather(pair, 'x')  11.2 us
    ppermute x1, starting transfers between devices, on_device(): other = lax.ppermute(features, 'c', [(0, 1), (1, 0)])  8.79 us
    dot_general x9, matrix products, product(): lax.dot_general(left, right, (dims, ((), ())), preferred_element_type=jnp...  7.51 us
  transfers between devices with their start and end apart: 6, of which 4 were waited for; matrix products, arithmetic and copies ran while one was open for 4% of the time, Pallas kernels for 0%

profile of v7, /device:TPU:1, one launch (start us, length us, event | category | flops | bytes accessed | tf_op | source)
XLA Modules:
  0.0 214.8 jit_solution(7711029855675769472)
XLA Ops:
  7.2 1.9 arrange.1
  9.1 8.8 %collective-permute-start = (bf16[512,440]{0,1:T(8,128)(2,1)}, bf16[512,440]{0,1:T(8,128)(2,1)S(1)}, u32[]{:S(2)}, u32[]{:S(2)}) collective-permute-start(bf16[512,440]{0,1:T(8,128)(2,1)} %param.5), channel_id=1, source_target_pairs={{0,4},{4,0},{1,5},{5,1},{2,6},{6,2},{3,7},{7,3},{8,12},{12,8},{9,1... | collective-permute-start | bytes 1351688 | tf_op jit(solution)/shard_map/ppermute | solution.py:130
  17.9 0.7 subtract_bitcast_fusion
  18.6 1.6 fusion.7
  20.3 0.6 fusion
  20.8 1.0 copy.23
  21.9 11.1 %all-to-all-start = ((bf16[64,8,440]{2,1,0:T(8,128)(2,1)}), bf16[64,8,440]{2,1,0:T(8,128)(2,1)S(1)}, u32[]{:S(2)}, u32[]{:S(2)}) async-start(bf16[64,8,440]{2,1,0:T(8,128)(2,1)} %bitcast.2), calls=%async_computation | async-start | bytes 1048576 | tf_op jit(solution)/shard_map/all_to_all | solution.py:18
  33.2 2.2 %collective-permute-start.1 = (bf16[152,128]{1,0:T(8,128)(2,1)S(1)}, bf16[152,128]{1,0:T(8,128)(2,1)S(1)}, u32[]{:S(2)}, u32[]{:S(2)}) collective-permute-start(bf16[152,128]{1,0:T(8,128)(2,1)S(1)} %pad.23), channel_id=1, source_target_pairs={{0,4},{4,0},{1,5},{5,1},{2,6},{6,2},{3,7},{7,3},{8,12},{12,8},{9,1... | collective-permute-start | bytes 116744 | tf_op jit(solution)/shard_map/ppermute | solution.py:136
  35.5 0.9 collective-permute-done.1
  36.4 14.6 %all-to-all-done = bf16[64,8,440]{2,1,0:T(8,128)(2,1)S(1)} async-done(((bf16[64,8,440]{2,1,0:T(8,128)(2,1)}), bf16[64,8,440]{2,1,0:T(8,128)(2,1)S(1)}, u32[]{:S(2)}, u32[]{:S(2)}) %all-to-all-start) | async-done | bytes 450592 | tf_op jit(solution)/shard_map/all_to_all | solution.py:18
  51.1 0.8 broadcast_in_dim.27
  52.0 6.8 %all-to-all-start.1 = ((bf16[64,8,440]{2,1,0:T(8,128)(2,1)}), bf16[64,8,440]{2,1,0:T(8,128)(2,1)S(1)}, u32[]{:S(2)}, u32[]{:S(2)}) async-start(bf16[64,8,440]{2,1,0:T(8,128)(2,1)} %broadcast_in_dim.27), calls=%async_computation.1 | async-start | bytes 1048576 | tf_op jit(solution)/shard_map/all_to_all | solution.py:18
  59.3 11.2 %all-gather = bf16[8,152,128]{2,1,0:T(8,128)(2,1)S(1)} all-gather(bf16[2,152,128]{2,1,0:T(8,128)(2,1)S(1)} %pad_maximum_fusion.1), channel_id=2, replica_groups=mesh['z'=8,'y'=8,'c'=2,'x'=4] {'x'}, dimensions={0}, use_global_device_ids=true | all-gather | bytes 389120 | tf_op jit(solution)/shard_map/all_gather | solution.py:140
  70.6 4.9 %all-to-all-done.1 = bf16[64,8,440]{2,1,0:T(8,128)(2,1)S(1)} async-done(((bf16[64,8,440]{2,1,0:T(8,128)(2,1)}), bf16[64,8,440]{2,1,0:T(8,128)(2,1)S(1)}, u32[]{:S(2)}, u32[]{:S(2)}) %all-to-all-start.1) | async-done | bytes 450592 | tf_op jit(solution)/shard_map/all_to_all | solution.py:18
  75.7 0.9 exponential_convert_fusion
  76.9 11.9 %all_to_all.65 = bf16[8,24,256]{2,1,0:T(8,128)(2,1)S(1)} all-to-all(bf16[8,24,256]{2,1,0:T(8,128)(2,1)S(1)} %bitcast.117), channel_id=1, replica_groups=mesh['z'=8,'y'=8,'c'=2,'x'=4] {'z'}, dimensions={0} | all-to-all | bytes 196608 | tf_op jit(solution)/shard_map/all_to_all | solution.py:18
  88.9 12.3 %all_to_all.66 = bf16[8,24,256]{2,1,0:T(8,128)(2,1)S(1)} all-to-all(bf16[8,24,256]{2,1,0:T(8,128)(2,1)S(1)} %broadcast_in_dim.28), channel_id=1, replica_groups=mesh['z'=8,'y'=8,'c'=2,'x'=4] {'y'}, dimensions={0} | all-to-all | bytes 196608 | tf_op jit(solution)/shard_map/all_to_all | solution.py:18
  101.2 14.4 %all_to_all.67 = bf16[8,24,256]{2,1,0:T(8,128)(2,1)S(1)} all-to-all(bf16[8,24,256]{2,1,0:T(8,128)(2,1)S(1)} %broadcast_in_dim.29), channel_id=1, replica_groups=mesh['z'=8,'y'=8,'c'=2,'x'=4] {'c','x'}, dimensions={0} | all-to-all | bytes 196608 | tf_op jit(solution)/shard_map/all_to_all | solution.py:18
  115.7 2.4 %fusion.6 = bf16[24,256]{1,0:T(8,128)(2,1)S(1)} fusion(bf16[256,512]{1,0:T(8,128)(2,1)S(1)} %fusion.15, bf16[24,2048]{1,0:T(8,128)(2,1)S(1)} %bitcast.111, bf16[512,2048]{1,0:T(8,128)(2,1)} %all-gather.3.cloned.1.call-done), kind=kOutput, calls=%fused_computation.13 | convolution fusion | flops 56641536 | bytes 2469888 | tf_op jit(solution)/shard_map/dot_general | solution.py:39
  118.1 9.9 %all_to_all.68 = bf16[8,24,256]{2,1,0:T(8,128)(2,1)S(1)} all-to-all(bf16[8,24,256]{2,1,0:T(8,128)(2,1)S(1)} %broadcast_in_dim.30), channel_id=1, replica_groups=mesh['z'=8,'y'=8,'c'=2,'x'=4] {'z'}, dimensions={0} | all-to-all | bytes 196608 | tf_op jit(solution)/shard_map/all_to_all | solution.py:18
  128.4 11.7 %all_to_all.69 = bf16[8,152,128]{2,1,0:T(8,128)(2,1)S(1)} all-to-all(bf16[8,152,128]{2,1,0:T(8,128)(2,1)S(1)} %bitcast.105), channel_id=1, replica_groups=mesh['z'=8,'y'=8,'c'=2,'x'=4] {'c','x'}, dimensions={0} | all-to-all | bytes 622592 | tf_op jit(solution)/shard_map/all_to_all | solution.py:18
  140.2 10.4 %all_to_all.70 = bf16[8,152,128]{2,1,0:T(8,128)(2,1)S(1)} all-to-all(bf16[8,152,128]{2,1,0:T(8,128)(2,1)S(1)} %broadcast_in_dim.31), channel_id=1, replica_groups=mesh['z'=8,'y'=8,'c'=2,'x'=4] {'c','x'}, dimensions={0} | all-to-all | bytes 622592 | tf_op jit(solution)/shard_map/all_to_all | solution.py:18
  151.0 9.9 %all_to_all.71 = bf16[8,24,256]{2,1,0:T(8,128)(2,1)S(1)} all-to-all(bf16[8,24,256]{2,1,0:T(8,128)(2,1)S(1)} %bitcast.118), channel_id=1, replica_groups=mesh['z'=8,'y'=8,'c'=2,'x'=4] {'z'}, dimensions={0} | all-to-all | bytes 196608 | tf_op jit(solution)/shard_map/all_to_all | solution.py:18
  161.0 11.2 %all_to_all.72 = bf16[8,24,256]{2,1,0:T(8,128)(2,1)S(1)} all-to-all(bf16[8,24,256]{2,1,0:T(8,128)(2,1)S(1)} %broadcast_in_dim.32), channel_id=1, replica_groups=mesh['z'=8,'y'=8,'c'=2,'x'=4] {'y'}, dimensions={0} | all-to-all | bytes 196608 | tf_op jit(solution)/shard_map/all_to_all | solution.py:18
  172.3 10.5 %all_to_all.73 = bf16[8,24,256]{2,1,0:T(8,128)(2,1)S(1)} all-to-all(bf16[8,24,256]{2,1,0:T(8,128)(2,1)S(1)} %broadcast_in_dim.33), channel_id=1, replica_groups=mesh['z'=8,'y'=8,'c'=2,'x'=4] {'c','x'}, dimensions={0} | all-to-all | bytes 196608 | tf_op jit(solution)/shard_map/all_to_all | solution.py:18
  182.8 0.8 fusion.5
  183.6 9.9 %all_to_all.74 = bf16[8,24,256]{2,1,0:T(8,128)(2,1)S(1)} all-to-all(bf16[8,24,256]{2,1,0:T(8,128)(2,1)S(1)} %broadcast_in_dim.34), channel_id=1, replica_groups=mesh['z'=8,'y'=8,'c'=2,'x'=4] {'z'}, dimensions={0} | all-to-all | bytes 196608 | tf_op jit(solution)/shard_map/all_to_all | solution.py:18
  194.3 0.8 copy.47
  195.1 5.1 %all-to-all-start.12 = ((bf16[8,152,128]{2,1,0:T(8,128)(2,1)}), bf16[8,152,128]{2,1,0:T(8,128)(2,1)S(1)}, u32[]{:S(2)}, u32[]{:S(2)}) async-start(bf16[8,152,128]{2,1,0:T(8,128)(2,1)} %bitcast.92), calls=%async_computation.12 | async-start | bytes 622592 | tf_op jit(solution)/shard_map/all_to_all | solution.py:18
  200.2 0.6 pad_maximum_fusion.2
  200.8 6.5 %all-to-all-done.12 = bf16[8,152,128]{2,1,0:T(8,128)(2,1)S(1)} async-done(((bf16[8,152,128]{2,1,0:T(8,128)(2,1)}), bf16[8,152,128]{2,1,0:T(8,128)(2,1)S(1)}, u32[]{:S(2)}, u32[]{:S(2)}) %all-to-all-start.12) | async-done | bytes 311328 | tf_op jit(solution)/shard_map/all_to_all | solution.py:18
  207.3 0.6 fusion.74
  (68 shorter events, 3.5 us)
Async XLA Ops:
  7.2 108.5 %all-gather.3.cloned.1.call-start = ((), (), s32[]{:S(2)}) async-start(), calls=%async_computation.13 | async-start | bytes 2129920 | tf_op jit(solution)/shard_map/all_gather | solution.py:118
  9.1 11.2 %collective-permute-start = (bf16[512,440]{0,1:T(8,128)(2,1)}, bf16[512,440]{0,1:T(8,128)(2,1)S(1)}, u32[]{:S(2)}, u32[]{:S(2)}) collective-permute-start(bf16[512,440]{0,1:T(8,128)(2,1)} %param.5), channel_id=1, source_target_pairs={{0,4},{4,0},{1,5},{5,1},{2,6},{6,2},{3,7},{7,3},{8,12},{12,8},{9,1... | collective-permute-start | bytes 1351688 | tf_op jit(solution)/shard_map/ppermute | solution.py:130
  20.2 13.0 %copy-start.2 = (f32[128,147]{0,1:T(8,128)S(1)}, f32[128,147]{0,1:T(8,128)}, u32[]{:S(2)}) copy-start(f32[128,147]{0,1:T(8,128)} %param.6) | copy-start | bytes 225796
  21.8 36.9 %copy-start.3 = (f32[2,4,147]{2,1,0:T(4,128)S(1)}, f32[2,4,147]{2,1,0:T(4,128)}, u32[]{:S(2)}) copy-start(f32[2,4,147]{2,1,0:T(4,128)} %param.7) | copy-start | bytes 14116
  21.8 36.9 %copy-start.1 = (bf16[512,440]{0,1:T(8,128)(2,1)S(1)}, bf16[512,440]{0,1:T(8,128)(2,1)}, u32[]{:S(2)}) copy-start(bf16[512,440]{0,1:T(8,128)(2,1)} %param.5) | copy-start | bytes 1351684
  21.9 29.2 %all-to-all-start = ((bf16[64,8,440]{2,1,0:T(8,128)(2,1)}), bf16[64,8,440]{2,1,0:T(8,128)(2,1)S(1)}, u32[]{:S(2)}, u32[]{:S(2)}) async-start(bf16[64,8,440]{2,1,0:T(8,128)(2,1)} %bitcast.2), calls=%async_computation | async-start | bytes 1048576 | tf_op jit(solution)/shard_map/all_to_all | solution.py:18
  33.2 3.1 %collective-permute-start.1 = (bf16[152,128]{1,0:T(8,128)(2,1)S(1)}, bf16[152,128]{1,0:T(8,128)(2,1)S(1)}, u32[]{:S(2)}, u32[]{:S(2)}) collective-permute-start(bf16[152,128]{1,0:T(8,128)(2,1)S(1)} %pad.23), channel_id=1, source_target_pairs={{0,4},{4,0},{1,5},{5,1},{2,6},{6,2},{3,7},{7,3},{8,12},{12,8},{9,1... | collective-permute-start | bytes 116744 | tf_op jit(solution)/shard_map/ppermute | solution.py:136
  52.0 23.5 %all-to-all-start.1 = ((bf16[64,8,440]{2,1,0:T(8,128)(2,1)}), bf16[64,8,440]{2,1,0:T(8,128)(2,1)S(1)}, u32[]{:S(2)}, u32[]{:S(2)}) async-start(bf16[64,8,440]{2,1,0:T(8,128)(2,1)} %broadcast_in_dim.27), calls=%async_computation.1 | async-start | bytes 1048576 | tf_op jit(solution)/shard_map/all_to_all | solution.py:18
  140.2 42.6 %copy-start = (bf16[512,2048]{1,0:T(8,128)(2,1)S(1)}, bf16[512,2048]{1,0:T(8,128)(2,1)}, u32[]{:S(2)}) copy-start(bf16[512,2048]{1,0:T(8,128)(2,1)} %all-gather.3.cloned.1.call-done) | copy-start | bytes 6291460
  195.1 12.2 %all-to-all-start.12 = ((bf16[8,152,128]{2,1,0:T(8,128)(2,1)}), bf16[8,152,128]{2,1,0:T(8,128)(2,1)S(1)}, u32[]{:S(2)}, u32[]{:S(2)}) async-start(bf16[8,152,128]{2,1,0:T(8,128)(2,1)} %bitcast.92), calls=%async_computation.12 | async-start | bytes 622592 | tf_op jit(solution)/shard_map/all_to_all | solution.py:18
Sparse Core Ops, SparseCore 0:
  11.6 95.0 all-gather.2

commit v8 on v6

--- a/solution.py
+++ b/solution.py
@@ -41,15 +41,17 @@
     )
 
 
-def arranged(rows, numbers, plane, cell):
+def arranged(rows, numbers, plane, cell, where):
     steps, own, columns = rows.shape
     count, group = steps * own, plane * own
     if columns % 2048 or count != 8 or cell * own != 32:
         rows = rows.astype(jnp.bfloat16).reshape(count, plane, cell, own)
+        member, base = where()
         numbers = numbers.reshape(steps, plane, cell, own).transpose(2, 0, 1, 3)
+        numbers = lax.dynamic_index_in_dim(numbers, member, 0, keepdims=False)
         return (
             rows.transpose(0, 2, 1, 3).reshape(count, columns),
-            numbers.reshape(cell, steps, group),
+            numbers.reshape(steps, group) - base,
         )
     blocks = columns // 128
     run = 128 // cell
@@ -68,6 +70,8 @@
         tall = jnp.dot(tall.astype(jnp.bfloat16), order, preferred_element_type=jnp.float32)
         part = lax.broadcasted_iota(jnp.int32, (16, 128), 1) >> 4
         wide = blocks // cell
+        here, base = where()
+        found = [jnp.zeros((steps, 128), jnp.float32)] * wide
         for out in range(blocks):
             member, first = out // wide, out % wide * cell
             joined = jnp.zeros((16, 128), jnp.float32)
@@ -79,14 +83,17 @@
                 joined = jnp.where(part == k, piece, joined)
             rows_out[:, 128 * out : 128 * (out + 1)] = joined[:count].astype(rows_out.dtype)
             number = joined[count : count + steps] * 256.0 + joined[count + steps : count + 2 * steps]
-            at = out % wide * 128
-            numbers_out[member, :, at : at + 128] = number.astype(jnp.int32)
+            at = out % wide
+            found[at] = jnp.where(here == member, number, found[at])
+        for at in range(wide):
+            local = found[at].astype(jnp.int32) - base
+            numbers_out[:, 128 * at : 128 * (at + 1)] = local
 
     return pl.pallas_call(
         kernel,
         out_shape=(
             jax.ShapeDtypeStruct((count, columns), jnp.bfloat16),
-            jax.ShapeDtypeStruct((cell, steps, group), jnp.int32),
+            jax.ShapeDtypeStruct((steps, group), jnp.int32),
         ),
         name="arrange",
     )(rows, numbers)
@@ -114,17 +121,20 @@
     gamma_rate = 4.0 / width
     low = jnp.bfloat16
 
-    inverse, chosen = arranged(block_inverse.transpose(0, 2, 1), block_columns, plane, cell)
+    def where():
+        at = lax.axis_index("z") * ny + lax.axis_index("y")
+        return lax.axis_index("c") * nx + lax.axis_index("x"), at * nc * features.shape[0]
+
+    inverse, chosen = arranged(block_inverse.transpose(0, 2, 1), block_columns, plane, cell, where)
     inverse = lax.all_gather(inverse, PLANE, axis=0, tiled=True)
     current = jnp.pad(residual.T, ((0, high - classes), (0, 0)))
     first = lax.axis_index("c") == 0
 
-    chosen = lax.dynamic_index_in_dim(chosen, member, 0, keepdims=False).reshape(steps * group)
-
+    chosen = chosen.reshape(steps * group)
     other = lax.ppermute(features, "c", [(0, 1), (1, 0)])
     frames = ordered(features, other, first).reshape(nc * features.shape[0], width)
     spots = lax.broadcasted_iota(jnp.int32, (steps * group, frames.shape[0]), 1)
-    picks = ((chosen - place * frames.shape[0])[:, None] == spots).astype(low)
+    picks = (chosen[:, None] == spots).astype(low)
     part = product(picks, frames, ((1,), (0,))).astype(low)
     part, pair = lax.optimization_barrier((part, residual))
     pair = jnp.pad(pair.T, ((0, high - classes), (0, 0))).astype(low)

time: 215 us -> 215 us (level)
  no operation moved by 1% of the time
where the time goes in v8:
time: 215 us; the launch traced here: 214 us
  blocking collectives  122 us (57%)
  starting transfers between devices  34.3 us (16%)
  waiting for transfers between devices  27.7 us (13%)
  between operations  14.4 us (7%)
  matrix products  6.13 us (3%)
  local copies, waits for them, and re-layouts  3.91 us (2%)
  other arithmetic  3.83 us (2%)
    all_to_all x10, blocking collectives, swap(): return lax.all_to_all(pieces, axis, 0, 0, tiled=True)  111 us
    all_to_all x3, waiting for transfers between devices, swap(): return lax.all_to_all(pieces, axis, 0, 0, tiled=True)  26.2 us
    all_to_all x3, starting transfers between devices, swap(): return lax.all_to_all(pieces, axis, 0, 0, tiled=True)  22.9 us
    all_gather x1, blocking collectives, on_device(): pair = lax.all_gather(pair, 'x')  10.8 us
    ppermute x1, starting transfers between devices, on_device(): other = lax.ppermute(features, 'c', [(0, 1), (1, 0)])  8.79 us
    dot_general x8, matrix products, product(): lax.dot_general(left, right, (dims, ((), ())), preferred_element_type=jnp...  6.13 us
  transfers between devices with their start and end apart: 6, of which 5 were waited for; matrix products, arithmetic and copies ran while one was open for 4% of the time, Pallas kernels for 0%

profile of v8, /device:TPU:1, one launch (start us, length us, event | category | flops | bytes accessed | tf_op | source)
XLA Modules:
  0.0 213.9 jit_solution(1805026097384603267)
XLA Ops:
  7.2 1.9 arrange.1
  9.1 8.8 %collective-permute-start = (bf16[512,440]{0,1:T(8,128)(2,1)}, bf16[512,440]{0,1:T(8,128)(2,1)S(1)}, u32[]{:S(2)}, u32[]{:S(2)}) collective-permute-start(bf16[512,440]{0,1:T(8,128)(2,1)} %param.5), channel_id=1, source_target_pairs={{0,4},{4,0},{1,5},{5,1},{2,6},{6,2},{3,7},{7,3},{8,12},{12,8},{9,1... | collective-permute-start | bytes 1351688 | tf_op jit(solution)/shard_map/ppermute | solution.py:134
  17.9 0.7 copy.39
  18.6 0.9 collective-permute-done
  19.5 1.1 select_bitcast_fusion.1
  20.8 0.8 fusion.1
  21.6 1.0 copy.24
  22.6 11.1 %all-to-all-start = ((bf16[64,8,440]{2,1,0:T(8,128)(2,1)}), bf16[64,8,440]{2,1,0:T(8,128)(2,1)S(1)}, u32[]{:S(2)}, u32[]{:S(2)}) async-start(bf16[64,8,440]{2,1,0:T(8,128)(2,1)} %bitcast.4), calls=%async_computation | async-start | bytes 1048576 | tf_op jit(solution)/shard_map/all_to_all | solution.py:18
  33.8 2.6 %collective-permute-start.1 = (bf16[152,128]{1,0:T(8,128)(2,1)S(1)}, bf16[152,128]{1,0:T(8,128)(2,1)S(1)}, u32[]{:S(2)}, u32[]{:S(2)}) collective-permute-start(bf16[152,128]{1,0:T(8,128)(2,1)S(1)} %pad.23), channel_id=1, source_target_pairs={{0,4},{4,0},{1,5},{5,1},{2,6},{6,2},{3,7},{7,3},{8,12},{12,8},{9,1... | collective-permute-start | bytes 116744 | tf_op jit(solution)/shard_map/ppermute | solution.py:141
  37.2 14.5 %all-to-all-done = bf16[64,8,440]{2,1,0:T(8,128)(2,1)S(1)} async-done(((bf16[64,8,440]{2,1,0:T(8,128)(2,1)}), bf16[64,8,440]{2,1,0:T(8,128)(2,1)S(1)}, u32[]{:S(2)}, u32[]{:S(2)}) %all-to-all-start) | async-done | bytes 450592 | tf_op jit(solution)/shard_map/all_to_all | solution.py:18
  51.9 0.8 broadcast_in_dim.27
  52.7 6.7 %all-to-all-start.1 = ((bf16[64,8,440]{2,1,0:T(8,128)(2,1)}), bf16[64,8,440]{2,1,0:T(8,128)(2,1)S(1)}, u32[]{:S(2)}, u32[]{:S(2)}) async-start(bf16[64,8,440]{2,1,0:T(8,128)(2,1)} %broadcast_in_dim.27), calls=%async_computation.1 | async-start | bytes 1048576 | tf_op jit(solution)/shard_map/all_to_all | solution.py:18
  59.7 10.8 %all-gather = bf16[8,152,128]{2,1,0:T(8,128)(2,1)S(1)} all-gather(bf16[2,152,128]{2,1,0:T(8,128)(2,1)S(1)} %pad_maximum_fusion.1), channel_id=2, replica_groups=mesh['z'=8,'y'=8,'c'=2,'x'=4] {'x'}, dimensions={0}, use_global_device_ids=true | all-gather | bytes 389120 | tf_op jit(solution)/shard_map/all_gather | solution.py:145
  70.7 5.2 %all-to-all-done.1 = bf16[64,8,440]{2,1,0:T(8,128)(2,1)S(1)} async-done(((bf16[64,8,440]{2,1,0:T(8,128)(2,1)}), bf16[64,8,440]{2,1,0:T(8,128)(2,1)S(1)}, u32[]{:S(2)}, u32[]{:S(2)}) %all-to-all-start.1) | async-done | bytes 450592 | tf_op jit(solution)/shard_map/all_to_all | solution.py:18
  76.1 0.9 exponential_convert_fusion
  77.4 11.8 %all_to_all.65 = bf16[8,24,256]{2,1,0:T(8,128)(2,1)S(1)} all-to-all(bf16[8,24,256]{2,1,0:T(8,128)(2,1)S(1)} %bitcast.113), channel_id=1, replica_groups=mesh['z'=8,'y'=8,'c'=2,'x'=4] {'z'}, dimensions={0} | all-to-all | bytes 196608 | tf_op jit(solution)/shard_map/all_to_all | solution.py:18
  89.2 11.6 %all_to_all.66 = bf16[8,24,256]{2,1,0:T(8,128)(2,1)S(1)} all-to-all(bf16[8,24,256]{2,1,0:T(8,128)(2,1)S(1)} %broadcast_in_dim.28), channel_id=1, replica_groups=mesh['z'=8,'y'=8,'c'=2,'x'=4] {'y'}, dimensions={0} | all-to-all | bytes 196608 | tf_op jit(solution)/shard_map/all_to_all | solution.py:18
  100.8 15.3 %all_to_all.67 = bf16[8,24,256]{2,1,0:T(8,128)(2,1)S(1)} all-to-all(bf16[8,24,256]{2,1,0:T(8,128)(2,1)S(1)} %broadcast_in_dim.29), channel_id=1, replica_groups=mesh['z'=8,'y'=8,'c'=2,'x'=4] {'c','x'}, dimensions={0} | all-to-all | bytes 196608 | tf_op jit(solution)/shard_map/all_to_all | solution.py:18
  116.2 2.4 %fusion.7 = bf16[24,256]{1,0:T(8,128)(2,1)S(1)} fusion(bf16[256,512]{1,0:T(8,128)(2,1)S(1)} %fusion.14, bf16[24,2048]{1,0:T(8,128)(2,1)S(1)} %bitcast.107, bf16[512,2048]{1,0:T(8,128)(2,1)} %all-gather.3.cloned.1.call-done), kind=kOutput, calls=%fused_computation.14 | convolution fusion | flops 56641536 | bytes 2469888 | tf_op jit(solution)/shard_map/dot_general | solution.py:39
  118.6 9.9 %all_to_all.68 = bf16[8,24,256]{2,1,0:T(8,128)(2,1)S(1)} all-to-all(bf16[8,24,256]{2,1,0:T(8,128)(2,1)S(1)} %broadcast_in_dim.30), channel_id=1, replica_groups=mesh['z'=8,'y'=8,'c'=2,'x'=4] {'z'}, dimensions={0} | all-to-all | bytes 196608 | tf_op jit(solution)/shard_map/all_to_all | solution.py:18
  128.9 11.7 %all_to_all.69 = bf16[8,152,128]{2,1,0:T(8,128)(2,1)S(1)} all-to-all(bf16[8,152,128]{2,1,0:T(8,128)(2,1)S(1)} %bitcast.100), channel_id=1, replica_groups=mesh['z'=8,'y'=8,'c'=2,'x'=4] {'c','x'}, dimensions={0} | all-to-all | bytes 622592 | tf_op jit(solution)/shard_map/all_to_all | solution.py:18
  140.7 10.4 %all_to_all.70 = bf16[8,152,128]{2,1,0:T(8,128)(2,1)S(1)} all-to-all(bf16[8,152,128]{2,1,0:T(8,128)(2,1)S(1)} %broadcast_in_dim.31), channel_id=1, replica_groups=mesh['z'=8,'y'=8,'c'=2,'x'=4] {'c','x'}, dimensions={0} | all-to-all | bytes 622592 | tf_op jit(solution)/shard_map/all_to_all | solution.py:18
  151.6 9.9 %all_to_all.71 = bf16[8,24,256]{2,1,0:T(8,128)(2,1)S(1)} all-to-all(bf16[8,24,256]{2,1,0:T(8,128)(2,1)S(1)} %bitcast.114), channel_id=1, replica_groups=mesh['z'=8,'y'=8,'c'=2,'x'=4] {'z'}, dimensions={0} | all-to-all | bytes 196608 | tf_op jit(solution)/shard_map/all_to_all | solution.py:18
  161.5 10.0 %all_to_all.72 = bf16[8,24,256]{2,1,0:T(8,128)(2,1)S(1)} all-to-all(bf16[8,24,256]{2,1,0:T(8,128)(2,1)S(1)} %broadcast_in_dim.32), channel_id=1, replica_groups=mesh['z'=8,'y'=8,'c'=2,'x'=4] {'y'}, dimensions={0} | all-to-all | bytes 196608 | tf_op jit(solution)/shard_map/all_to_all | solution.py:18
  171.6 10.3 %all_to_all.73 = bf16[8,24,256]{2,1,0:T(8,128)(2,1)S(1)} all-to-all(bf16[8,24,256]{2,1,0:T(8,128)(2,1)S(1)} %broadcast_in_dim.33), channel_id=1, replica_groups=mesh['z'=8,'y'=8,'c'=2,'x'=4] {'c','x'}, dimensions={0} | all-to-all | bytes 196608 | tf_op jit(solution)/shard_map/all_to_all | solution.py:18
  181.8 0.8 fusion.6
  182.7 9.9 %all_to_all.74 = bf16[8,24,256]{2,1,0:T(8,128)(2,1)S(1)} all-to-all(bf16[8,24,256]{2,1,0:T(8,128)(2,1)S(1)} %broadcast_in_dim.34), channel_id=1, replica_groups=mesh['z'=8,'y'=8,'c'=2,'x'=4] {'z'}, dimensions={0} | all-to-all | bytes 196608 | tf_op jit(solution)/shard_map/all_to_all | solution.py:18
  193.4 0.8 copy.46
  194.1 5.1 %all-to-all-start.12 = ((bf16[8,152,128]{2,1,0:T(8,128)(2,1)}), bf16[8,152,128]{2,1,0:T(8,128)(2,1)S(1)}, u32[]{:S(2)}, u32[]{:S(2)}) async-start(bf16[8,152,128]{2,1,0:T(8,128)(2,1)} %bitcast.87), calls=%async_computation.12 | async-start | bytes 622592 | tf_op jit(solution)/shard_map/all_to_all | solution.py:18
  199.3 0.6 pad_maximum_fusion.2
  199.9 6.5 %all-to-all-done.12 = bf16[8,152,128]{2,1,0:T(8,128)(2,1)S(1)} async-done(((bf16[8,152,128]{2,1,0:T(8,128)(2,1)}), bf16[8,152,128]{2,1,0:T(8,128)(2,1)S(1)}, u32[]{:S(2)}, u32[]{:S(2)}) %all-to-all-start.12) | async-done | bytes 311328 | tf_op jit(solution)/shard_map/all_to_all | solution.py:18
  206.4 0.6 fusion.73
  (63 shorter events, 4.0 us)
Async XLA Ops:
  7.2 109.0 %all-gather.3.cloned.1.call-start = ((), (), s32[]{:S(2)}) async-start(), calls=%async_computation.13 | async-start | bytes 2129920 | tf_op jit(solution)/shard_map/all_gather | solution.py:129
  9.1 10.4 %collective-permute-start = (bf16[512,440]{0,1:T(8,128)(2,1)}, bf16[512,440]{0,1:T(8,128)(2,1)S(1)}, u32[]{:S(2)}, u32[]{:S(2)}) collective-permute-start(bf16[512,440]{0,1:T(8,128)(2,1)} %param.5), channel_id=1, source_target_pairs={{0,4},{4,0},{1,5},{5,1},{2,6},{6,2},{3,7},{7,3},{8,12},{12,8},{9,1... | collective-permute-start | bytes 1351688 | tf_op jit(solution)/shard_map/ppermute | solution.py:134
  20.8 12.9 %copy-start.1 = (f32[128,147]{0,1:T(8,128)S(1)}, f32[128,147]{0,1:T(8,128)}, u32[]{:S(2)}) copy-start(f32[128,147]{0,1:T(8,128)} %param.6) | copy-start | bytes 225796
  22.6 36.9 %copy-start.2 = (f32[2,4,147]{2,1,0:T(4,128)S(1)}, f32[2,4,147]{2,1,0:T(4,128)}, u32[]{:S(2)}) copy-start(f32[2,4,147]{2,1,0:T(4,128)} %param.7) | copy-start | bytes 14116
  22.6 29.1 %all-to-all-start = ((bf16[64,8,440]{2,1,0:T(8,128)(2,1)}), bf16[64,8,440]{2,1,0:T(8,128)(2,1)S(1)}, u32[]{:S(2)}, u32[]{:S(2)}) async-start(bf16[64,8,440]{2,1,0:T(8,128)(2,1)} %bitcast.4), calls=%async_computation | async-start | bytes 1048576 | tf_op jit(solution)/shard_map/all_to_all | solution.py:18
  33.8 3.4 %collective-permute-start.1 = (bf16[152,128]{1,0:T(8,128)(2,1)S(1)}, bf16[152,128]{1,0:T(8,128)(2,1)S(1)}, u32[]{:S(2)}, u32[]{:S(2)}) collective-permute-start(bf16[152,128]{1,0:T(8,128)(2,1)S(1)} %pad.23), channel_id=1, source_target_pairs={{0,4},{4,0},{1,5},{5,1},{2,6},{6,2},{3,7},{7,3},{8,12},{12,8},{9,1... | collective-permute-start | bytes 116744 | tf_op jit(solution)/shard_map/ppermute | solution.py:141
  52.7 23.1 %all-to-all-start.1 = ((bf16[64,8,440]{2,1,0:T(8,128)(2,1)}), bf16[64,8,440]{2,1,0:T(8,128)(2,1)S(1)}, u32[]{:S(2)}, u32[]{:S(2)}) async-start(bf16[64,8,440]{2,1,0:T(8,128)(2,1)} %broadcast_in_dim.27), calls=%async_computation.1 | async-start | bytes 1048576 | tf_op jit(solution)/shard_map/all_to_all | solution.py:18
  140.7 41.1 %copy-start = (bf16[512,2048]{1,0:T(8,128)(2,1)S(1)}, bf16[512,2048]{1,0:T(8,128)(2,1)}, u32[]{:S(2)}) copy-start(bf16[512,2048]{1,0:T(8,128)(2,1)} %all-gather.3.cloned.1.call-done) | copy-start | bytes 6291460
  194.1 12.2 %all-to-all-start.12 = ((bf16[8,152,128]{2,1,0:T(8,128)(2,1)}), bf16[8,152,128]{2,1,0:T(8,128)(2,1)S(1)}, u32[]{:S(2)}, u32[]{:S(2)}) async-start(bf16[8,152,128]{2,1,0:T(8,128)(2,1)} %bitcast.87), calls=%async_computation.12 | async-start | bytes 622592 | tf_op jit(solution)/shard_map/all_to_all | solution.py:18
Sparse Core Ops, SparseCore 0:
  11.6 93.9 all-gather.2

commit v9 on v6

--- a/solution.py
+++ b/solution.py
@@ -109,8 +109,8 @@
     columns = block_columns.shape[1]
     group = plane * own
     high = -(-classes // 8) * 8
-    share = -(-classes // (nz * 8)) * 8
-    tall = nz * share
+    share = -(-classes // (ny * 8)) * 8
+    tall = ny * share
     gamma_rate = 4.0 / width
     low = jnp.bfloat16
 
@@ -155,15 +155,15 @@
         for i in range(own):
             gradient = jnp.where(lanes == i, gradient - RIDGE * weights[:, i : i + 1], gradient)
         gradient = gradient.astype(low)
-        part = total(swap(gradient.reshape(nz, share, group), "z"))
-        part = total(spread(part.astype(low), "y"))
+        part = total(swap(gradient.reshape(ny, share, group), "y"))
+        part = total(spread(part.astype(low), "z"))
         part = part.astype(low)
         if step > 0:
             places = step_places(step, steps, plane, own)
         part = side_by_side(spread(part, CELL))
         part = product(part, inverse, ((1,), (1,))).astype(low)
         part = product(part, places, ((1,), (1,))).astype(low)
-        change = spread(part, "z").reshape(tall, group)[:high]
+        change = spread(part, "y").reshape(tall, group)[:high]
         update = product(change, kernel[block], ((1,), (0,))).astype(low)
         update = update.reshape(high, cell, own_rows).transpose(1, 0, 2)
         current = current - total(swap(update, CELL))

time: 215 us -> 215 us (level)
  no operation moved by 1% of the time
where the time goes in v9:
time: 215 us; the launch traced here: 214 us
  blocking collectives  122 us (57%)
  starting transfers between devices  34.3 us (16%)
  waiting for transfers between devices  27.7 us (13%)
  between operations  14.4 us (7%)
  matrix products  6.13 us (3%)
  other arithmetic  4.51 us (2%)
  local copies, waits for them, and re-layouts  3.23 us (2%)
    all_to_all x10, blocking collectives, swap(): return lax.all_to_all(pieces, axis, 0, 0, tiled=True)  111 us
    all_to_all x3, waiting for transfers between devices, swap(): return lax.all_to_all(pieces, axis, 0, 0, tiled=True)  26.2 us
    all_to_all x3, starting transfers between devices, swap(): return lax.all_to_all(pieces, axis, 0, 0, tiled=True)  22.9 us
    all_gather x1, blocking collectives, on_device(): pair = lax.all_gather(pair, 'x')  10.8 us
    ppermute x1, starting transfers between devices, on_device(): other = lax.ppermute(features, 'c', [(0, 1), (1, 0)])  8.79 us
    dot_general x8, matrix products, product(): lax.dot_general(left, right, (dims, ((), ())), preferred_element_type=jnp...  6.13 us
  transfers between devices with their start and end apart: 6, of which 5 were waited for; matrix products, arithmetic and copies ran while one was open for 4% of the time, Pallas kernels for 0%

profile of v9, /device:TPU:1, one launch (start us, length us, event | category | flops | bytes accessed | tf_op | source)
XLA Modules:
  0.0 214.2 jit_solution(7929694044578772873)
XLA Ops:
  7.2 1.9 arrange.1
  9.1 8.8 %collective-permute-start = (bf16[512,440]{0,1:T(8,128)(2,1)}, bf16[512,440]{0,1:T(8,128)(2,1)S(1)}, u32[]{:S(2)}, u32[]{:S(2)}) collective-permute-start(bf16[512,440]{0,1:T(8,128)(2,1)} %param.5), channel_id=1, source_target_pairs={{0,4},{4,0},{1,5},{5,1},{2,6},{6,2},{3,7},{7,3},{8,12},{12,8},{9,1... | collective-permute-start | bytes 1351688 | tf_op jit(solution)/shard_map/ppermute | solution.py:124
  17.9 0.7 subtract_bitcast_fusion
  18.6 0.9 collective-permute-done
  19.5 1.1 select_bitcast_fusion.1
  20.8 0.8 fusion.1
  21.6 1.0 copy.24
  22.6 11.1 %all-to-all-start = ((bf16[64,8,440]{2,1,0:T(8,128)(2,1)}), bf16[64,8,440]{2,1,0:T(8,128)(2,1)S(1)}, u32[]{:S(2)}, u32[]{:S(2)}) async-start(bf16[64,8,440]{2,1,0:T(8,128)(2,1)} %bitcast.4), calls=%async_computation | async-start | bytes 1048576 | tf_op jit(solution)/shard_map/all_to_all | solution.py:18
  33.8 2.6 %collective-permute-start.1 = (bf16[152,128]{1,0:T(8,128)(2,1)S(1)}, bf16[152,128]{1,0:T(8,128)(2,1)S(1)}, u32[]{:S(2)}, u32[]{:S(2)}) collective-permute-start(bf16[152,128]{1,0:T(8,128)(2,1)S(1)} %pad.23), channel_id=1, source_target_pairs={{0,4},{4,0},{1,5},{5,1},{2,6},{6,2},{3,7},{7,3},{8,12},{12,8},{9,1... | collective-permute-start | bytes 116744 | tf_op jit(solution)/shard_map/ppermute | solution.py:131
  37.2 14.5 %all-to-all-done = bf16[64,8,440]{2,1,0:T(8,128)(2,1)S(1)} async-done(((bf16[64,8,440]{2,1,0:T(8,128)(2,1)}), bf16[64,8,440]{2,1,0:T(8,128)(2,1)S(1)}, u32[]{:S(2)}, u32[]{:S(2)}) %all-to-all-start) | async-done | bytes 450592 | tf_op jit(solution)/shard_map/all_to_all | solution.py:18
  51.9 0.8 broadcast_in_dim.27
  52.7 6.7 %all-to-all-start.1 = ((bf16[64,8,440]{2,1,0:T(8,128)(2,1)}), bf16[64,8,440]{2,1,0:T(8,128)(2,1)S(1)}, u32[]{:S(2)}, u32[]{:S(2)}) async-start(bf16[64,8,440]{2,1,0:T(8,128)(2,1)} %broadcast_in_dim.27), calls=%async_computation.1 | async-start | bytes 1048576 | tf_op jit(solution)/shard_map/all_to_all | solution.py:18
  59.7 10.8 %all-gather = bf16[8,152,128]{2,1,0:T(8,128)(2,1)S(1)} all-gather(bf16[2,152,128]{2,1,0:T(8,128)(2,1)S(1)} %pad_maximum_fusion.1), channel_id=2, replica_groups=mesh['z'=8,'y'=8,'c'=2,'x'=4] {'x'}, dimensions={0}, use_global_device_ids=true | all-gather | bytes 389120 | tf_op jit(solution)/shard_map/all_gather | solution.py:135
  70.6 5.2 %all-to-all-done.1 = bf16[64,8,440]{2,1,0:T(8,128)(2,1)S(1)} async-done(((bf16[64,8,440]{2,1,0:T(8,128)(2,1)}), bf16[64,8,440]{2,1,0:T(8,128)(2,1)S(1)}, u32[]{:S(2)}, u32[]{:S(2)}) %all-to-all-start.1) | async-done | bytes 450592 | tf_op jit(solution)/shard_map/all_to_all | solution.py:18
  76.1 0.9 exponential_convert_fusion
  77.4 12.2 %all_to_all.65 = bf16[8,24,256]{2,1,0:T(8,128)(2,1)S(1)} all-to-all(bf16[8,24,256]{2,1,0:T(8,128)(2,1)S(1)} %bitcast.114), channel_id=1, replica_groups=mesh['z'=8,'y'=8,'c'=2,'x'=4] {'y'}, dimensions={0} | all-to-all | bytes 196608 | tf_op jit(solution)/shard_map/all_to_all | solution.py:18
  89.6 11.4 %all_to_all.66 = bf16[8,24,256]{2,1,0:T(8,128)(2,1)S(1)} all-to-all(bf16[8,24,256]{2,1,0:T(8,128)(2,1)S(1)} %broadcast_in_dim.28), channel_id=1, replica_groups=mesh['z'=8,'y'=8,'c'=2,'x'=4] {'z'}, dimensions={0} | all-to-all | bytes 196608 | tf_op jit(solution)/shard_map/all_to_all | solution.py:18
  101.0 15.5 %all_to_all.67 = bf16[8,24,256]{2,1,0:T(8,128)(2,1)S(1)} all-to-all(bf16[8,24,256]{2,1,0:T(8,128)(2,1)S(1)} %broadcast_in_dim.29), channel_id=1, replica_groups=mesh['z'=8,'y'=8,'c'=2,'x'=4] {'c','x'}, dimensions={0} | all-to-all | bytes 196608 | tf_op jit(solution)/shard_map/all_to_all | solution.py:18
  116.5 2.4 %fusion.7 = bf16[24,256]{1,0:T(8,128)(2,1)S(1)} fusion(bf16[256,512]{1,0:T(8,128)(2,1)S(1)} %fusion.14, bf16[24,2048]{1,0:T(8,128)(2,1)S(1)} %bitcast.108, bf16[512,2048]{1,0:T(8,128)(2,1)} %all-gather.3.cloned.1.call-done), kind=kOutput, calls=%fused_computation.14 | convolution fusion | flops 56641536 | bytes 2469888 | tf_op jit(solution)/shard_map/dot_general | solution.py:39
  119.0 9.9 %all_to_all.68 = bf16[8,24,256]{2,1,0:T(8,128)(2,1)S(1)} all-to-all(bf16[8,24,256]{2,1,0:T(8,128)(2,1)S(1)} %broadcast_in_dim.30), channel_id=1, replica_groups=mesh['z'=8,'y'=8,'c'=2,'x'=4] {'y'}, dimensions={0} | all-to-all | bytes 196608 | tf_op jit(solution)/shard_map/all_to_all | solution.py:18
  129.2 11.7 %all_to_all.69 = bf16[8,152,128]{2,1,0:T(8,128)(2,1)S(1)} all-to-all(bf16[8,152,128]{2,1,0:T(8,128)(2,1)S(1)} %bitcast.101), channel_id=1, replica_groups=mesh['z'=8,'y'=8,'c'=2,'x'=4] {'c','x'}, dimensions={0} | all-to-all | bytes 622592 | tf_op jit(solution)/shard_map/all_to_all | solution.py:18
  141.0 10.4 %all_to_all.70 = bf16[8,152,128]{2,1,0:T(8,128)(2,1)S(1)} all-to-all(bf16[8,152,128]{2,1,0:T(8,128)(2,1)S(1)} %broadcast_in_dim.31), channel_id=1, replica_groups=mesh['z'=8,'y'=8,'c'=2,'x'=4] {'c','x'}, dimensions={0} | all-to-all | bytes 622592 | tf_op jit(solution)/shard_map/all_to_all | solution.py:18
  151.9 9.9 %all_to_all.71 = bf16[8,24,256]{2,1,0:T(8,128)(2,1)S(1)} all-to-all(bf16[8,24,256]{2,1,0:T(8,128)(2,1)S(1)} %bitcast.115), channel_id=1, replica_groups=mesh['z'=8,'y'=8,'c'=2,'x'=4] {'y'}, dimensions={0} | all-to-all | bytes 196608 | tf_op jit(solution)/shard_map/all_to_all | solution.py:18
  161.8 10.0 %all_to_all.72 = bf16[8,24,256]{2,1,0:T(8,128)(2,1)S(1)} all-to-all(bf16[8,24,256]{2,1,0:T(8,128)(2,1)S(1)} %broadcast_in_dim.32), channel_id=1, replica_groups=mesh['z'=8,'y'=8,'c'=2,'x'=4] {'z'}, dimensions={0} | all-to-all | bytes 196608 | tf_op jit(solution)/shard_map/all_to_all | solution.py:18
  171.9 10.3 %all_to_all.73 = bf16[8,24,256]{2,1,0:T(8,128)(2,1)S(1)} all-to-all(bf16[8,24,256]{2,1,0:T(8,128)(2,1)S(1)} %broadcast_in_dim.33), channel_id=1, replica_groups=mesh['z'=8,'y'=8,'c'=2,'x'=4] {'c','x'}, dimensions={0} | all-to-all | bytes 196608 | tf_op jit(solution)/shard_map/all_to_all | solution.py:18
  182.2 0.8 fusion.6
  183.0 9.9 %all_to_all.74 = bf16[8,24,256]{2,1,0:T(8,128)(2,1)S(1)} all-to-all(bf16[8,24,256]{2,1,0:T(8,128)(2,1)S(1)} %broadcast_in_dim.34), channel_id=1, replica_groups=mesh['z'=8,'y'=8,'c'=2,'x'=4] {'y'}, dimensions={0} | all-to-all | bytes 196608 | tf_op jit(solution)/shard_map/all_to_all | solution.py:18
  193.7 0.8 copy.46
  194.5 5.1 %all-to-all-start.12 = ((bf16[8,152,128]{2,1,0:T(8,128)(2,1)}), bf16[8,152,128]{2,1,0:T(8,128)(2,1)S(1)}, u32[]{:S(2)}, u32[]{:S(2)}) async-start(bf16[8,152,128]{2,1,0:T(8,128)(2,1)} %bitcast.88), calls=%async_computation.12 | async-start | bytes 622592 | tf_op jit(solution)/shard_map/all_to_all | solution.py:18
  199.6 0.6 pad_maximum_fusion.2
  200.2 6.5 %all-to-all-done.12 = bf16[8,152,128]{2,1,0:T(8,128)(2,1)S(1)} async-done(((bf16[8,152,128]{2,1,0:T(8,128)(2,1)}), bf16[8,152,128]{2,1,0:T(8,128)(2,1)S(1)}, u32[]{:S(2)}, u32[]{:S(2)}) %all-to-all-start.12) | async-done | bytes 311328 | tf_op jit(solution)/shard_map/all_to_all | solution.py:18
  206.7 0.6 fusion.73
  (64 shorter events, 4.0 us)
Async XLA Ops:
  7.2 109.3 %all-gather.3.cloned.1.call-start = ((), (), s32[]{:S(2)}) async-start(), calls=%async_computation.13 | async-start | bytes 2129920 | tf_op jit(solution)/shard_map/all_gather | solution.py:118
  9.1 10.4 %collective-permute-start = (bf16[512,440]{0,1:T(8,128)(2,1)}, bf16[512,440]{0,1:T(8,128)(2,1)S(1)}, u32[]{:S(2)}, u32[]{:S(2)}) collective-permute-start(bf16[512,440]{0,1:T(8,128)(2,1)} %param.5), channel_id=1, source_target_pairs={{0,4},{4,0},{1,5},{5,1},{2,6},{6,2},{3,7},{7,3},{8,12},{12,8},{9,1... | collective-permute-start | bytes 1351688 | tf_op jit(solution)/shard_map/ppermute | solution.py:124
  20.8 12.9 %copy-start.1 = (f32[128,147]{0,1:T(8,128)S(1)}, f32[128,147]{0,1:T(8,128)}, u32[]{:S(2)}) copy-start(f32[128,147]{0,1:T(8,128)} %param.6) | copy-start | bytes 225796
  22.6 36.9 %copy-start.2 = (f32[2,4,147]{2,1,0:T(4,128)S(1)}, f32[2,4,147]{2,1,0:T(4,128)}, u32[]{:S(2)}) copy-start(f32[2,4,147]{2,1,0:T(4,128)} %param.7) | copy-start | bytes 14116
  22.6 29.1 %all-to-all-start = ((bf16[64,8,440]{2,1,0:T(8,128)(2,1)}), bf16[64,8,440]{2,1,0:T(8,128)(2,1)S(1)}, u32[]{:S(2)}, u32[]{:S(2)}) async-start(bf16[64,8,440]{2,1,0:T(8,128)(2,1)} %bitcast.4), calls=%async_computation | async-start | bytes 1048576 | tf_op jit(solution)/shard_map/all_to_all | solution.py:18
  33.8 3.4 %collective-permute-start.1 = (bf16[152,128]{1,0:T(8,128)(2,1)S(1)}, bf16[152,128]{1,0:T(8,128)(2,1)S(1)}, u32[]{:S(2)}, u32[]{:S(2)}) collective-permute-start(bf16[152,128]{1,0:T(8,128)(2,1)S(1)} %pad.23), channel_id=1, source_target_pairs={{0,4},{4,0},{1,5},{5,1},{2,6},{6,2},{3,7},{7,3},{8,12},{12,8},{9,1... | collective-permute-start | bytes 116744 | tf_op jit(solution)/shard_map/ppermute | solution.py:131
  52.7 23.1 %all-to-all-start.1 = ((bf16[64,8,440]{2,1,0:T(8,128)(2,1)}), bf16[64,8,440]{2,1,0:T(8,128)(2,1)S(1)}, u32[]{:S(2)}, u32[]{:S(2)}) async-start(bf16[64,8,440]{2,1,0:T(8,128)(2,1)} %broadcast_in_dim.27), calls=%async_computation.1 | async-start | bytes 1048576 | tf_op jit(solution)/shard_map/all_to_all | solution.py:18
  141.0 41.1 %copy-start = (bf16[512,2048]{1,0:T(8,128)(2,1)S(1)}, bf16[512,2048]{1,0:T(8,128)(2,1)}, u32[]{:S(2)}) copy-start(bf16[512,2048]{1,0:T(8,128)(2,1)} %all-gather.3.cloned.1.call-done) | copy-start | bytes 6291460
  194.5 12.2 %all-to-all-start.12 = ((bf16[8,152,128]{2,1,0:T(8,128)(2,1)}), bf16[8,152,128]{2,1,0:T(8,128)(2,1)S(1)}, u32[]{:S(2)}, u32[]{:S(2)}) async-start(bf16[8,152,128]{2,1,0:T(8,128)(2,1)} %bitcast.88), calls=%async_computation.12 | async-start | bytes 622592 | tf_op jit(solution)/shard_map/all_to_all | solution.py:18
Sparse Core Ops, SparseCore 0:
  11.6 93.3 all-gather.2
